TPU v7x, 32 devices: a whole 2x2x4 slice. The times are simulated.
32 devices in a mesh: groups: 2 (over x), dom: 8 (over z, y), mp: 2 (over core).
Axes of the slice: x: 2, y: 2, z: 4, core: 2. Of those that a mesh axis runs over, the one named last changes fastest.
Arguments:
- feats: bfloat16 [24576, 256], P(('groups', 'dom')), parts along dimension 0, may hold values from -6 to 6
- cell_count: int32 [16], P(('groups', 'dom')), parts along dimension 0, may hold values from 1 to 1536, 9216 in all
- tile_col: int32 [192, 8], P(('groups', 'dom')), parts along dimension 0, may hold values from 0 to 11, all different within a row
- tile_val: bfloat16 [192, 8, 128, 128], P(('groups', 'dom')), parts along dimension 0, may hold values from -0.1875 to 0.1875
- send_list: int32 [16, 8, 64], P(('groups', 'dom')), parts along dimension 0, may hold values from 0 to 1535
- send_count: int32 [16, 8], P(('groups', 'dom')), parts along dimension 0, may hold values from 1 to 64, 256 in all within a row
- recv_list: int32 [16, 8, 64], P(('groups', 'dom')), parts along dimension 0, may hold values from 0 to 1535
- gate_weight_matrix: bfloat16 [2, 256, 512], P(None, None, 'mp'), may hold values from -0.375 to 0.375
- w_up: bfloat16 [2, 256, 512], P(None, None, 'mp'), may hold values from -0.375 to 0.375
- w_down: bfloat16 [2, 512, 256], P(None, 'mp'), may hold values from -0.25 to 0.25
- out_grad: bfloat16 [24576, 256], P(('groups', 'dom')), parts along dimension 0, may hold values from -6 to 6
Outputs:
- final: bfloat16 [24576, 256], P(('groups', 'dom')), parts along dimension 0
- feat_grad: float32 [24576, 256], P(('groups', 'dom')), parts along dimension 0
- grad_gate: float32 [4, 256, 512], P('groups', None, 'mp'), parts along dimension 0
- grad_up: float32 [4, 256, 512], P('groups', None, 'mp'), parts along dimension 0
- down_weight_gradient: float32 [4, 512, 256], P('groups', 'mp'), parts along dimension 0
There are 2 independent parts, one for each index of `groups`. A program takes and returns all parts, laid end to end along the dimension named above; an argument that names none is the same for every part. Nothing has to cross between parts.
Inputs may be any that keep to these rules, and one draw needn't show every extreme that they name: Partition p has live cells in its rows 0 to cell_count[p] - 1; some partition is full in every draw, and the counts sum to 9216. `tile_col`: the entries of one row block are distinct local block columns; every block column is named somewhere. `send_list`: slots at or past send_count are unused. `send_count`: entry [s, q] counts live slots from partition s to partition q, its own included; each row sums to 256 and its largest entry is exactly 64. `recv_list`: entry [q, s, k] is the receiver's local row fed by slot k from partition s.
All inputs are finite; a program needn't handle non-finite values. No bound on the sum of `cell_count` on one device may be relied on, other than what follows from the above.
Results may differ from a plain program's by a relative error of at most 0.03.
Values may be sent and summed in bfloat16 or wider, within the bound.
No kernel may reach another device: no remote copies, remote signals or barrier semaphores. Data moves between devices by JAX's collectives and lax.ppermute only.
A program may use at most 128 MiB of HBM per device.

v0:
```python
import functools

import jax
import jax.numpy as jnp
from jax import lax
from jax.experimental import pallas as pl
from jax.experimental.pallas import tpu as pltpu
from jax.sharding import PartitionSpec as P

BF16 = jnp.bfloat16
F32 = jnp.float32
LANES = 128
BLOCK = 128
SMEM = pl.BlockSpec(memory_space=pltpu.SMEM)
CHUNK = 1536
SUB = 512
SLOTS = 512


def shape(dims, dtype):
    return jax.ShapeDtypeStruct(tuple(dims), dtype)


def part(ref, cut, c):
    if cut == "whole":
        return ref
    if cut == "rows":
        return ref.at[pl.ds(c * CHUNK, CHUNK)]
    if cut == "columns":
        return ref.at[:, pl.ds(c * CHUNK, CHUNK)]
    return ref.at[pl.ds(c * cut, cut)]


class Layer:
    def __init__(self, index):
        self.index = index


class Traffic:
    def __init__(self, steps, ins, outs, in_sems, out_sems):
        self.steps, self.ins, self.outs, self.in_sems, self.out_sems = steps, ins, outs, in_sems, out_sems
        self.leaving = []
        for c in range(steps):
            for k in range(len(ins)):
                if self.has(k, c):
                    self.arriving(k, c).start()

    def has(self, k, c):
        cut = self.ins[k][2]
        return cut not in ("near", "later") and (c == 0 or not (cut == "whole" or isinstance(cut, Layer)))

    def arriving(self, k, c):
        far, near, cut = self.ins[k]
        if isinstance(cut, Layer):
            return pltpu.make_async_copy(far.at[cut.index], near, self.in_sems.at[k, 0])
        return pltpu.make_async_copy(part(far, cut, c), part(near, cut, c), self.in_sems.at[k, c])

    def need(self, c, *which):
        for k in which or range(len(self.ins)):
            if self.has(k, c):
                self.arriving(k, c).wait()

    def put(self, k, c=0):
        near, far, cut = self.outs[k]
        copy = pltpu.make_async_copy(part(near, cut, c), part(far, cut, c), self.out_sems.at[k, c])
        copy.start()
        self.leaving.append(copy)

    def finish(self):
        for copy in self.leaving:
            copy.wait()


def call(kernel, steps, outs, ins, flops, name, scratch=()):
    moved = sum(x.size * x.dtype.itemsize for x, _ in (*ins, *outs))
    far_ins = [(x, cut) for x, cut in ins if cut is not None]
    scalars = len(ins) - len(far_ins)
    kept_outs = [k for k, (_, cut) in enumerate(outs) if cut != "later"]
    staged = [k for k, (_, cut) in enumerate(far_ins) if cut not in ("near", "later")]

    def body(*refs):
        fixed = refs[:scalars]
        far_in = refs[scalars : len(ins)]
        far_out = refs[len(ins) : len(ins) + len(outs)]
        rest = refs[len(ins) + len(outs) :]
        near_in = list(far_in)
        for slot, k in enumerate(staged):
            near_in[k] = rest[slot]
        rest = rest[len(staged) :]
        near_out, rest = rest[: len(kept_outs)], rest[len(kept_outs) :]
        near_out = [near_out[kept_outs.index(k)] if k in kept_outs else None for k in range(len(outs))]
        (in_sems, out_sems), own = rest[:2], rest[2:]
        traffic = Traffic(
            steps,
            [(f, n, cut) for f, n, (_, cut) in zip(far_in, near_in, far_ins)],
            [(n, f, cut) for n, f, (_, cut) in zip(near_out, far_out, outs)],
            in_sems,
            out_sems,
        )
        kernel(traffic, *fixed, *near_in, *(near_out[k] for k in kept_outs), *own)
        traffic.finish()

    def held(x, cut):
        return pltpu.VMEM(x.shape[1:] if isinstance(cut, Layer) else x.shape, x.dtype)

    spaces = [pltpu.VMEM if cut == "near" else pl.ANY for _, cut in far_ins]
    return pl.pallas_call(
        body,
        out_shape=[x for x, _ in outs],
        in_specs=[SMEM] * scalars + [pl.BlockSpec(memory_space=space) for space in spaces],
        out_specs=[pl.BlockSpec(memory_space=pl.ANY)] * len(outs),
        scratch_shapes=[
            *(held(*far_ins[k]) for k in staged),
            *(pltpu.VMEM(outs[k][0].shape, outs[k][0].dtype) for k in kept_outs),
            pltpu.SemaphoreType.DMA((len(far_ins), steps)),
            pltpu.SemaphoreType.DMA((len(outs), steps)),
            *scratch,
        ],
        cost_estimate=pl.CostEstimate(flops=flops, bytes_accessed=moved, transcendentals=0),
        name=name,
    )(*[x for x, _ in ins])


def rows_of(c):
    return slice(c * CHUNK, (c + 1) * CHUNK)


def inner(c):
    return range(c * CHUNK, (c + 1) * CHUNK, SUB)


def mm(a, b):
    return jnp.dot(a, b, preferred_element_type=F32)


def mm_t(a, b):
    return lax.dot_general(a, b, (((1,), (1,)), ((), ())), preferred_element_type=F32)


def mm_rows(a, b):
    return lax.dot_general(a, b, (((0,), (0,)), ((), ())), preferred_element_type=F32)


def live(count_ref, start, rows, width):
    index = lax.broadcasted_iota(jnp.int32, (rows, width), 0) + start
    return index < count_ref[0]


def fill_columns(col_ref, list_ref, used):
    peers, n = list_ref.shape[1:]
    down = lax.broadcasted_iota(jnp.int32, (n, n), 0)
    across = lax.broadcasted_iota(jnp.int32, (n, n), 1)

    def step(q, carry):
        line = jnp.broadcast_to(list_ref[0, pl.ds(q, 1), :], (n, n))
        kept = (down == across) & used(q, across, line)
        col = jnp.sum(jnp.where(kept, line + 1, 0), axis=1, keepdims=True) - 1
        col_ref[pl.ds(pl.multiple_of(q * n, n), n), :] = jnp.broadcast_to(col, (n, LANES))
        return carry

    lax.fori_loop(0, peers, step, 0, unroll=4)


def fill_row(row_ref, list_ref, used):
    peers, n = list_ref.shape[1:]
    across = lax.broadcasted_iota(jnp.int32, (1, n), 1)
    for q in range(peers):
        line = list_ref[0, q : q + 1, :]
        row_ref[0:1, q * n : (q + 1) * n] = jnp.where(used(q, across, line), line, -1)


def sent(count_ref, used_ref):
    return lambda q, k, row: (k < used_ref[0, q]) & (row < count_ref[0])


def always(q, k, row):
    return row >= 0


def gather_rows(col_ref, source_ref, out_ref):
    slots, rows = out_ref.shape[0], source_ref.shape[0]
    lanes = lax.broadcasted_iota(jnp.int32, (SLOTS, LANES), 1)

    def step(i, carry):
        at = pl.ds(pl.multiple_of(i * SLOTS, SLOTS), SLOTS)
        col = col_ref[at, :]
        pick = jnp.concatenate(
            [jnp.where(col == lanes + first, 1.0, 0.0).astype(BF16) for first in range(0, rows, LANES)], axis=1
        )
        out_ref[at, :] = mm(pick, source_ref[...]).astype(BF16)
        return carry

    lax.fori_loop(0, slots // SLOTS, step, 0)


def scatter_rows(row_ref, start, rows, arriving):
    slots = row_ref.shape[1]
    index = lax.broadcasted_iota(jnp.int32, (rows, slots), 0) + start
    pick = jnp.where(row_ref[0:1, :] == index, 1.0, 0.0).astype(BF16)
    return mm(pick, arriving[...])


def send_kernel(traffic, count_ref, used_ref, list_ref, feats_ref, out_ref, col_ref):
    traffic.need(0)
    fill_columns(col_ref, list_ref, sent(count_ref, used_ref))
    traffic.put(1)
    for c in range(1, traffic.steps):
        traffic.need(c)
    gather_rows(col_ref, feats_ref, out_ref)
    traffic.put(0)


class Dense:
    def __init__(self, cols_ref, tile_ref, dense_ref, sems):
        self.tile_ref, self.dense_ref, self.sems = tile_ref, dense_ref, sems
        self.row_blocks, self.per_row = tile_ref.shape[:2]
        self.cols_ref = cols_ref
        for r in range(self.row_blocks):
            for j in range(self.per_row):
                self.copy(r, j).start()

    def copy(self, r, j):
        at = pl.ds(pl.multiple_of(self.cols_ref[r, j] * BLOCK, BLOCK), BLOCK)
        return pltpu.make_async_copy(
            self.tile_ref.at[r, j], self.dense_ref.at[pl.ds(r * BLOCK, BLOCK), at], self.sems.at[r]
        )

    def zero_others(self, rest_ref):
        columns = self.dense_ref.shape[1] // BLOCK
        for r in range(self.row_blocks):
            named = 0
            for j in range(self.per_row):
                named = named | (1 << self.cols_ref[r, j])
            count = 0
            for c in range(columns):
                rest_ref[count] = c
                count = count + 1 - ((named >> c) & 1)
            for k in range(columns - self.per_row):
                at = pl.ds(pl.multiple_of(rest_ref[k] * BLOCK, BLOCK), BLOCK)
                self.dense_ref[r * BLOCK : (r + 1) * BLOCK, at] = jnp.zeros((BLOCK, BLOCK), BF16)

    def need(self, r):
        for j in range(self.per_row):
            self.copy(r, j).wait()


def first_local_kernel(
    traffic, count_ref, used_ref, cols_ref, send_ref, recv_ref, feats_ref, tile_ref,
    state_ref, sum_ref, send_row_ref, recv_row_ref, recv_col_ref, dense_ref, rest_ref, sems,
):
    dense = Dense(cols_ref, tile_ref, dense_ref, sems)
    dense.zero_others(rest_ref)
    rows, width = feats_ref.shape
    traffic.need(0)
    fill_row(send_row_ref, send_ref, sent(count_ref, used_ref))
    fill_row(recv_row_ref, recv_ref, always)
    fill_columns(recv_col_ref, recv_ref, always)
    state_ref[...] = jnp.where(live(count_ref, 0, rows, width), feats_ref[...], jnp.zeros((), BF16))
    for k in (0, 2, 3, 4):
        traffic.put(k)
    local_sums(traffic, dense, dense_ref, state_ref, sum_ref, 1)


def local_sums(traffic, dense, dense_ref, state_ref, sum_ref, out):
    for c in range(traffic.steps):
        for r in range(c * CHUNK // BLOCK, (c + 1) * CHUNK // BLOCK):
            dense.need(r)
        sum_ref[rows_of(c), :] = mm(dense_ref[rows_of(c), :], state_ref[...])
        traffic.put(out, c)


def local_kernel(traffic, cols_ref, state_ref, tile_ref, sum_ref, dense_ref, rest_ref, sems):
    dense = Dense(cols_ref, tile_ref, dense_ref, sems)
    dense.zero_others(rest_ref)
    traffic.need(0)
    local_sums(traffic, dense, dense_ref, state_ref, sum_ref, 0)


def turned_local_kernel(traffic, count_ref, cols_ref, agg_ref, up_ref, tile_ref, sum_ref, dense_ref, rest_ref, sems):
    dense = Dense(cols_ref, tile_ref, dense_ref, sems)
    dense.zero_others(rest_ref)
    width = agg_ref.shape[1]
    traffic.need(0)
    for r in range(dense.row_blocks):
        dense.need(r)
    for c in range(traffic.steps):
        if c > 0:
            traffic.need(c)
        at = rows_of(c)
        upstream = jnp.where(live(count_ref, c * CHUNK, CHUNK, width), up_ref[at, :].astype(F32), 0.0)
        sum_ref[at, :] = mm_rows(dense_ref[:, at], agg_ref[...]) + upstream
        traffic.put(0, c)


def triples(refs):
    return [tuple(refs[i : i + 3]) for i in range(0, len(refs), 3)]


def gates(acts, weights):
    result = []
    for gate_ref, up_ref, _ in weights:
        gate = mm(acts, gate_ref[...])
        up = mm(acts, up_ref[...])
        sig = 0.5 * jnp.tanh(0.5 * gate) + 0.5
        result.append((gate, up, sig, gate * sig))
    return result


def layer_grads(at, acts, terms, down_in, weights, agg_ref, kept):
    agg = None
    for part, ((gate, up, sig, silu), (gate_ref, up_ref, down_ref)) in enumerate(zip(terms, weights)):
        hidden_grad = mm_t(down_in, down_ref[...])
        slope = sig * (1.0 + gate * (1.0 - sig))
        gate_grad = (hidden_grad * up * slope).astype(BF16)
        up_grad = (hidden_grad * silu).astype(BF16)
        more = mm_t(gate_grad, gate_ref[...]) + mm_t(up_grad, up_ref[...])
        agg = more if agg is None else agg + more
        if part == 0:
            for ref, value in zip(kept, ((silu * up).astype(BF16), gate_grad, up_grad, down_in)):
                ref[at, :] = value
    agg_ref[at, :] = agg.astype(BF16)


def weight_grads(acts_ref, kept, dw_ref):
    hidden_ref, gate_ref, up_ref, down_ref = kept
    pairs = ((acts_ref, gate_ref), (acts_ref, up_ref), (hidden_ref, down_ref))
    for k, (left_ref, right_ref) in enumerate(pairs):
        size = left_ref.shape[1]
        dw_ref[k * size : (k + 1) * size, :] = mm_rows(left_ref[...], right_ref[...]).astype(BF16)


def mix(terms, weights):
    mixed = None
    for (gate, up, sig, silu), (_, _, down_ref) in zip(terms, weights):
        part = mm((silu * up).astype(BF16), down_ref[...])
        mixed = part if mixed is None else mixed + part
    return mixed


def forward_kernel(parts, traffic, count_ref, col_ref, row_ref, arriving_ref, *refs):
    weights = triples(refs[: 3 * parts])
    sum_ref, state_ref, acts_ref, next_ref, out_ref = refs[3 * parts :]
    width = state_ref.shape[1]
    for c in range(traffic.steps):
        traffic.need(c, *range(1, len(traffic.ins)))
        for first in inner(c):
            at = slice(first, first + SUB)
            acts = (sum_ref[at, :] + scatter_rows(row_ref, first, SUB, arriving_ref)).astype(BF16)
            acts_ref[at, :] = acts
            after = state_ref[at, :].astype(F32) + mix(gates(acts, weights), weights)
            next_ref[at, :] = jnp.where(live(count_ref, first, SUB, width), after, 0.0).astype(BF16)
        traffic.put(0, c)
        traffic.put(1, c)
    traffic.need(0, 0)
    gather_rows(col_ref, next_ref, out_ref)
    traffic.put(2)


def turn_kernel(parts, traffic, count_ref, col_ref, row_ref, arriving_ref, *refs):
    weights = triples(refs[: 3 * parts])
    sum_ref, state_ref, grad_ref, final_ref, agg_ref, out_ref, dw_ref, acts_ref, *kept = refs[3 * parts :]
    width = state_ref.shape[1]
    for c in range(traffic.steps):
        traffic.need(c, *range(1, len(traffic.ins)))
        for first in inner(c):
            at = slice(first, first + SUB)
            acts = (sum_ref[at, :] + scatter_rows(row_ref, first, SUB, arriving_ref)).astype(BF16)
            acts_ref[at, :] = acts
            terms = gates(acts, weights)
            after = state_ref[at, :].astype(F32) + mix(terms, weights)
            alive = live(count_ref, first, SUB, width)
            final_ref[at, :] = jnp.where(alive, after, 0.0).astype(BF16)
            down_in = jnp.where(alive, grad_ref[at, :], jnp.zeros((), BF16))
            layer_grads(at, acts, terms, down_in, weights, agg_ref, kept)
        traffic.put(0, c)
        traffic.put(1, c)
    traffic.need(0, 0)
    gather_rows(col_ref, agg_ref, out_ref)
    traffic.put(2)
    weight_grads(acts_ref, kept, dw_ref)
    traffic.put(3)


def put_pieces(traffic, k, sources, sem):
    far = traffic.outs[k][1]
    for q in range(far.shape[0]):
        first = 0
        for source in sources:
            rows = source.shape[0] // far.shape[0]
            copy = pltpu.make_async_copy(
                source.at[pl.ds(q * rows, rows)], far.at[q, pl.ds(first, rows)], sem.at[q]
            )
            copy.start()
            traffic.leaving.append(copy)
            first += rows


def backward_kernel(parts, traffic, count_ref, col_ref, row_ref, arriving_ref, *refs):
    weights = triples(refs[: 3 * parts])
    sum_ref, acts_ref, upstream_ref, agg_ref, out_ref, dw_ref, sem, *kept = refs[3 * parts :]
    width = acts_ref.shape[1]
    for c in range(traffic.steps):
        traffic.need(c, *range(1, len(traffic.ins)))
        for first in inner(c):
            at = slice(first, first + SUB)
            carried = sum_ref[at, :] + scatter_rows(row_ref, first, SUB, arriving_ref)
            upstream = jnp.where(live(count_ref, first, SUB, width), carried, 0.0)
            upstream_ref[at, :] = upstream
            acts = acts_ref[at, :]
            layer_grads(at, acts, gates(acts, weights), upstream.astype(BF16), weights, agg_ref, kept)
        traffic.put(0, c)
        traffic.put(1, c)
    traffic.need(0, 0)
    gather_rows(col_ref, agg_ref, out_ref)
    weight_grads(acts_ref, kept, dw_ref)
    put_pieces(traffic, 2, (out_ref, dw_ref), sem)


def last_kernel(traffic, count_ref, row_ref, arriving_ref, sum_ref, out_ref):
    width = out_ref.shape[1]
    for c in range(traffic.steps):
        traffic.need(c)
        for first in inner(c):
            at = slice(first, first + SUB)
            carried = sum_ref[at, :] + scatter_rows(row_ref, first, SUB, arriving_ref)
            out_ref[at, :] = jnp.where(live(count_ref, first, SUB, width), carried, 0.0)
        traffic.put(0, c)


def local(
    feats,
    cell_count,
    tile_col,
    tile_val,
    send_list,
    send_count,
    recv_list,
    gate_weight_matrix,
    w_up,
    w_down,
    out_grad,
):
    rows, width = feats.shape
    peers, slot_count = send_list.shape[1:]
    slots = peers * slot_count
    layers = gate_weight_matrix.shape[0]
    hidden_width = gate_weight_matrix.shape[2]
    parts = lax.axis_size("mp")
    steps = rows // CHUNK

    def swap(blocks):
        return lax.all_to_all(blocks, "dom", split_axis=0, concat_axis=0, tiled=True)

    def exchange(outgoing):
        return swap(outgoing.reshape(peers, slot_count, width)).reshape(slots, width)

    def chunked(x):
        return x, "rows"

    def fixed(x):
        return x, "whole"

    def near(x):
        return x, "near"

    state_shape, sum_shape = shape((rows, width), BF16), shape((rows, width), F32)
    slot_shape = shape((slots, width), BF16)
    dense_scratch = [
        pltpu.VMEM((rows, rows), BF16),
        pltpu.SMEM((rows // BLOCK + 1,), jnp.int32),
        pltpu.SemaphoreType.DMA((rows // BLOCK,)),
    ]
    tiles, cols = (tile_val, "later"), (tile_col, None)
    row_shape, col_shape = shape((1, slots), jnp.int32), shape((slots, LANES), jnp.int32)
    dw_shape = shape((3 * width, hidden_width), BF16)
    half = pltpu.VMEM((rows, hidden_width), BF16)
    kept_shapes = [half, half, half, pltpu.VMEM((rows, width), BF16)]
    local_flops = 2 * rows * rows * width
    slot_flops = 2 * rows * slots * width
    layer_flops = 6 * rows * width * hidden_width * parts
    count = (cell_count, None)

    outgoing, send_col = call(
        send_kernel,
        steps,
        [fixed(slot_shape), fixed(col_shape)],
        [count, (send_count, None), fixed(send_list), chunked(feats)],
        slot_flops,
        "send",
    )
    outgoing, mine = lax.optimization_barrier((outgoing, (gate_weight_matrix, w_up, w_down)))
    arriving = exchange(outgoing)
    turns = [[(d, (d + t) % parts) for d in range(parts)] for t in range(1, parts)]
    held = [mine] + [tuple(lax.ppermute(w, "mp", turn) for w in mine) for turn in turns]

    def weights(layer):
        return [(w, Layer(layer)) for trio in held for w in trio]

    state, total, send_row, recv_row, recv_col = call(
        first_local_kernel,
        steps,
        [
            fixed(state_shape),
            chunked(sum_shape),
            fixed(row_shape),
            fixed(row_shape),
            fixed(col_shape),
        ],
        [
            count,
            (send_count, None),
            cols,
            fixed(send_list),
            fixed(recv_list),
            fixed(feats),
            tiles,
        ],
        local_flops,
        "first_local",
        dense_scratch,
    )
    kept = []
    for layer in range(layers - 1):
        acts, state, outgoing = call(
            functools.partial(forward_kernel, parts),
            steps,
            [chunked(state_shape), chunked(state_shape), fixed(slot_shape)],
            [count, fixed(send_col), fixed(recv_row), near(arriving), *weights(layer), chunked(total), chunked(state)],
            layer_flops + 2 * slot_flops,
            "forward",
        )
        kept.append(acts)
        arriving = exchange(outgoing)
        (total,) = call(
            local_kernel, steps, [chunked(sum_shape)], [cols, fixed(state), tiles], local_flops, "local", dense_scratch
        )
    final, agg, outgoing, dw = call(
        functools.partial(turn_kernel, parts),
        steps,
        [chunked(state_shape), chunked(state_shape), fixed(slot_shape), fixed(dw_shape)],
        [
            count, fixed(recv_col), fixed(recv_row), near(arriving), *weights(layers - 1), chunked(total),
            chunked(state), chunked(out_grad),
        ],
        3 * layer_flops + 2 * slot_flops,
        "turn",
        [pltpu.VMEM((rows, width), BF16), *kept_shapes],
    )
    piece = dw_shape.shape[0] // peers
    both_shape = shape((peers, slot_count + piece, width), BF16)

    def turned_local(agg, upstream):
        return call(
            turned_local_kernel,
            steps,
            [chunked(sum_shape)],
            [count, cols, fixed(agg), chunked(upstream), tiles],
            local_flops,
            "turned_local",
            dense_scratch,
        )[0]

    def added(pieces):
        return jnp.sum(pieces.astype(F32), axis=0).astype(BF16)

    arriving = exchange(outgoing)
    total = turned_local(agg, out_grad)
    reduced = [None] * layers
    for layer in reversed(range(layers - 1)):
        if layer == layers - 2:
            total, arriving, dw = lax.optimization_barrier((total, arriving, dw))
            reduced[layer + 1] = added(swap(dw.reshape(peers, piece, width)))
        upstream, agg, both = call(
            functools.partial(backward_kernel, parts),
            steps,
            [chunked(sum_shape), chunked(state_shape), (both_shape, "later")],
            [
                count, fixed(recv_col), fixed(send_row), near(arriving), *weights(layer), chunked(total),
                chunked(kept[layer]),
            ],
            3 * layer_flops + 2 * slot_flops,
            "backward",
            [
                pltpu.VMEM(slot_shape.shape, BF16),
                pltpu.VMEM(dw_shape.shape, BF16),
                pltpu.SemaphoreType.DMA((peers,)),
                *kept_shapes,
            ],
        )
        both, reduced = lax.optimization_barrier((both, reduced))
        both = swap(both)
        total = turned_local(agg, upstream)
        arriving = both[:, :slot_count].reshape(slots, width)
        reduced[layer] = added(both[:, slot_count:])
    own = jnp.concatenate(reduced)
    full = swap(jnp.broadcast_to(own[None], (peers, *own.shape)))
    (feat_grad,) = call(
        last_kernel,
        steps,
        [chunked(sum_shape)],
        [count, fixed(send_row), near(arriving), chunked(total)],
        slot_flops,
        "last",
    )
    full = full.reshape(peers, layers, piece, width).swapaxes(0, 1).reshape(layers, 3, width, hidden_width)
    full = full.swapaxes(0, 1).astype(F32)
    return (final, feat_grad, full[0], full[1], full[2])


def solution(mesh):
    return jax.shard_map(
        local,
        mesh=mesh,
        in_specs=(
            P(("groups", "dom"), None),
            P(("groups", "dom")),
            P(("groups", "dom"), None),
            P(("groups", "dom"), None, None, None),
            P(("groups", "dom"), None, None),
            P(("groups", "dom"), None),
            P(("groups", "dom"), None, None),
            P(None, None, "mp"),
            P(None, None, "mp"),
            P(None, "mp", None),
            P(("groups", "dom"), None),
        ),
        out_specs=(
            P(("groups", "dom"), None),
            P(("groups", "dom"), None),
            P("groups", None, "mp"),
            P("groups", None, "mp"),
            P("groups", "mp", None),
        ),
        check_vma=False,
    )
```

profile of v0, /device:TPU:0, one launch (start us, length us, event | category | flops | bytes accessed | tf_op | source)
XLA Modules:
  0.0 127.5 jit_solution(5708688042550525271)
XLA Ops:
  0.6 0.0 copy-start.6
  0.6 0.0 copy-start.5
  0.7 0.0 copy-start.4
  0.7 0.0 copy-start.3
  1.4 3.4 %send.1 = (bf16[512,256]{1,0:T(8,128)(2,1)}, s32[512,128]{1,0:T(8,128)}) custom-call(s32[1]{0:T(128)S(6)} %copy.29.refs_0_, s32[1,8]{1,0:T(1,128)} %refs_1_.5, s32[1,8,64]{2,1,0:T(8,128)} %refs_2_.3, bf16[1536,256]{1,0:T(8,128)(2,1)} %refs_3_.4), custom_call_target="tpu_custom_call" | custom-call | flops 402653184 | bytes 1312804 | tf_op jit(solution)/shard_map/send/pallas_call | solution.py:107
  4.8 7.3 %all-to-all-start = ((bf16[8,64,256]{2,1,0:T(8,128)(2,1)}), bf16[8,64,256]{2,1,0:T(8,128)(2,1)S(1)}, u32[]{:S(2)}, u32[]{:S(2)}) async-start(bf16[8,64,256]{2,1,0:T(8,128)(2,1)} %bitcast.25), calls=%async_computation | async-start | bytes 524288 | tf_op jit(solution)/shard_map/all_to_all | solution.py:452
  12.1 0.0 copy-done.4
  12.1 0.1 collective-permute-start
  12.2 0.0 copy-done.5
  12.2 0.5 collective-permute-start.1
  12.7 0.0 copy-done.6
  12.7 0.1 collective-permute-start.2
  12.8 0.0 copy-done.3
  12.8 0.7 copy.24.refs_2_.refs_0_.refs_1_
  13.5 6.4 %first_local.1 = (bf16[1536,256]{1,0:T(8,128)(2,1)}, f32[1536,256]{1,0:T(8,128)}, s32[1,512]{1,0:T(1,128)}, s32[1,512]{1,0:T(1,128)}, s32[512,128]{1,0:T(8,128)}) custom-call(s32[1]{0:T(128)S(6)} %copy.29.refs_0_, s32[1,8]{1,0:T(1,128)} %refs_1_.5, s32[12,8]{1,0:T(8,128)} %copy.24.refs_2_.refs_0_.refs_1_, s32[1,8,64]{2,1,0:T(8,128)} %refs_2_.3, ...), custom_call_target="tpu_custom_call" | custom-call | flops 1207959552 | bytes 6562212 | tf_op jit(solution)/shard_map/first_local/pallas_call | solution.py:107
  19.9 0.0 collective-permute-done.refs_7_
  19.9 0.0 copy-start.7
  19.9 0.0 collective-permute-done.1.refs_8_
  19.9 0.0 copy-start.8
  19.9 0.0 collective-permute-done.2.refs_9_
  19.9 0.0 copy-start.9
  19.9 1.1 all-to-all-done
  21.1 0.0 copy-done.7
  21.1 0.7 copy-done
  21.8 6.9 %forward.1 = (bf16[1536,256]{1,0:T(8,128)(2,1)}, bf16[1536,256]{1,0:T(8,128)(2,1)}, bf16[512,256]{1,0:T(8,128)(2,1)}) custom-call(s32[1]{0:T(128)S(6)} %copy.29.refs_0_, s32[512,128]{1,0:T(8,128)} %get-tuple-element.33.refs_1_, s32[1,512]{1,0:T(1,128)} %get-tuple-element.32.refs_2_, bf16[512,256]{1,0:T(8,128)(2,1)} %bitcast.24, ...), custom_call_target="tpu_custom_call" | custom-call | flops 2013265920 | bytes 6293508 | tf_op jit(solution)/shard_map/forward/pallas_call | solution.py:107
  28.7 5.0 %all-to-all-start.1 = ((bf16[8,64,256]{2,1,0:T(8,128)(2,1)}), bf16[8,64,256]{2,1,0:T(8,128)(2,1)S(1)}, u32[]{:S(2)}, u32[]{:S(2)}) async-start(bf16[8,64,256]{2,1,0:T(8,128)(2,1)} %bitcast.29), calls=%async_computation.1 | async-start | bytes 524288 | tf_op jit(solution)/shard_map/all_to_all | solution.py:452
  33.7 5.8 %local.1.refs_10_ = f32[1536,256]{1,0:T(8,128)} custom-call(s32[12,8]{1,0:T(8,128)} %copy.24.refs_2_.refs_0_.refs_1_, bf16[1536,256]{1,0:T(8,128)(2,1)} %get-tuple-element.42.refs_1_.refs_11_, bf16[12,8,128,128]{3,2,1,0:T(8,128)(2,1)} %refs_4_.8), custom_call_target="tpu_custom_call" | custom-call | flops 1207959552 | bytes 5505408 | tf_op jit(solution)/shard_map/local/pallas_call | solution.py:107
  39.5 3.7 %all-to-all-done.1 = bf16[8,64,256]{2,1,0:T(8,128)(2,1)S(1)} async-done(((bf16[8,64,256]{2,1,0:T(8,128)(2,1)}), bf16[8,64,256]{2,1,0:T(8,128)(2,1)S(1)}, u32[]{:S(2)}, u32[]{:S(2)}) %all-to-all-start.1) | async-done | bytes 262176 | tf_op jit(solution)/shard_map/all_to_all | solution.py:452
  43.2 0.7 copy-done.2
  43.9 9.1 %turn.1 = (bf16[1536,256]{1,0:T(8,128)(2,1)}, bf16[1536,256]{1,0:T(8,128)(2,1)}, bf16[512,256]{1,0:T(8,128)(2,1)}, bf16[768,256]{1,0:T(8,128)(2,1)}) custom-call(s32[1]{0:T(128)S(6)} %copy.29.refs_0_, s32[512,128]{1,0:T(8,128)} %get-tuple-element.31.refs_1_, s32[1,512]{1,0:T(1,128)} %get-tuple-element.32.refs_2_, bf16[512,256]{1,0:T(8,128)(2,1)} %bitcast.27, ...), custom_call_target="tpu_custom_call" | custom-call | flops 4429185024 | bytes 7473156 | tf_op jit(solution)/shard_map/turn/pallas_call | solution.py:107
  53.0 3.6 %all-to-all-start.2 = ((bf16[8,64,256]{2,1,0:T(8,128)(2,1)}), bf16[8,64,256]{2,1,0:T(8,128)(2,1)S(1)}, u32[]{:S(2)}, u32[]{:S(2)}) async-start(bf16[8,64,256]{2,1,0:T(8,128)(2,1)} %bitcast.28), calls=%async_computation.2 | async-start | bytes 524288 | tf_op jit(solution)/shard_map/all_to_all | solution.py:452
  56.6 6.1 %turned_local.2.refs_10_ = f32[1536,256]{1,0:T(8,128)} custom-call(s32[1]{0:T(128)S(6)} %copy.29.refs_0_, s32[12,8]{1,0:T(8,128)} %copy.24.refs_2_.refs_0_.refs_1_, bf16[1536,256]{1,0:T(8,128)(2,1)} %get-tuple-element.45.refs_2_, bf16[1536,256]{1,0:T(8,128)(2,1)} %refs_3_.5, bf16[12,8,128,128]{3,2,1,0:T(8,128)(2,1)} %refs_4_.8), custom_call_target="tpu_custom_call" | custom-call | flops 1207959552 | bytes 6291844 | tf_op jit(solution)/shard_map/turned_local/pallas_call | solution.py:107
  62.7 3.0 %all-to-all-done.2 = bf16[8,64,256]{2,1,0:T(8,128)(2,1)S(1)} async-done(((bf16[8,64,256]{2,1,0:T(8,128)(2,1)}), bf16[8,64,256]{2,1,0:T(8,128)(2,1)S(1)}, u32[]{:S(2)}, u32[]{:S(2)}) %all-to-all-start.2) | async-done | bytes 262176 | tf_op jit(solution)/shard_map/all_to_all | solution.py:452
  65.7 3.7 %all-to-all-start.3 = ((bf16[8,96,256]{2,1,0:T(8,128)(2,1)}), bf16[8,96,256]{2,1,0:T(8,128)(2,1)S(1)}, u32[]{:S(2)}, u32[]{:S(2)}) async-start(bf16[8,96,256]{2,1,0:T(8,128)(2,1)} %bitcast.6), calls=%async_computation.3 | async-start | bytes 786432 | tf_op jit(solution)/shard_map/all_to_all | solution.py:452
  69.4 8.6 %backward.1 = (f32[1536,256]{1,0:T(8,128)}, bf16[1536,256]{1,0:T(8,128)(2,1)}, bf16[8,160,256]{2,1,0:T(8,128)(2,1)}) custom-call(s32[1]{0:T(128)S(6)} %copy.29.refs_0_, s32[512,128]{1,0:T(8,128)} %get-tuple-element.31.refs_1_, s32[1,512]{1,0:T(1,128)} %get-tuple-element.44.refs_2_.refs_1_, bf16[512,256]{1,0:T(8,128)(2,1)} %bitcast.26, ...), custom_call_target="tpu_custom_call" | custom-call | flops 4429185024 | bytes 7473156 | tf_op jit(solution)/shard_map/backward/pallas_call | solution.py:107
  78.0 2.7 %all-to-all-done.3 = bf16[8,96,256]{2,1,0:T(8,128)(2,1)S(1)} async-done(((bf16[8,96,256]{2,1,0:T(8,128)(2,1)}), bf16[8,96,256]{2,1,0:T(8,128)(2,1)S(1)}, u32[]{:S(2)}, u32[]{:S(2)}) %all-to-all-start.3) | async-done | bytes 393248 | tf_op jit(solution)/shard_map/all_to_all | solution.py:452
  80.7 0.1 reduce_sum.24
  80.7 21.1 %all_to_all.30 = bf16[8,160,256]{2,1,0:T(8,128)(2,1)S(1)} all-to-all(bf16[8,160,256]{2,1,0:T(8,128)(2,1)} %get-tuple-element.53), channel_id=1, replica_groups=mesh['groups'=2,'dom'=8,'mp'=2] {'dom'}, dimensions={0} | all-to-all | bytes 1310720 | tf_op jit(solution)/shard_map/all_to_all | solution.py:452
  101.9 0.1 slice_reduce_fusion
  101.9 0.9 broadcast_in_dim.2
  102.9 3.5 %all-to-all-start.5 = ((bf16[8,192,256]{2,1,0:T(8,128)(2,1)}), bf16[8,192,256]{2,1,0:T(8,128)(2,1)S(1)}, u32[]{:S(2)}, u32[]{:S(2)}) async-start(bf16[8,192,256]{2,1,0:T(8,128)(2,1)} %broadcast_in_dim.2), calls=%async_computation.5 | async-start | bytes 1572864 | tf_op jit(solution)/shard_map/all_to_all | solution.py:452
  106.4 6.4 %turned_local.3.refs_3_ = f32[1536,256]{1,0:T(8,128)} custom-call(s32[1]{0:T(128)S(6)} %copy.29.refs_0_, s32[12,8]{1,0:T(8,128)} %copy.24.refs_2_.refs_0_.refs_1_, bf16[1536,256]{1,0:T(8,128)(2,1)} %get-tuple-element.54.refs_2_, f32[1536,256]{1,0:T(8,128)} %get-tuple-element.55.refs_3_, bf16[12,8,128,128]{3,2,1,0:T(8,128)(2,1)} %refs_4_.8), custom_call_target="tpu_custom_call" | custom-call | flops 1207959552 | bytes 7078276 | tf_op jit(solution)/shard_map/turned_local/pallas_call | solution.py:107
  112.8 0.7 slice.20
  113.5 4.1 %last.1 = f32[1536,256]{1,0:T(8,128)} custom-call(s32[1]{0:T(128)S(6)} %copy.29.refs_0_, s32[1,512]{1,0:T(1,128)} %get-tuple-element.44.refs_2_.refs_1_, bf16[512,256]{1,0:T(8,128)(2,1)} %bitcast.23, f32[1536,256]{1,0:T(8,128)} %turned_local.3.refs_3_), custom_call_target="tpu_custom_call" | custom-call | flops 402653184 | bytes 3409924 | tf_op jit(solution)/shard_map/last/pallas_call | solution.py:107
  117.7 8.4 %all-to-all-done.5 = bf16[8,192,256]{2,1,0:T(8,128)(2,1)S(1)} async-done(((bf16[8,192,256]{2,1,0:T(8,128)(2,1)}), bf16[8,192,256]{2,1,0:T(8,128)(2,1)S(1)}, u32[]{:S(2)}, u32[]{:S(2)}) %all-to-all-start.5) | async-done | bytes 786464 | tf_op jit(solution)/shard_map/all_to_all | solution.py:452
  126.0 0.2 convert_bitcast_fusion
  126.2 0.1 copy.28
  126.4 1.2 slice_bitcast_fusion
  (7 shorter events, 0.0 us)
Async XLA Ops:
  0.6 12.1 %copy-start.6 = (bf16[2,256,256]{2,1,0:T(8,128)(2,1)S(1)}, bf16[2,256,256]{2,1,0:T(8,128)(2,1)}, u32[]{:S(2)}) copy-start(bf16[2,256,256]{2,1,0:T(8,128)(2,1)} %refs_6_.4) | copy-start | bytes 786436
  0.6 11.6 %copy-start.5 = (bf16[2,256,256]{2,1,0:T(8,128)(2,1)S(1)}, bf16[2,256,256]{2,1,0:T(8,128)(2,1)}, u32[]{:S(2)}) copy-start(bf16[2,256,256]{2,1,0:T(8,128)(2,1)} %refs_5_.4) | copy-start | bytes 786436
  0.7 11.5 %copy-start.4 = (bf16[2,256,256]{2,1,0:T(8,128)(2,1)S(1)}, bf16[2,256,256]{2,1,0:T(8,128)(2,1)}, u32[]{:S(2)}) copy-start(bf16[2,256,256]{2,1,0:T(8,128)(2,1)} %refs_4_.7) | copy-start | bytes 786436
  0.7 12.1 %copy-start.3 = (s32[12,8]{0,1:T(8,128)S(1)}, s32[12,8]{0,1:T(8,128)}, u32[]{:S(2)}) copy-start(s32[12,8]{0,1:T(8,128)} %param.13) | copy-start | bytes 1156
  4.8 16.2 %all-to-all-start = ((bf16[8,64,256]{2,1,0:T(8,128)(2,1)}), bf16[8,64,256]{2,1,0:T(8,128)(2,1)S(1)}, u32[]{:S(2)}, u32[]{:S(2)}) async-start(bf16[8,64,256]{2,1,0:T(8,128)(2,1)} %bitcast.25), calls=%async_computation | async-start | bytes 524288 | tf_op jit(solution)/shard_map/all_to_all | solution.py:452
  12.1 7.7 %collective-permute-start = (bf16[2,256,256]{2,1,0:T(8,128)(2,1)S(1)}, bf16[2,256,256]{2,1,0:T(8,128)(2,1)S(1)}, u32[]{:S(2)}, u32[]{:S(2)}) collective-permute-start(bf16[2,256,256]{2,1,0:T(8,128)(2,1)S(1)} %copy-done.4), channel_id=1, source_target_pairs={{0,1},{1,0},{2,3},{3,2},{4,5},{5,4},{6,7},{7,6},{8,9},{9,8},{10,11... | collective-permute-start | bytes 786440 | tf_op jit(solution)/shard_map/ppermute | solution.py:494
  12.2 7.7 %collective-permute-start.1 = (bf16[2,256,256]{2,1,0:T(8,128)(2,1)S(1)}, bf16[2,256,256]{2,1,0:T(8,128)(2,1)S(1)}, u32[]{:S(2)}, u32[]{:S(2)}) collective-permute-start(bf16[2,256,256]{2,1,0:T(8,128)(2,1)S(1)} %copy-done.5), channel_id=1, source_target_pairs={{0,1},{1,0},{2,3},{3,2},{4,5},{5,4},{6,7},{7,6},{8,9},{9,8},{10,11... | collective-permute-start | bytes 786440 | tf_op jit(solution)/shard_map/ppermute | solution.py:494
  12.7 7.2 %collective-permute-start.2 = (bf16[2,256,256]{2,1,0:T(8,128)(2,1)S(1)}, bf16[2,256,256]{2,1,0:T(8,128)(2,1)S(1)}, u32[]{:S(2)}, u32[]{:S(2)}) collective-permute-start(bf16[2,256,256]{2,1,0:T(8,128)(2,1)S(1)} %copy-done.6), channel_id=1, source_target_pairs={{0,1},{1,0},{2,3},{3,2},{4,5},{5,4},{6,7},{7,6},{8,9},{9,8},{10,11... | collective-permute-start | bytes 786440 | tf_op jit(solution)/shard_map/ppermute | solution.py:494
  19.9 1.2 copy-start.7
  19.9 1.2 copy-start.8
  19.9 1.2 copy-start.9
  21.1 0.7 copy-start
  28.7 14.5 %all-to-all-start.1 = ((bf16[8,64,256]{2,1,0:T(8,128)(2,1)}), bf16[8,64,256]{2,1,0:T(8,128)(2,1)S(1)}, u32[]{:S(2)}, u32[]{:S(2)}) async-start(bf16[8,64,256]{2,1,0:T(8,128)(2,1)} %bitcast.29), calls=%async_computation.1 | async-start | bytes 524288 | tf_op jit(solution)/shard_map/all_to_all | solution.py:452
  43.2 0.7 copy-start.2
  53.0 12.7 %all-to-all-start.2 = ((bf16[8,64,256]{2,1,0:T(8,128)(2,1)}), bf16[8,64,256]{2,1,0:T(8,128)(2,1)S(1)}, u32[]{:S(2)}, u32[]{:S(2)}) async-start(bf16[8,64,256]{2,1,0:T(8,128)(2,1)} %bitcast.28), calls=%async_computation.2 | async-start | bytes 524288 | tf_op jit(solution)/shard_map/all_to_all | solution.py:452
  65.7 3.7 %copy-start.1 = (bf16[8,64,256]{2,1,0:T(8,128)(2,1)}, bf16[8,64,256]{2,1,0:T(8,128)(2,1)S(1)}, u32[]{:S(2)}) copy-start(bf16[8,64,256]{2,1,0:T(8,128)(2,1)S(1)} %all-to-all-done.2) | copy-start | bytes 786436
  65.7 15.0 %all-to-all-start.3 = ((bf16[8,96,256]{2,1,0:T(8,128)(2,1)}), bf16[8,96,256]{2,1,0:T(8,128)(2,1)S(1)}, u32[]{:S(2)}, u32[]{:S(2)}) async-start(bf16[8,96,256]{2,1,0:T(8,128)(2,1)} %bitcast.6), calls=%async_computation.3 | async-start | bytes 786432 | tf_op jit(solution)/shard_map/all_to_all | solution.py:452
  102.9 23.2 %all-to-all-start.5 = ((bf16[8,192,256]{2,1,0:T(8,128)(2,1)}), bf16[8,192,256]{2,1,0:T(8,128)(2,1)S(1)}, u32[]{:S(2)}, u32[]{:S(2)}) async-start(bf16[8,192,256]{2,1,0:T(8,128)(2,1)} %broadcast_in_dim.2), calls=%async_computation.5 | async-start | bytes 1572864 | tf_op jit(solution)/shard_map/all_to_all | solution.py:452
where the time goes:
time: 129 us; the launch traced here: 128 us
  Pallas kernels  56.8 us (44%)
  starting transfers between devices  23.8 us (18%)
  blocking collectives  21.1 us (16%)
  waiting for transfers between devices  18.8 us (15%)
  local copies, waits for them, and re-layouts  5.08 us (4%)
  between operations  1.58 us (1%)
    pallas_call x9, Pallas kernels, call(): pl.pallas_call(body, out_shape=[x for x, _ in outs], in_specs=[SMEM] * sc...  56.8 us
    all_to_all x5, starting transfers between devices, swap(): lax.all_to_all(blocks, 'dom', split_axis=0, concat_axis=0, tiled=True)  23.1 us
    all_to_all x1, blocking collectives, swap(): lax.all_to_all(blocks, 'dom', split_axis=0, concat_axis=0, tiled=True)  21.1 us
    all_to_all x5, waiting for transfers between devices, swap(): lax.all_to_all(blocks, 'dom', split_axis=0, concat_axis=0, tiled=True)  18.8 us
  transfers between devices with their start and end apart: 8, of which 5 were waited for; matrix products, arithmetic and copies ran while one was open for 1% of the time, Pallas kernels for 29%

commit v1 on v0

v1 whole, which is shorter than its diff:
```python
import functools

import jax
import jax.numpy as jnp
from jax import lax
from jax.experimental import pallas as pl
from jax.experimental.pallas import tpu as pltpu
from jax.sharding import PartitionSpec as P

BF16 = jnp.bfloat16
F32 = jnp.float32
LANES = 128
BLOCK = 128
SMEM = pl.BlockSpec(memory_space=pltpu.SMEM)
SUB = 512
SLOTS = 512
GRANT = 48 * 1024 * 1024
TILE_COPIES = 3


def shape(dims, dtype):
    return jax.ShapeDtypeStruct(tuple(dims), dtype)


class Layer:
    def __init__(self, index):
        self.index = index


class Traffic:
    def __init__(self, ins, outs, in_sems, out_sems):
        self.ins, self.outs, self.in_sems, self.out_sems = ins, outs, in_sems, out_sems
        self.leaving = []
        for k in range(len(ins)):
            if self.moves(k):
                self.arriving(k).start()

    def moves(self, k):
        return self.ins[k][2] not in ("near", "later")

    def arriving(self, k):
        far, near, cut = self.ins[k]
        source = far.at[cut.index] if isinstance(cut, Layer) else far
        return pltpu.make_async_copy(source, near, self.in_sems.at[k])

    def need(self, *names):
        for k, (_, near, _) in enumerate(self.ins):
            if self.moves(k) and any(near is name for name in names):
                self.arriving(k).wait()

    def put(self, k):
        near, far, cut = self.outs[k]
        if cut != "near":
            copy = pltpu.make_async_copy(near, far, self.out_sems.at[k])
            copy.start()
            self.leaving.append(copy)

    def finish(self):
        for copy in self.leaving:
            copy.wait()


def call(kernel, outs, ins, flops, name, scratch=()):
    moved = sum(x.size * x.dtype.itemsize for x, _ in (*ins, *outs))
    far_ins = [(x, cut) for x, cut in ins if cut is not None]
    scalars = len(ins) - len(far_ins)
    staged = [k for k, (_, cut) in enumerate(far_ins) if cut not in ("near", "later")]
    staged_outs = [k for k, (_, cut) in enumerate(outs) if cut not in ("near", "later")]

    def body(*refs):
        fixed, refs = refs[:scalars], refs[scalars:]
        far_in, refs = refs[: len(far_ins)], refs[len(far_ins) :]
        far_out, refs = refs[: len(outs)], refs[len(outs) :]
        near_in, near_out = list(far_in), list(far_out)
        for k in staged:
            near_in[k], *refs = refs
        for k in staged_outs:
            near_out[k], *refs = refs
        in_sems, out_sems, *own = refs
        traffic = Traffic(
            [(f, n, cut) for f, n, (_, cut) in zip(far_in, near_in, far_ins)],
            [(n, f, cut) for n, f, (_, cut) in zip(near_out, far_out, outs)],
            in_sems,
            out_sems,
        )
        shown = [near_out[k] for k in range(len(outs)) if outs[k][1] != "later"]
        kernel(traffic, *fixed, *near_in, *shown, *own)
        traffic.finish()

    def held(x, cut):
        if cut == "scalars":
            return pltpu.SMEM(x.shape, x.dtype)
        return pltpu.VMEM(x.shape[1:] if isinstance(cut, Layer) else x.shape, x.dtype)

    def space(cut):
        return pltpu.VMEM if cut == "near" else pltpu.HBM

    return pl.pallas_call(
        body,
        out_shape=[space(cut)(x.shape, x.dtype) for x, cut in outs],
        in_specs=[SMEM] * scalars + [pl.BlockSpec(memory_space=space(cut)) for _, cut in far_ins],
        out_specs=[pl.BlockSpec(memory_space=space(cut)) for _, cut in outs],
        scratch_shapes=[
            *(held(*far_ins[k]) for k in staged),
            *(held(*outs[k]) for k in staged_outs),
            pltpu.SemaphoreType.DMA((len(far_ins),)),
            pltpu.SemaphoreType.DMA((len(outs),)),
            *scratch,
        ],
        cost_estimate=pl.CostEstimate(flops=flops, bytes_accessed=moved, transcendentals=0),
        compiler_params=pltpu.CompilerParams(vmem_limit_bytes=GRANT),
        name=name,
    )(
        *[x for x, _ in ins[:scalars]],
        *[pltpu.with_memory_space_constraint(x, space(cut)) for x, cut in far_ins],
    )


def pieces_of(rows):
    size = SUB if rows % SUB == 0 else BLOCK
    return [slice(first, first + size) for first in range(0, rows, size)]


def mm(a, b):
    return jnp.dot(a, b, preferred_element_type=F32)


def mm_t(a, b):
    return lax.dot_general(a, b, (((1,), (1,)), ((), ())), preferred_element_type=F32)


def mm_rows(a, b):
    return lax.dot_general(a, b, (((0,), (0,)), ((), ())), preferred_element_type=F32)


def live(count_ref, start, rows, width):
    index = lax.broadcasted_iota(jnp.int32, (rows, width), 0) + start
    return index < count_ref[0]


def fill_columns(col_ref, list_ref, used):
    peers, n = list_ref.shape[1:]
    w = col_ref.shape[0] // peers
    down = lax.broadcasted_iota(jnp.int32, (w, n), 0) + lax.axis_index("mp") * w
    across = lax.broadcasted_iota(jnp.int32, (w, n), 1)

    def step(q, carry):
        line = jnp.broadcast_to(list_ref[0, pl.ds(q, 1), :], (w, n))
        kept = (down == across) & used(q, across, line)
        col = jnp.sum(jnp.where(kept, line + 1, 0), axis=1, keepdims=True) - 1
        col_ref[pl.ds(pl.multiple_of(q * w, w), w), :] = jnp.broadcast_to(col, (w, LANES))
        return carry

    lax.fori_loop(0, peers, step, 0, unroll=4)


def fill_row(parts, row_ref, list_ref, used):
    peers, n = list_ref.shape[1:]
    w = n // parts
    across = lax.broadcasted_iota(jnp.int32, (1, n), 1)
    me = lax.axis_index("mp")
    for q in range(peers):
        line = list_ref[0, q : q + 1, :]
        line = jnp.where(used(q, across, line), line, -1)
        for t in range(parts):
            owner = lax.rem(me + t, parts)
            piece = line[:, :w]
            for p in range(1, parts):
                piece = jnp.where(owner == p, line[:, p * w : (p + 1) * w], piece)
            row_ref[0:1, (t * peers + q) * w : (t * peers + q + 1) * w] = piece


def sent(count_ref, used_ref):
    return lambda q, k, row: (k < used_ref[0, q]) & (row < count_ref[0])


def always(q, k, row):
    return row >= 0


def picks(col, rows):
    lanes = lax.broadcasted_iota(jnp.int32, col.shape, 1)
    return jnp.concatenate(
        [jnp.where(col == lanes + lane, 1.0, 0.0).astype(BF16) for lane in range(0, rows, LANES)], axis=1
    )


def gather_rows(col_ref, source_ref, out_ref):
    slots, rows = out_ref.shape[0], source_ref.shape[0]
    size = min(slots, SLOTS)
    for first in range(0, slots, size):
        at = slice(first, first + size)
        out_ref[at, :] = mm(picks(col_ref[at, :], rows), source_ref[...]).astype(BF16)


def scatter_rows(row_ref, start, rows, arriving):
    slots = row_ref.shape[1] // len(arriving)
    index = lax.broadcasted_iota(jnp.int32, (rows, slots), 0) + start
    total = None
    for t, ref in enumerate(arriving):
        pick = jnp.where(row_ref[0:1, t * slots : (t + 1) * slots] == index, 1.0, 0.0).astype(BF16)
        total = mm(pick, ref[...]) if total is None else total + mm(pick, ref[...])
    return total


def send_kernel(traffic, count_ref, used_ref, list_ref, feats_ref, out_ref, col_ref, pick_ref):
    traffic.need(used_ref, list_ref)
    fill_columns(col_ref, list_ref, sent(count_ref, used_ref))
    traffic.put(1)
    pick_ref[...] = picks(col_ref[...], feats_ref.shape[0])
    traffic.need(feats_ref)
    out_ref[...] = mm(pick_ref[...], feats_ref[...]).astype(BF16)
    traffic.put(0)


class Dense:
    def __init__(self, cols_ref, tile_ref, near_ref, dense_ref, sems):
        self.cols_ref, self.near_ref, self.dense_ref = cols_ref, near_ref, dense_ref
        pieces = sems.shape[0]
        self.size = tile_ref.shape[0] // pieces
        self.copies = [
            pltpu.make_async_copy(
                tile_ref.at[pl.ds(p * self.size, self.size)], near_ref.at[pl.ds(p * self.size, self.size)], sems.at[p]
            )
            for p in range(pieces)
        ]
        for copy in self.copies:
            copy.start()

    def zero(self):
        self.dense_ref[...] = jnp.zeros_like(self.dense_ref)

    def fill(self, p):
        self.copies[p].wait()
        for r in range(p * self.size, (p + 1) * self.size):
            for j in range(self.near_ref.shape[1]):
                at = pl.ds(pl.multiple_of(self.cols_ref[r, j] * BLOCK, BLOCK), BLOCK)
                self.dense_ref[r * BLOCK : (r + 1) * BLOCK, at] = self.near_ref[r, j]


def local_sums(traffic, dense, state_ref, sum_ref, out):
    for p in range(len(dense.copies)):
        dense.fill(p)
    sum_ref[...] = mm(dense.dense_ref[...], state_ref[...]).astype(sum_ref.dtype)
    traffic.put(out)


def first_local_kernel(
    parts, traffic, count_ref, used_ref, cols_ref, send_ref, recv_ref, feats_ref, tile_ref,
    state_ref, sum_ref, send_row_ref, recv_row_ref, recv_col_ref, near_ref, dense_ref, sems,
):
    dense = Dense(cols_ref, tile_ref, near_ref, dense_ref, sems)
    dense.zero()
    rows, width = feats_ref.shape
    traffic.need(send_ref, recv_ref, feats_ref)
    fill_row(parts, send_row_ref, send_ref, sent(count_ref, used_ref))
    fill_row(parts, recv_row_ref, recv_ref, always)
    fill_columns(recv_col_ref, recv_ref, always)
    state_ref[...] = jnp.where(live(count_ref, 0, rows, width), feats_ref[...], jnp.zeros((), BF16))
    for k in (0, 2, 3, 4):
        traffic.put(k)
    local_sums(traffic, dense, state_ref, sum_ref, 1)


def local_kernel(traffic, cols_ref, state_ref, tile_ref, sum_ref, near_ref, dense_ref, sems):
    dense = Dense(cols_ref, tile_ref, near_ref, dense_ref, sems)
    dense.zero()
    local_sums(traffic, dense, state_ref, sum_ref, 0)


def turned_local_kernel(traffic, count_ref, cols_ref, agg_ref, up_ref, tile_ref, sum_ref, near_ref, dense_ref, sems):
    dense = Dense(cols_ref, tile_ref, near_ref, dense_ref, sems)
    dense.zero()
    for p in range(len(dense.copies)):
        dense.fill(p)
    traffic.need(up_ref)
    upstream = jnp.where(live(count_ref, 0, *sum_ref.shape), up_ref[...].astype(F32), 0.0)
    sum_ref[...] = (mm_rows(dense_ref[...], agg_ref[...]) + upstream).astype(sum_ref.dtype)
    traffic.put(0)


def triples(refs, layer):
    return [(refs[i].at[layer], refs[i + 1].at[layer], refs[i + 2]) for i in range(0, len(refs), 3)]


def gates(acts, weights):
    result = []
    for gate_ref, up_ref, _ in weights:
        gate = mm(acts, gate_ref[...])
        up = mm(acts, up_ref[...])
        sig = 0.5 * jnp.tanh(0.5 * gate) + 0.5
        result.append((gate, up, sig, gate * sig))
    return result


def layer_grads(at, acts, terms, down_in, weights, agg_ref, kept):
    agg = None
    for part, ((gate, up, sig, silu), (gate_ref, up_ref, down_ref)) in enumerate(zip(terms, weights)):
        hidden_grad = mm_t(down_in, down_ref[...])
        slope = sig * (1.0 + gate * (1.0 - sig))
        gate_grad = (hidden_grad * up * slope).astype(BF16)
        up_grad = (hidden_grad * silu).astype(BF16)
        more = mm_t(gate_grad, gate_ref[...]) + mm_t(up_grad, up_ref[...])
        agg = more if agg is None else agg + more
        if part == 0:
            for ref, value in zip(kept, ((silu * up).astype(BF16), gate_grad, up_grad, down_in)):
                ref[at, :] = value
    agg_ref[at, :] = agg.astype(BF16)


def weight_grads(acts_ref, kept, dw_ref):
    hidden_ref, gate_ref, up_ref, down_ref = kept
    pairs = ((acts_ref, gate_ref), (acts_ref, up_ref), (hidden_ref, down_ref))
    for k, (left_ref, right_ref) in enumerate(pairs):
        size = left_ref.shape[1]
        dw_ref[k * size : (k + 1) * size, :] = mm_rows(left_ref[...], right_ref[...]).astype(BF16)


def mix(terms, weights):
    mixed = None
    for (gate, up, sig, silu), (_, _, down_ref) in zip(terms, weights):
        part = mm((silu * up).astype(BF16), down_ref[...])
        mixed = part if mixed is None else mixed + part
    return mixed


def forward_kernel(parts, layer, traffic, count_ref, col_ref, row_ref, *refs):
    arriving, refs = refs[:parts], refs[parts:]
    weights = triples(refs[: 3 * parts], layer)
    sum_ref, state_ref, acts_ref, next_ref, out_ref = refs[3 * parts :]
    width = state_ref.shape[1]
    for at in pieces_of(state_ref.shape[0]):
        size = at.stop - at.start
        acts = (sum_ref[at, :].astype(F32) + scatter_rows(row_ref, at.start, size, arriving)).astype(BF16)
        acts_ref[at, :] = acts
        terms = gates(acts, weights)
        if at.start == 0:
            traffic.need(*(down_ref for _, _, down_ref in weights))
        after = state_ref[at, :].astype(F32) + mix(terms, weights)
        next_ref[at, :] = jnp.where(live(count_ref, at.start, size, width), after, 0.0).astype(BF16)
    traffic.put(0)
    gather_rows(col_ref, next_ref, out_ref)
    traffic.put(2)


def turn_kernel(parts, layer, traffic, count_ref, col_ref, row_ref, *refs):
    arriving, refs = refs[:parts], refs[parts:]
    weights = triples(refs[: 3 * parts], layer)
    sum_ref, state_ref, grad_ref, final_ref, agg_ref, out_ref, dw_ref, acts_ref, *kept = refs[3 * parts :]
    width = state_ref.shape[1]
    for at in pieces_of(state_ref.shape[0]):
        size = at.stop - at.start
        acts = (sum_ref[at, :].astype(F32) + scatter_rows(row_ref, at.start, size, arriving)).astype(BF16)
        acts_ref[at, :] = acts
        terms = gates(acts, weights)
        if at.start == 0:
            traffic.need(*(down_ref for _, _, down_ref in weights), grad_ref)
        after = state_ref[at, :].astype(F32) + mix(terms, weights)
        alive = live(count_ref, at.start, size, width)
        final_ref[at, :] = jnp.where(alive, after, 0.0).astype(BF16)
        down_in = jnp.where(alive, grad_ref[at, :], jnp.zeros((), BF16))
        layer_grads(at, acts, terms, down_in, weights, agg_ref, kept)
    traffic.put(0)
    gather_rows(col_ref, agg_ref, out_ref)
    traffic.put(2)
    weight_grads(acts_ref, kept, dw_ref)
    traffic.put(3)


def put_pieces(traffic, k, sources, sem):
    far = traffic.outs[k][1]
    for q in range(far.shape[0]):
        first = 0
        for source in sources:
            rows = source.shape[0] // far.shape[0]
            copy = pltpu.make_async_copy(
                source.at[pl.ds(q * rows, rows)], far.at[q, pl.ds(first, rows)], sem.at[q]
            )
            copy.start()
            traffic.leaving.append(copy)
            first += rows


def backward_kernel(parts, layer, traffic, count_ref, col_ref, row_ref, *refs):
    arriving, refs = refs[:parts], refs[parts:]
    weights = triples(refs[: 3 * parts], layer)
    sum_ref, acts_ref, upstream_ref, agg_ref, out_ref, dw_ref, sem, *kept = refs[3 * parts :]
    rows, width = acts_ref.shape
    for at in pieces_of(rows):
        size = at.stop - at.start
        carried = sum_ref[at, :].astype(F32) + scatter_rows(row_ref, at.start, size, arriving)
        upstream_ref[at, :] = jnp.where(live(count_ref, at.start, size, width), carried, 0.0).astype(BF16)
    traffic.put(0)
    traffic.need(acts_ref, *(down_ref for _, _, down_ref in weights))
    for at in pieces_of(rows):
        acts = acts_ref[at, :]
        layer_grads(at, acts, gates(acts, weights), upstream_ref[at, :], weights, agg_ref, kept)
    gather_rows(col_ref, agg_ref, out_ref)
    weight_grads(acts_ref, (*kept, upstream_ref), dw_ref)
    put_pieces(traffic, 2, (out_ref, dw_ref), sem)


def last_kernel(traffic, count_ref, row_ref, *refs):
    *arriving, sum_ref, out_ref = refs
    width = out_ref.shape[1]
    for at in pieces_of(out_ref.shape[0]):
        size = at.stop - at.start
        carried = sum_ref[at, :].astype(F32) + scatter_rows(row_ref, at.start, size, arriving)
        out_ref[at, :] = jnp.where(live(count_ref, at.start, size, width), carried, 0.0)
    traffic.put(0)


def local(
    feats,
    cell_count,
    tile_col,
    tile_val,
    send_list,
    send_count,
    recv_list,
    gate_weight_matrix,
    w_up,
    w_down,
    out_grad,
):
    rows, width = feats.shape
    peers, slot_count = send_list.shape[1:]
    slots = peers * slot_count
    layers = gate_weight_matrix.shape[0]
    hidden_width = gate_weight_matrix.shape[2]
    parts = lax.axis_size("mp")

    turns = [[(d, (d - t) % parts) for d in range(parts)] for t in range(1, parts)]

    def swap(blocks):
        return lax.all_to_all(blocks, "dom", split_axis=0, concat_axis=0, tiled=True)

    def share(rows):
        rows = rows.reshape(slots // parts, width)
        return [rows] + [lax.ppermute(rows, "mp", turn) for turn in turns]

    def exchange(outgoing):
        return swap(outgoing.reshape(peers, slot_count // parts, width))

    def share_after(total, moved):
        total, moved = lax.optimization_barrier((total, moved))
        return total, share(moved)

    def far(x):
        return x, "far"

    def near(x):
        return x, "near"

    state_shape, sum_shape = shape((rows, width), BF16), shape((rows, width), BF16)
    slot_shape = shape((slots // parts, width), BF16)
    dense_scratch = [
        pltpu.VMEM(tile_val.shape, BF16),
        pltpu.VMEM((rows, rows), BF16),
        pltpu.SemaphoreType.DMA((TILE_COPIES,)),
    ]
    tiles, cols = (tile_val, "later"), (tile_col, None)
    row_shape, col_shape = shape((1, slots), jnp.int32), shape((slots // parts, LANES), jnp.int32)
    dw_shape = shape((3 * width, hidden_width), BF16)
    half = pltpu.VMEM((rows, hidden_width), BF16)
    kept_shapes = [half, half, half, pltpu.VMEM((rows, width), BF16)]
    local_flops = 2 * rows * rows * width
    slot_flops = 2 * rows * slots * width
    layer_flops = 6 * rows * width * hidden_width * parts
    count = (cell_count, None)

    outgoing, send_col = call(
        send_kernel,
        [far(slot_shape), near(col_shape)],
        [count, (send_count, "scalars"), far(send_list), far(feats)],
        slot_flops,
        "send",
        [pltpu.VMEM((slots // parts, rows), BF16)],
    )
    outgoing, mine = lax.optimization_barrier((outgoing, (gate_weight_matrix, w_up, w_down)))
    arriving = exchange(outgoing)
    held = [mine] + [tuple(lax.ppermute(w, "mp", turn) for w in mine) for turn in turns]

    def weights(layer):
        return [spec for gate, up, down in held for spec in (near(gate), near(up), (down, Layer(layer)))]

    state, total, send_row, recv_row, recv_col = call(
        functools.partial(first_local_kernel, parts),
        [
            near(state_shape),
            near(sum_shape),
            near(row_shape),
            near(row_shape),
            near(col_shape),
        ],
        [
            count,
            (send_count, None),
            cols,
            far(send_list),
            far(recv_list),
            far(feats),
            tiles,
        ],
        local_flops,
        "first_local",
        dense_scratch,
    )
    total, arriving = share_after(total, arriving)
    kept = []
    for layer in range(layers - 1):
        acts, state, outgoing = call(
            functools.partial(forward_kernel, parts, layer),
            [far(state_shape), near(state_shape), far(slot_shape)],
            [count, near(send_col), near(recv_row), *map(near, arriving), *weights(layer), near(total), near(state)],
            layer_flops + 2 * slot_flops,
            "forward",
        )
        kept.append(acts)
        arriving = exchange(outgoing)
        (total,) = call(
            local_kernel, [near(sum_shape)], [cols, near(state), tiles], local_flops, "local", dense_scratch
        )
        total, arriving = share_after(total, arriving)
    final, agg, outgoing, dw = call(
        functools.partial(turn_kernel, parts, layers - 1),
        [far(state_shape), near(state_shape), far(slot_shape), far(dw_shape)],
        [
            count, near(recv_col), near(recv_row), *map(near, arriving), *weights(layers - 1), near(total),
            near(state), far(out_grad),
        ],
        3 * layer_flops + 2 * slot_flops,
        "turn",
        [pltpu.VMEM((rows, width), BF16), *kept_shapes],
    )
    piece = dw_shape.shape[0] // peers
    own_slots = slot_count // parts
    both_shape = shape((peers, own_slots + piece, width), BF16)

    def turned_local(agg, upstream):
        return call(
            turned_local_kernel,
            [near(sum_shape)],
            [count, cols, near(agg), far(upstream), tiles],
            local_flops,
            "turned_local",
            dense_scratch,
        )[0]

    def added(pieces):
        return jnp.sum(pieces.astype(F32), axis=0).astype(BF16)

    arriving = exchange(outgoing)
    total, arriving = share_after(turned_local(agg, out_grad), arriving)
    reduced = [None] * layers
    for layer in reversed(range(layers - 1)):
        if layer == layers - 2:
            arriving, dw = lax.optimization_barrier((arriving, dw))
            pieces = swap(dw.reshape(peers, piece, width))
        upstream, agg, both = call(
            functools.partial(backward_kernel, parts, layer),
            [far(sum_shape), near(state_shape), (both_shape, "later")],
            [
                count, near(recv_col), near(send_row), *map(near, arriving), *weights(layer), near(total),
                far(kept[layer]),
            ],
            3 * layer_flops + 2 * slot_flops,
            "backward",
            [
                pltpu.VMEM(slot_shape.shape, BF16),
                pltpu.VMEM(dw_shape.shape, BF16),
                pltpu.SemaphoreType.DMA((peers,)),
                *kept_shapes[:3],
            ],
        )
        if layer == layers - 2:
            both, pieces = lax.optimization_barrier((both, pieces))
            reduced[layer + 1] = added(pieces)
        both = swap(both)
        total, both = lax.optimization_barrier((turned_local(agg, upstream), both))
        arriving = share(both[:, :own_slots])
        reduced[layer] = added(both[:, own_slots:])
    own = jnp.concatenate(reduced)
    full = swap(jnp.broadcast_to(own[None], (peers, *own.shape)))
    (feat_grad,) = call(
        last_kernel,
        [far(shape((rows, width), F32))],
        [count, near(send_row), *map(near, arriving), near(total)],
        slot_flops,
        "last",
    )
    full = full.reshape(peers, layers, piece, width).swapaxes(0, 1).reshape(layers, 3, width, hidden_width)
    full = full.swapaxes(0, 1).astype(F32)
    return (final, feat_grad, full[0], full[1], full[2])


def solution(mesh):
    return jax.shard_map(
        local,
        mesh=mesh,
        in_specs=(
            P(("groups", "dom"), None),
            P(("groups", "dom")),
            P(("groups", "dom"), None),
            P(("groups", "dom"), None, None, None),
            P(("groups", "dom"), None, None),
            P(("groups", "dom"), None),
            P(("groups", "dom"), None, None),
            P(None, None, "mp"),
            P(None, None, "mp"),
            P(None, "mp", None),
            P(("groups", "dom"), None),
        ),
        out_specs=(
            P(("groups", "dom"), None),
            P(("groups", "dom"), None),
            P("groups", None, "mp"),
            P("groups", None, "mp"),
            P("groups", "mp", None),
        ),
        check_vma=False,
    )
```

time: 129 us -> 120 us (0.930)
  waiting for transfers between devices: 18.8 us -> 44.7 us
  blocking collectives: 21.1 us -> 0 us
  Pallas kernels: 56.8 us -> 38 us
  starting transfers between devices: 23.8 us -> 27.7 us
  local copies, waits for them, and re-layouts: 5.08 us -> 6.94 us
    all_to_all x1 -> x0, blocking collectives: 21.1 us -> none  [swap(): lax.all_to_all(blocks, 'dom', split_axis=0, concat_axis=0, tiled=True)]
    all_to_all x5 -> x6, waiting for transfers between devices: 18.8 us -> 39.3 us  [swap(): lax.all_to_all(blocks, 'dom', split_axis=0, concat_axis=0, tiled=True)]
    pallas_call x9, Pallas kernels: 56.8 us -> 38 us  [call(): pl.pallas_call(body, out_shape=[space(cut)(x.shape, x.dtype) for x, cut i...]
    ppermute x0 -> x4, waiting for transfers between devices: none -> 5.34 us  [share(): return [rows] + [lax.ppermute(rows, 'mp', turn) for turn in turns]]
    all_to_all x5 -> x6, starting transfers between devices: 23.1 us -> 27 us  [swap(): lax.all_to_all(blocks, 'dom', split_axis=0, concat_axis=0, tiled=True)]
    unnamed x21 -> x27, local copies, waits for them, and re-layouts: 2.11 us -> 4.68 us
  transfers between devices with their start and end apart: 8 -> 13, of which waited for: 5 -> 10; matrix products, arithmetic and copies ran while one was open for 1% -> 0% of each run, Pallas kernels for 29% -> 22%
where the time goes in v1:
time: 120 us; the launch traced here: 119 us
  waiting for transfers between devices  44.7 us (37%)
  Pallas kernels  38 us (32%)
  starting transfers between devices  27.7 us (23%)
  local copies, waits for them, and re-layouts  6.94 us (6%)
  between operations  1.61 us (1%)
    all_to_all x6, waiting for transfers between devices, swap(): lax.all_to_all(blocks, 'dom', split_axis=0, concat_axis=0, tiled=True)  39.3 us
    pallas_call x9, Pallas kernels, call(): pl.pallas_call(body, out_shape=[space(cut)(x.shape, x.dtype) for x, cut i...  38 us
    all_to_all x6, starting transfers between devices, swap(): lax.all_to_all(blocks, 'dom', split_axis=0, concat_axis=0, tiled=True)  27 us
    ppermute x4, waiting for transfers between devices, share(): return [rows] + [lax.ppermute(rows, 'mp', turn) for turn in turns]  5.34 us
    unnamed x27, local copies, waits for them, and re-layouts  4.68 us
  transfers between devices with their start and end apart: 13, of which 10 were waited for; matrix products, arithmetic and copies ran while one was open for 0% of the time, Pallas kernels for 22%

profile of v1, /device:TPU:0, one launch (start us, length us, event | category | flops | bytes accessed | tf_op | source)
XLA Modules:
  0.0 119.2 jit_solution(4989390819852941341)
XLA Ops:
  0.6 0.0 copy-start.11
  1.4 2.2 %send.1 = (bf16[256,256]{1,0:T(8,128)(2,1)}, s32[256,128]{1,0:T(8,128)S(1)}) custom-call(s32[1]{0:T(128)S(6)} %copy.29.refs_0_, s32[1,8]{1,0:T(1,128)} %refs_1_.5, s32[1,8,64]{2,1,0:T(8,128)} %refs_2_.3, bf16[1536,256]{1,0:T(8,128)(2,1)} %refs_3_.4), custom_call_target="tpu_custom_call" | custom-call | flops 402653184 | bytes 1050660 | tf_op jit(solution)/shard_map/send/pallas_call | solution.py:98
  3.6 7.3 %all-to-all-start = ((bf16[8,32,256]{2,1,0:T(8,128)(2,1)}), bf16[8,32,256]{2,1,0:T(8,128)(2,1)S(1)}, u32[]{:S(2)}, u32[]{:S(2)}) async-start(bf16[8,32,256]{2,1,0:T(8,128)(2,1)} %bitcast.31), calls=%async_computation | async-start | bytes 262144 | tf_op jit(solution)/shard_map/all_to_all | solution.py:436
  11.0 0.1 collective-permute-start.1
  11.0 0.5 collective-permute-start.2
  11.5 0.1 collective-permute-start.3
  11.6 0.1 copy.24.refs_2_.refs_0_.refs_1_
  11.7 5.0 %first_local.1 = (bf16[1536,256]{1,0:T(8,128)(2,1)S(1)}, bf16[1536,256]{1,0:T(8,128)(2,1)S(1)}, s32[1,512]{1,0:T(1,128)S(1)}, s32[1,512]{1,0:T(1,128)S(1)}, s32[256,128]{1,0:T(8,128)S(1)}) custom-call(s32[1]{0:T(128)S(6)} %copy.29.refs_0_, s32[1,8]{1,0:T(1,128)S(1)} %copy-done.2, s32[12,8]{1,0:T(8,128)S(1)} %copy.24.refs_2_.refs_0_.refs_1_, ...), custom_call_target="tpu_custom_call" | custom-call | flops 1207959552 | bytes 5644708 | tf_op jit(solution)/shard_map/first_local/pallas_call | solution.py:98
  16.8 0.0 copy-start.3
  16.8 0.9 copy-done.3
  17.6 0.7 all-to-all-done
  18.3 0.0 collective-permute-start
  18.3 0.0 collective-permute-done.1.refs_8_
  18.3 0.0 copy-start.12
  18.3 1.3 %collective-permute-done.refs_4_ = bf16[256,256]{1,0:T(8,128)(2,1)S(1)} collective-permute-done((bf16[256,256]{1,0:T(8,128)(2,1)S(1)}, bf16[256,256]{1,0:T(8,128)(2,1)S(1)}, u32[]{:S(2)}, u32[]{:S(2)}) %collective-permute-start) | collective-permute-done | bytes 131104 | tf_op jit(solution)/shard_map/ppermute | solution.py:440
  19.7 1.1 copy-done.4
  20.8 3.6 %forward.1 = (bf16[1536,256]{1,0:T(8,128)(2,1)}, bf16[1536,256]{1,0:T(8,128)(2,1)S(1)}, bf16[256,256]{1,0:T(8,128)(2,1)}) custom-call(s32[1]{0:T(128)S(6)} %copy.29.refs_0_, s32[256,128]{1,0:T(8,128)S(1)} %get-tuple-element.41.refs_1_, s32[1,512]{1,0:T(1,128)S(1)} %get-tuple-element.40.refs_2_, bf16[256,256]{1,0:T(8,128)(2,1)S(1)} %bitcast.24, ...), custom_call_target="tpu_custom_call" | custom-call | flops 2013265920 | bytes 5244932 | tf_op jit(solution)/shard_map/forward/pallas_call | solution.py:98
  24.4 5.3 %all-to-all-start.1 = ((bf16[8,32,256]{2,1,0:T(8,128)(2,1)}), bf16[8,32,256]{2,1,0:T(8,128)(2,1)S(1)}, u32[]{:S(2)}, u32[]{:S(2)}) async-start(bf16[8,32,256]{2,1,0:T(8,128)(2,1)} %bitcast.33), calls=%async_computation.1 | async-start | bytes 262144 | tf_op jit(solution)/shard_map/all_to_all | solution.py:436
  29.7 4.1 %local.1.refs_11_ = bf16[1536,256]{1,0:T(8,128)(2,1)S(1)} custom-call(s32[12,8]{1,0:T(8,128)S(1)} %copy.24.refs_2_.refs_0_.refs_1_, bf16[1536,256]{1,0:T(8,128)(2,1)S(1)} %get-tuple-element.51.refs_1_.refs_12_, bf16[12,8,128,128]{3,2,1,0:T(8,128)(2,1)} %refs_4_.5), custom_call_target="tpu_custom_call" | custom-call | flops 1207959552 | bytes 4718976 | tf_op jit(solution)/shard_map/local/pallas_call | solution.py:98
  33.9 3.4 %all-to-all-done.1 = bf16[8,32,256]{2,1,0:T(8,128)(2,1)S(1)} async-done(((bf16[8,32,256]{2,1,0:T(8,128)(2,1)}), bf16[8,32,256]{2,1,0:T(8,128)(2,1)S(1)}, u32[]{:S(2)}, u32[]{:S(2)}) %all-to-all-start.1) | async-done | bytes 131104 | tf_op jit(solution)/shard_map/all_to_all | solution.py:436
  37.2 0.0 collective-permute-start.4
  37.3 1.3 %collective-permute-done.4.refs_4_ = bf16[256,256]{1,0:T(8,128)(2,1)S(1)} collective-permute-done((bf16[256,256]{1,0:T(8,128)(2,1)S(1)}, bf16[256,256]{1,0:T(8,128)(2,1)S(1)}, u32[]{:S(2)}, u32[]{:S(2)}) %collective-permute-start.4) | collective-permute-done | bytes 131104 | tf_op jit(solution)/shard_map/ppermute | solution.py:440
  38.6 0.9 copy-done.6
  39.5 6.2 %turn.1 = (bf16[1536,256]{1,0:T(8,128)(2,1)}, bf16[1536,256]{1,0:T(8,128)(2,1)S(1)}, bf16[256,256]{1,0:T(8,128)(2,1)}, bf16[768,256]{1,0:T(8,128)(2,1)}) custom-call(s32[1]{0:T(128)S(6)} %copy.29.refs_0_, s32[256,128]{1,0:T(8,128)S(1)} %copy-done.6, s32[1,512]{1,0:T(1,128)S(1)} %get-tuple-element.40.refs_2_, bf16[256,256]{1,0:T(8,128)(2,1)S(1)} %bitcast.28, ...), custom_call_target="tpu_custom_call" | custom-call | flops 4429185024 | bytes 6424580 | tf_op jit(solution)/shard_map/turn/pallas_call | solution.py:98
  45.7 3.4 %all-to-all-start.2 = ((bf16[8,32,256]{2,1,0:T(8,128)(2,1)}), bf16[8,32,256]{2,1,0:T(8,128)(2,1)S(1)}, u32[]{:S(2)}, u32[]{:S(2)}) async-start(bf16[8,32,256]{2,1,0:T(8,128)(2,1)} %bitcast.32), calls=%async_computation.2 | async-start | bytes 262144 | tf_op jit(solution)/shard_map/all_to_all | solution.py:436
  49.1 4.5 %turned_local.2.refs_11_ = bf16[1536,256]{1,0:T(8,128)(2,1)S(1)} custom-call(s32[1]{0:T(128)S(6)} %copy.29.refs_0_, s32[12,8]{1,0:T(8,128)S(1)} %copy.24.refs_2_.refs_0_.refs_1_, bf16[1536,256]{1,0:T(8,128)(2,1)S(1)} %get-tuple-element.57.refs_2_, bf16[1536,256]{1,0:T(8,128)(2,1)} %refs_3_.5, bf16[12,8,128,128]{3,2,1,0:T(8,128)(2,1)} %refs_4_.5), custom_call_target="tpu_custom_call" | custom-call | flops 1207959552 | bytes 5505412 | tf_op jit(solution)/shard_map/turned_local/pallas_call | solution.py:98
  53.6 3.0 %all-to-all-done.2 = bf16[8,32,256]{2,1,0:T(8,128)(2,1)S(1)} async-done(((bf16[8,32,256]{2,1,0:T(8,128)(2,1)}), bf16[8,32,256]{2,1,0:T(8,128)(2,1)S(1)}, u32[]{:S(2)}, u32[]{:S(2)}) %all-to-all-start.2) | async-done | bytes 131104 | tf_op jit(solution)/shard_map/all_to_all | solution.py:436
  56.6 1.3 %collective-permute-done.5.refs_4_ = bf16[256,256]{1,0:T(8,128)(2,1)S(1)} collective-permute-done((bf16[256,256]{1,0:T(8,128)(2,1)S(1)}, bf16[256,256]{1,0:T(8,128)(2,1)S(1)}, u32[]{:S(2)}, u32[]{:S(2)}) %collective-permute-start.5) | collective-permute-done | bytes 131104 | tf_op jit(solution)/shard_map/ppermute | solution.py:440
  58.0 3.7 %all-to-all-start.3 = ((bf16[8,96,256]{2,1,0:T(8,128)(2,1)}), bf16[8,96,256]{2,1,0:T(8,128)(2,1)S(1)}, u32[]{:S(2)}, u32[]{:S(2)}) async-start(bf16[8,96,256]{2,1,0:T(8,128)(2,1)} %bitcast.6), calls=%async_computation.3 | async-start | bytes 786432 | tf_op jit(solution)/shard_map/all_to_all | solution.py:436
  61.6 0.0 copy-start.7
  61.6 0.9 copy-done.7
  62.5 6.1 %backward.1 = (bf16[1536,256]{1,0:T(8,128)(2,1)}, bf16[1536,256]{1,0:T(8,128)(2,1)S(1)}, bf16[8,128,256]{2,1,0:T(8,128)(2,1)}) custom-call(s32[1]{0:T(128)S(6)} %copy.29.refs_0_, s32[256,128]{1,0:T(8,128)S(1)} %copy-done.7, s32[1,512]{1,0:T(1,128)S(1)} %get-tuple-element.56.refs_2_.refs_1_, bf16[256,256]{1,0:T(8,128)(2,1)S(1)} %bitcast.26, ...), custom_call_target="tpu_custom_call" | custom-call | flops 4429185024 | bytes 5638148 | tf_op jit(solution)/shard_map/backward/pallas_call | solution.py:98
  68.7 4.9 %all-to-all-done.3 = bf16[8,96,256]{2,1,0:T(8,128)(2,1)S(1)} async-done(((bf16[8,96,256]{2,1,0:T(8,128)(2,1)}), bf16[8,96,256]{2,1,0:T(8,128)(2,1)S(1)}, u32[]{:S(2)}, u32[]{:S(2)}) %all-to-all-start.3) | async-done | bytes 393248 | tf_op jit(solution)/shard_map/all_to_all | solution.py:436
  73.6 0.7 copy-done.8
  74.4 3.6 %all-to-all-start.4 = ((bf16[8,128,256]{2,1,0:T(8,128)(2,1)}), bf16[8,128,256]{2,1,0:T(8,128)(2,1)S(1)}, u32[]{:S(2)}, u32[]{:S(2)}) async-start(bf16[8,128,256]{2,1,0:T(8,128)(2,1)} %get-tuple-element.69), calls=%async_computation.4 | async-start | bytes 1048576 | tf_op jit(solution)/shard_map/all_to_all | solution.py:436
  78.0 4.5 %turned_local.3.refs_4_ = bf16[1536,256]{1,0:T(8,128)(2,1)S(1)} custom-call(s32[1]{0:T(128)S(6)} %copy.29.refs_0_, s32[12,8]{1,0:T(8,128)S(1)} %copy.24.refs_2_.refs_0_.refs_1_, bf16[1536,256]{1,0:T(8,128)(2,1)S(1)} %get-tuple-element.65.refs_2_, bf16[1536,256]{1,0:T(8,128)(2,1)} %get-tuple-element.66.refs_3_, bf16[12,8,128,128]{3,2,1,0:T(8,128)(2,1)} %refs_4_.5), custom_call_target="tpu_custom_call" | custom-call | flops 1207959552 | bytes 5505412 | tf_op jit(solution)/shard_map/turned_local/pallas_call | solution.py:98
  82.4 0.1 reduce_sum.25
  82.5 10.1 %all-to-all-done.4 = bf16[8,128,256]{2,1,0:T(8,128)(2,1)S(1)} async-done(((bf16[8,128,256]{2,1,0:T(8,128)(2,1)}), bf16[8,128,256]{2,1,0:T(8,128)(2,1)S(1)}, u32[]{:S(2)}, u32[]{:S(2)}) %all-to-all-start.4) | async-done | bytes 524320 | tf_op jit(solution)/shard_map/all_to_all | solution.py:436
  92.7 0.1 slice_reduce_fusion
  92.7 0.9 broadcast_in_dim.2
  93.7 3.6 %all-to-all-start.5 = ((bf16[8,192,256]{2,1,0:T(8,128)(2,1)}), bf16[8,192,256]{2,1,0:T(8,128)(2,1)S(1)}, u32[]{:S(2)}, u32[]{:S(2)}) async-start(bf16[8,192,256]{2,1,0:T(8,128)(2,1)} %broadcast_in_dim.2), calls=%async_computation.5 | async-start | bytes 1572864 | tf_op jit(solution)/shard_map/all_to_all | solution.py:436
  97.3 0.1 collective-permute-start.6
  97.4 1.3 %collective-permute-done.6.refs_3_ = bf16[256,256]{1,0:T(8,128)(2,1)S(1)} collective-permute-done((bf16[256,256]{1,0:T(8,128)(2,1)S(1)}, bf16[256,256]{1,0:T(8,128)(2,1)S(1)}, u32[]{:S(2)}, u32[]{:S(2)}) %collective-permute-start.6) | collective-permute-done | bytes 131104 | tf_op jit(solution)/shard_map/ppermute | solution.py:440
  98.7 1.8 %last.1 = f32[1536,256]{1,0:T(8,128)} custom-call(s32[1]{0:T(128)S(6)} %copy.29.refs_0_, s32[1,512]{1,0:T(1,128)S(1)} %get-tuple-element.56.refs_2_.refs_1_, bf16[256,256]{1,0:T(8,128)(2,1)S(1)} %bitcast.22, bf16[256,256]{1,0:T(8,128)(2,1)S(1)} %collective-permute-done.6.refs_3_, bf16[1536,256]{1,0:T(8,128)(2,1)S(1)} %turned_local.3.refs_4_), custom_call_target="tpu_custom_call" | custom-call | flops 402653184 | bytes 2623492 | tf_op jit(solution)/shard_map/last/pallas_call | solution.py:98
  100.5 17.2 %all-to-all-done.5 = bf16[8,192,256]{2,1,0:T(8,128)(2,1)S(1)} async-done(((bf16[8,192,256]{2,1,0:T(8,128)(2,1)}), bf16[8,192,256]{2,1,0:T(8,128)(2,1)S(1)}, u32[]{:S(2)}, u32[]{:S(2)}) %all-to-all-start.5) | async-done | bytes 786464 | tf_op jit(solution)/shard_map/all_to_all | solution.py:436
  117.7 0.2 convert_bitcast_fusion
  117.9 0.1 copy.28
  118.0 1.2 slice_bitcast_fusion
  (22 shorter events, 0.1 us)
Async XLA Ops:
  0.6 11.1 %copy-start.2 = (s32[1,8]{1,0:T(1,128)S(1)}, s32[1,8]{1,0:T(1,128)}, u32[]{:S(2)}) copy-start(s32[1,8]{1,0:T(1,128)} %refs_1_.5) | copy-start | bytes 100
  0.6 10.9 %copy-start.11 = (bf16[2,256,256]{2,1,0:T(8,128)(2,1)S(1)}, bf16[2,256,256]{2,1,0:T(8,128)(2,1)}, u32[]{:S(2)}) copy-start(bf16[2,256,256]{2,1,0:T(8,128)(2,1)} %refs_7_.2) | copy-start | bytes 786436
  0.7 10.4 %copy-start.1 = (bf16[2,256,256]{2,1,0:T(8,128)(2,1)S(1)}, bf16[2,256,256]{2,1,0:T(8,128)(2,1)}, u32[]{:S(2)}) copy-start(bf16[2,256,256]{2,1,0:T(8,128)(2,1)} %refs_6_.4) | copy-start | bytes 786436
  0.7 10.3 %copy-start = (bf16[2,256,256]{2,1,0:T(8,128)(2,1)S(1)}, bf16[2,256,256]{2,1,0:T(8,128)(2,1)}, u32[]{:S(2)}) copy-start(bf16[2,256,256]{2,1,0:T(8,128)(2,1)} %refs_5_.4) | copy-start | bytes 786436
  0.7 11.0 %copy-start.10 = (s32[12,8]{0,1:T(8,128)S(1)}, s32[12,8]{0,1:T(8,128)}, u32[]{:S(2)}) copy-start(s32[12,8]{0,1:T(8,128)} %param.13) | copy-start | bytes 1156
  3.6 14.7 %all-to-all-start = ((bf16[8,32,256]{2,1,0:T(8,128)(2,1)}), bf16[8,32,256]{2,1,0:T(8,128)(2,1)S(1)}, u32[]{:S(2)}, u32[]{:S(2)}) async-start(bf16[8,32,256]{2,1,0:T(8,128)(2,1)} %bitcast.31), calls=%async_computation | async-start | bytes 262144 | tf_op jit(solution)/shard_map/all_to_all | solution.py:436
  11.0 7.3 %collective-permute-start.1 = (bf16[2,256,256]{2,1,0:T(8,128)(2,1)S(1)}, bf16[2,256,256]{2,1,0:T(8,128)(2,1)S(1)}, u32[]{:S(2)}, u32[]{:S(2)}) collective-permute-start(bf16[2,256,256]{2,1,0:T(8,128)(2,1)S(1)} %copy-done), channel_id=1, source_target_pairs={{0,1},{1,0},{2,3},{3,2},{4,5},{5,4},{6,7},{7,6},{8,9},{9,8},{10,11... | collective-permute-start | bytes 786440 | tf_op jit(solution)/shard_map/ppermute | solution.py:482
  11.0 7.3 %collective-permute-start.2 = (bf16[2,256,256]{2,1,0:T(8,128)(2,1)S(1)}, bf16[2,256,256]{2,1,0:T(8,128)(2,1)S(1)}, u32[]{:S(2)}, u32[]{:S(2)}) collective-permute-start(bf16[2,256,256]{2,1,0:T(8,128)(2,1)S(1)} %copy-done.1), channel_id=1, source_target_pairs={{0,1},{1,0},{2,3},{3,2},{4,5},{5,4},{6,7},{7,6},{8,9},{9,8},{10,11... | collective-permute-start | bytes 786440 | tf_op jit(solution)/shard_map/ppermute | solution.py:482
  11.5 6.8 %collective-permute-start.3 = (bf16[2,256,256]{2,1,0:T(8,128)(2,1)S(1)}, bf16[2,256,256]{2,1,0:T(8,128)(2,1)S(1)}, u32[]{:S(2)}, u32[]{:S(2)}) collective-permute-start(bf16[2,256,256]{2,1,0:T(8,128)(2,1)S(1)} %copy-done.11), channel_id=1, source_target_pairs={{0,1},{1,0},{2,3},{3,2},{4,5},{5,4},{6,7},{7,6},{8,9},{9,8},{10,11... | collective-permute-start | bytes 786440 | tf_op jit(solution)/shard_map/ppermute | solution.py:482
  16.8 0.9 copy-start.3
  17.6 6.8 %copy-start.5 = (s32[256,128]{1,0:T(8,128)}, s32[256,128]{1,0:T(8,128)S(1)}, u32[]{:S(2)}) copy-start(s32[256,128]{1,0:T(8,128)S(1)} %get-tuple-element.39.refs_1_) | copy-start | bytes 393220
  18.3 1.3 %collective-permute-start = (bf16[256,256]{1,0:T(8,128)(2,1)S(1)}, bf16[256,256]{1,0:T(8,128)(2,1)S(1)}, u32[]{:S(2)}, u32[]{:S(2)}) collective-permute-start(bf16[256,256]{1,0:T(8,128)(2,1)S(1)} %bitcast.23), channel_id=1, source_target_pairs={{0,1},{1,0},{2,3},{3,2},{4,5},{5,4},{6,7},{7,6},{8,9},{9,8},{10,11... | collective-permute-start | bytes 393224 | tf_op jit(solution)/shard_map/ppermute | solution.py:440
  18.3 1.3 %copy-start.12 = (bf16[2,256,256]{2,1,0:T(8,128)(2,1)}, bf16[2,256,256]{2,1,0:T(8,128)(2,1)S(1)}, u32[]{:S(2)}) copy-start(bf16[2,256,256]{2,1,0:T(8,128)(2,1)S(1)} %collective-permute-done.3.refs_10_) | copy-start | bytes 786436
  19.6 1.1 copy-start.4
  24.4 12.9 %all-to-all-start.1 = ((bf16[8,32,256]{2,1,0:T(8,128)(2,1)}), bf16[8,32,256]{2,1,0:T(8,128)(2,1)S(1)}, u32[]{:S(2)}, u32[]{:S(2)}) async-start(bf16[8,32,256]{2,1,0:T(8,128)(2,1)} %bitcast.33), calls=%async_computation.1 | async-start | bytes 262144 | tf_op jit(solution)/shard_map/all_to_all | solution.py:436
  37.2 1.3 %collective-permute-start.4 = (bf16[256,256]{1,0:T(8,128)(2,1)S(1)}, bf16[256,256]{1,0:T(8,128)(2,1)S(1)}, u32[]{:S(2)}, u32[]{:S(2)}) collective-permute-start(bf16[256,256]{1,0:T(8,128)(2,1)S(1)} %bitcast.27), channel_id=1, source_target_pairs={{0,1},{1,0},{2,3},{3,2},{4,5},{5,4},{6,7},{7,6},{8,9},{9,8},{10,11... | collective-permute-start | bytes 393224 | tf_op jit(solution)/shard_map/ppermute | solution.py:440
  38.6 0.9 copy-start.6
  45.7 10.9 %all-to-all-start.2 = ((bf16[8,32,256]{2,1,0:T(8,128)(2,1)}), bf16[8,32,256]{2,1,0:T(8,128)(2,1)S(1)}, u32[]{:S(2)}, u32[]{:S(2)}) async-start(bf16[8,32,256]{2,1,0:T(8,128)(2,1)} %bitcast.32), calls=%async_computation.2 | async-start | bytes 262144 | tf_op jit(solution)/shard_map/all_to_all | solution.py:436
  56.6 1.3 %collective-permute-start.5 = (bf16[256,256]{1,0:T(8,128)(2,1)S(1)}, bf16[256,256]{1,0:T(8,128)(2,1)S(1)}, u32[]{:S(2)}, u32[]{:S(2)}) collective-permute-start(bf16[256,256]{1,0:T(8,128)(2,1)S(1)} %bitcast.25), channel_id=1, source_target_pairs={{0,1},{1,0},{2,3},{3,2},{4,5},{5,4},{6,7},{7,6},{8,9},{9,8},{10,11... | collective-permute-start | bytes 393224 | tf_op jit(solution)/shard_map/ppermute | solution.py:440
  58.0 15.7 %all-to-all-start.3 = ((bf16[8,96,256]{2,1,0:T(8,128)(2,1)}), bf16[8,96,256]{2,1,0:T(8,128)(2,1)S(1)}, u32[]{:S(2)}, u32[]{:S(2)}) async-start(bf16[8,96,256]{2,1,0:T(8,128)(2,1)} %bitcast.6), calls=%async_computation.3 | async-start | bytes 786432 | tf_op jit(solution)/shard_map/all_to_all | solution.py:436
  61.6 0.9 copy-start.7
  73.6 0.7 copy-start.8
  74.4 18.3 %all-to-all-start.4 = ((bf16[8,128,256]{2,1,0:T(8,128)(2,1)}), bf16[8,128,256]{2,1,0:T(8,128)(2,1)S(1)}, u32[]{:S(2)}, u32[]{:S(2)}) async-start(bf16[8,128,256]{2,1,0:T(8,128)(2,1)} %get-tuple-element.69), calls=%async_computation.4 | async-start | bytes 1048576 | tf_op jit(solution)/shard_map/all_to_all | solution.py:436
  78.0 4.5 %copy-start.9 = (bf16[8,96,256]{2,1,0:T(8,128)(2,1)S(1)}, bf16[8,96,256]{2,1,0:T(8,128)(2,1)}, u32[]{:S(2)}) copy-start(bf16[8,96,256]{2,1,0:T(8,128)(2,1)} %copy-done.8) | copy-start | bytes 1179652
  93.7 24.0 %all-to-all-start.5 = ((bf16[8,192,256]{2,1,0:T(8,128)(2,1)}), bf16[8,192,256]{2,1,0:T(8,128)(2,1)S(1)}, u32[]{:S(2)}, u32[]{:S(2)}) async-start(bf16[8,192,256]{2,1,0:T(8,128)(2,1)} %broadcast_in_dim.2), calls=%async_computation.5 | async-start | bytes 1572864 | tf_op jit(solution)/shard_map/all_to_all | solution.py:436
  97.3 1.4 %collective-permute-start.6 = (bf16[256,256]{1,0:T(8,128)(2,1)S(1)}, bf16[256,256]{1,0:T(8,128)(2,1)S(1)}, u32[]{:S(2)}, u32[]{:S(2)}) collective-permute-start(bf16[256,256]{1,0:T(8,128)(2,1)S(1)} %bitcast.21), channel_id=1, source_target_pairs={{0,1},{1,0},{2,3},{3,2},{4,5},{5,4},{6,7},{7,6},{8,9},{9,8},{10,11... | collective-permute-start | bytes 393224 | tf_op jit(solution)/shard_map/ppermute | solution.py:440

commit v2 on v1

--- a/solution.py
+++ b/solution.py
@@ -247,7 +247,7 @@
 
 def first_local_kernel(
     parts, traffic, count_ref, used_ref, cols_ref, send_ref, recv_ref, feats_ref, tile_ref,
-    state_ref, sum_ref, send_row_ref, recv_row_ref, recv_col_ref, near_ref, dense_ref, sems,
+    sum_ref, send_row_ref, recv_row_ref, recv_col_ref, near_ref, dense_ref, sems, state_ref,
 ):
     dense = Dense(cols_ref, tile_ref, near_ref, dense_ref, sems)
     dense.zero()
@@ -257,9 +257,9 @@
     fill_row(parts, recv_row_ref, recv_ref, always)
     fill_columns(recv_col_ref, recv_ref, always)
     state_ref[...] = jnp.where(live(count_ref, 0, rows, width), feats_ref[...], jnp.zeros((), BF16))
-    for k in (0, 2, 3, 4):
+    for k in (1, 2, 3):
         traffic.put(k)
-    local_sums(traffic, dense, state_ref, sum_ref, 1)
+    local_sums(traffic, dense, state_ref, sum_ref, 0)
 
 
 def local_kernel(traffic, cols_ref, state_ref, tile_ref, sum_ref, near_ref, dense_ref, sems):
@@ -297,23 +297,30 @@
     agg = None
     for part, ((gate, up, sig, silu), (gate_ref, up_ref, down_ref)) in enumerate(zip(terms, weights)):
         hidden_grad = mm_t(down_in, down_ref[...])
-        slope = sig * (1.0 + gate * (1.0 - sig))
+        slope = sig + silu * (1.0 - sig)
         gate_grad = (hidden_grad * up * slope).astype(BF16)
         up_grad = (hidden_grad * silu).astype(BF16)
         more = mm_t(gate_grad, gate_ref[...]) + mm_t(up_grad, up_ref[...])
         agg = more if agg is None else agg + more
         if part == 0:
-            for ref, value in zip(kept, ((silu * up).astype(BF16), gate_grad, up_grad, down_in)):
-                ref[at, :] = value
+            hidden_ref, both_ref, *down = kept
+            half = gate_grad.shape[1]
+            hidden_ref[at, :] = (silu * up).astype(BF16)
+            both_ref[at, :half] = gate_grad
+            both_ref[at, half:] = up_grad
+            for ref in down:
+                ref[at, :] = down_in
     agg_ref[at, :] = agg.astype(BF16)
 
 
 def weight_grads(acts_ref, kept, dw_ref):
-    hidden_ref, gate_ref, up_ref, down_ref = kept
-    pairs = ((acts_ref, gate_ref), (acts_ref, up_ref), (hidden_ref, down_ref))
-    for k, (left_ref, right_ref) in enumerate(pairs):
-        size = left_ref.shape[1]
-        dw_ref[k * size : (k + 1) * size, :] = mm_rows(left_ref[...], right_ref[...]).astype(BF16)
+    hidden_ref, both_ref, down_ref = kept
+    size = acts_ref.shape[1]
+    half = both_ref.shape[1] // 2
+    both = mm_rows(acts_ref[...], both_ref[...]).astype(BF16)
+    dw_ref[:size, :] = both[:, :half]
+    dw_ref[size : 2 * size, :] = both[:, half:]
+    dw_ref[2 * size :, :] = mm_rows(hidden_ref[...], down_ref[...]).astype(BF16)
 
 
 def mix(terms, weights):
@@ -335,10 +342,11 @@
         acts_ref[at, :] = acts
         terms = gates(acts, weights)
         if at.start == 0:
-            traffic.need(*(down_ref for _, _, down_ref in weights))
+            traffic.need(*(down_ref for _, _, down_ref in weights), state_ref)
         after = state_ref[at, :].astype(F32) + mix(terms, weights)
         next_ref[at, :] = jnp.where(live(count_ref, at.start, size, width), after, 0.0).astype(BF16)
     traffic.put(0)
+    traffic.need(col_ref)
     gather_rows(col_ref, next_ref, out_ref)
     traffic.put(2)
 
@@ -354,13 +362,14 @@
         acts_ref[at, :] = acts
         terms = gates(acts, weights)
         if at.start == 0:
-            traffic.need(*(down_ref for _, _, down_ref in weights), grad_ref)
+            traffic.need(*(down_ref for _, _, down_ref in weights), state_ref, grad_ref)
         after = state_ref[at, :].astype(F32) + mix(terms, weights)
         alive = live(count_ref, at.start, size, width)
         final_ref[at, :] = jnp.where(alive, after, 0.0).astype(BF16)
         down_in = jnp.where(alive, grad_ref[at, :], jnp.zeros((), BF16))
         layer_grads(at, acts, terms, down_in, weights, agg_ref, kept)
     traffic.put(0)
+    traffic.need(col_ref)
     gather_rows(col_ref, agg_ref, out_ref)
     traffic.put(2)
     weight_grads(acts_ref, kept, dw_ref)
@@ -395,6 +404,7 @@
     for at in pieces_of(rows):
         acts = acts_ref[at, :]
         layer_grads(at, acts, gates(acts, weights), upstream_ref[at, :], weights, agg_ref, kept)
+    traffic.need(col_ref)
     gather_rows(col_ref, agg_ref, out_ref)
     weight_grads(acts_ref, (*kept, upstream_ref), dw_ref)
     put_pieces(traffic, 2, (out_ref, dw_ref), sem)
@@ -463,7 +473,7 @@
     row_shape, col_shape = shape((1, slots), jnp.int32), shape((slots // parts, LANES), jnp.int32)
     dw_shape = shape((3 * width, hidden_width), BF16)
     half = pltpu.VMEM((rows, hidden_width), BF16)
-    kept_shapes = [half, half, half, pltpu.VMEM((rows, width), BF16)]
+    kept_shapes = [half, pltpu.VMEM((rows, 2 * hidden_width), BF16), pltpu.VMEM((rows, width), BF16)]
     local_flops = 2 * rows * rows * width
     slot_flops = 2 * rows * slots * width
     layer_flops = 6 * rows * width * hidden_width * parts
@@ -471,7 +481,7 @@
 
     outgoing, send_col = call(
         send_kernel,
-        [far(slot_shape), near(col_shape)],
+        [far(slot_shape), far(col_shape)],
         [count, (send_count, "scalars"), far(send_list), far(feats)],
         slot_flops,
         "send",
@@ -484,14 +494,13 @@
     def weights(layer):
         return [spec for gate, up, down in held for spec in (near(gate), near(up), (down, Layer(layer)))]
 
-    state, total, send_row, recv_row, recv_col = call(
+    total, send_row, recv_row, recv_col = call(
         functools.partial(first_local_kernel, parts),
         [
-            near(state_shape),
             near(sum_shape),
             near(row_shape),
             near(row_shape),
-            near(col_shape),
+            far(col_shape),
         ],
         [
             count,
@@ -504,30 +513,32 @@
         ],
         local_flops,
         "first_local",
-        dense_scratch,
+        [*dense_scratch, pltpu.VMEM((rows, width), BF16)],
     )
     total, arriving = share_after(total, arriving)
+    state = far(feats)
     kept = []
     for layer in range(layers - 1):
-        acts, state, outgoing = call(
+        acts, after, outgoing = call(
             functools.partial(forward_kernel, parts, layer),
             [far(state_shape), near(state_shape), far(slot_shape)],
-            [count, near(send_col), near(recv_row), *map(near, arriving), *weights(layer), near(total), near(state)],
+            [count, far(send_col), near(recv_row), *map(near, arriving), *weights(layer), near(total), state],
             layer_flops + 2 * slot_flops,
             "forward",
         )
         kept.append(acts)
+        state = near(after)
         arriving = exchange(outgoing)
         (total,) = call(
-            local_kernel, [near(sum_shape)], [cols, near(state), tiles], local_flops, "local", dense_scratch
+            local_kernel, [near(sum_shape)], [cols, state, tiles], local_flops, "local", dense_scratch
         )
         total, arriving = share_after(total, arriving)
     final, agg, outgoing, dw = call(
         functools.partial(turn_kernel, parts, layers - 1),
         [far(state_shape), near(state_shape), far(slot_shape), far(dw_shape)],
         [
-            count, near(recv_col), near(recv_row), *map(near, arriving), *weights(layers - 1), near(total),
-            near(state), far(out_grad),
+            count, far(recv_col), near(recv_row), *map(near, arriving), *weights(layers - 1), near(total),
+            state, far(out_grad),
         ],
         3 * layer_flops + 2 * slot_flops,
         "turn",
@@ -561,7 +572,7 @@
             functools.partial(backward_kernel, parts, layer),
             [far(sum_shape), near(state_shape), (both_shape, "later")],
             [
-                count, near(recv_col), near(send_row), *map(near, arriving), *weights(layer), near(total),
+                count, far(recv_col), near(send_row), *map(near, arriving), *weights(layer), near(total),
                 far(kept[layer]),
             ],
             3 * layer_flops + 2 * slot_flops,
@@ -570,12 +581,11 @@
                 pltpu.VMEM(slot_shape.shape, BF16),
                 pltpu.VMEM(dw_shape.shape, BF16),
                 pltpu.SemaphoreType.DMA((peers,)),
-                *kept_shapes[:3],
+                *kept_shapes[:2],
             ],
         )
         if layer == layers - 2:
-            both, pieces = lax.optimization_barrier((both, pieces))
-            reduced[layer + 1] = added(pieces)
+            both, reduced[layer + 1] = lax.optimization_barrier((both, added(pieces)))
         both = swap(both)
         total, both = lax.optimization_barrier((turned_local(agg, upstream), both))
         arriving = share(both[:, :own_slots])

time: 120 us -> 117 us (0.975)
  local copies, waits for them, and re-layouts: 6.94 us -> 2.36 us
  waiting for transfers between devices: 44.7 us -> 46.2 us
    unnamed x27 -> x13, local copies, waits for them, and re-layouts: 4.68 us -> 0.11 us
    all_to_all x6, waiting for transfers between devices: 39.3 us -> 40.8 us  [swap(): lax.all_to_all(blocks, 'dom', split_axis=0, concat_axis=0, tiled=True)]
  transfers between devices with their start and end apart: 13 -> 13, of which waited for: 10 -> 10; matrix products, arithmetic and copies ran while one was open for 0% -> 0% of each run, Pallas kernels for 22% -> 23%
where the time goes in v2:
time: 117 us; the launch traced here: 116 us
  waiting for transfers between devices  46.2 us (39%)
  Pallas kernels  39 us (33%)
  starting transfers between devices  26.9 us (23%)
  local copies, waits for them, and re-layouts  2.36 us (2%)
  between operations  1.57 us (1%)
    all_to_all x6, waiting for transfers between devices, swap(): lax.all_to_all(blocks, 'dom', split_axis=0, concat_axis=0, tiled=True)  40.8 us
    pallas_call x9, Pallas kernels, call(): pl.pallas_call(body, out_shape=[space(cut)(x.shape, x.dtype) for x, cut i...  39 us
    all_to_all x6, starting transfers between devices, swap(): lax.all_to_all(blocks, 'dom', split_axis=0, concat_axis=0, tiled=True)  26.2 us
    ppermute x4, waiting for transfers between devices, share(): return [rows] + [lax.ppermute(rows, 'mp', turn) for turn in turns]  5.34 us
  transfers between devices with their start and end apart: 13, of which 10 were waited for; matrix products, arithmetic and copies ran while one was open for 0% of the time, Pallas kernels for 23%

profile of v2, /device:TPU:0, one launch (start us, length us, event | category | flops | bytes accessed | tf_op | source)
XLA Modules:
  0.0 116.3 jit_solution(944515568112015436)
XLA Ops:
  0.6 0.0 copy-start.2
  0.6 0.0 copy-start.4
  1.4 2.2 %send.1 = (bf16[256,256]{1,0:T(8,128)(2,1)}, s32[256,128]{1,0:T(8,128)}) custom-call(s32[1]{0:T(128)S(6)} %copy.29.refs_0_, s32[1,8]{1,0:T(1,128)} %refs_1_.5, s32[1,8,64]{2,1,0:T(8,128)} %refs_2_.3, bf16[1536,256]{1,0:T(8,128)(2,1)} %refs_12_.1), custom_call_target="tpu_custom_call" | custom-call | flops 402653184 | bytes 1050660 | tf_op jit(solution)/shard_map/send/pallas_call | solution.py:98
  3.6 7.3 %all-to-all-start = ((bf16[8,32,256]{2,1,0:T(8,128)(2,1)}), bf16[8,32,256]{2,1,0:T(8,128)(2,1)S(1)}, u32[]{:S(2)}, u32[]{:S(2)}) async-start(bf16[8,32,256]{2,1,0:T(8,128)(2,1)} %bitcast.31), calls=%async_computation | async-start | bytes 262144 | tf_op jit(solution)/shard_map/all_to_all | solution.py:446
  11.0 0.1 collective-permute-start.1
  11.0 0.0 copy-done.1
  11.0 0.5 collective-permute-start.2
  11.5 0.0 copy-done.4
  11.5 0.1 collective-permute-start.3
  11.6 0.1 copy.24.refs_2_.refs_0_.refs_1_
  11.7 0.0 copy-done.2
  11.7 5.1 %first_local.1 = (bf16[1536,256]{1,0:T(8,128)(2,1)S(1)}, s32[1,512]{1,0:T(1,128)S(1)}, s32[1,512]{1,0:T(1,128)S(1)}, s32[256,128]{1,0:T(8,128)}) custom-call(s32[1]{0:T(128)S(6)} %copy.29.refs_0_, s32[1,8]{1,0:T(1,128)S(1)} %copy-done.2, s32[12,8]{1,0:T(8,128)S(1)} %copy.24.refs_2_.refs_0_.refs_1_, s32[1,8,64]{2,1,0:T(8,128)} %refs_2_.3, ...), custom_call_target="tpu_custom_call" | custom-call | flops 1207959552 | bytes 4858276 | tf_op jit(solution)/shard_map/first_local/pallas_call | solution.py:98
  16.8 1.5 %all-to-all-done = bf16[8,32,256]{2,1,0:T(8,128)(2,1)S(1)} async-done(((bf16[8,32,256]{2,1,0:T(8,128)(2,1)}), bf16[8,32,256]{2,1,0:T(8,128)(2,1)S(1)}, u32[]{:S(2)}, u32[]{:S(2)}) %all-to-all-start) | async-done | bytes 131104 | tf_op jit(solution)/shard_map/all_to_all | solution.py:446
  18.3 0.0 collective-permute-start
  18.3 0.0 collective-permute-done.1.refs_8_
  18.3 0.0 collective-permute-done.2.refs_9_
  18.3 0.0 collective-permute-done.3.refs_10_
  18.3 0.0 copy-start.5
  18.3 1.3 %collective-permute-done.refs_4_ = bf16[256,256]{1,0:T(8,128)(2,1)S(1)} collective-permute-done((bf16[256,256]{1,0:T(8,128)(2,1)S(1)}, bf16[256,256]{1,0:T(8,128)(2,1)S(1)}, u32[]{:S(2)}, u32[]{:S(2)}) %collective-permute-start) | collective-permute-done | bytes 131104 | tf_op jit(solution)/shard_map/ppermute | solution.py:450
  19.6 4.3 %forward.1 = (bf16[1536,256]{1,0:T(8,128)(2,1)}, bf16[1536,256]{1,0:T(8,128)(2,1)S(1)}, bf16[256,256]{1,0:T(8,128)(2,1)}) custom-call(s32[1]{0:T(128)S(6)} %copy.29.refs_0_, s32[256,128]{1,0:T(8,128)} %get-tuple-element.40.refs_1_, s32[1,512]{1,0:T(1,128)S(1)} %get-tuple-element.39.refs_2_, bf16[256,256]{1,0:T(8,128)(2,1)S(1)} %bitcast.24, ...), custom_call_target="tpu_custom_call" | custom-call | flops 2013265920 | bytes 5244932 | tf_op jit(solution)/shard_map/forward/pallas_call | solution.py:98
  23.9 4.6 %all-to-all-start.1 = ((bf16[8,32,256]{2,1,0:T(8,128)(2,1)}), bf16[8,32,256]{2,1,0:T(8,128)(2,1)S(1)}, u32[]{:S(2)}, u32[]{:S(2)}) async-start(bf16[8,32,256]{2,1,0:T(8,128)(2,1)} %bitcast.33), calls=%async_computation.1 | async-start | bytes 262144 | tf_op jit(solution)/shard_map/all_to_all | solution.py:446
  28.5 4.1 %local.1.refs_11_ = bf16[1536,256]{1,0:T(8,128)(2,1)S(1)} custom-call(s32[12,8]{1,0:T(8,128)S(1)} %copy.24.refs_2_.refs_0_.refs_1_, bf16[1536,256]{1,0:T(8,128)(2,1)S(1)} %get-tuple-element.49.refs_1_.refs_12_, bf16[12,8,128,128]{3,2,1,0:T(8,128)(2,1)} %refs_4_.5), custom_call_target="tpu_custom_call" | custom-call | flops 1207959552 | bytes 4718976 | tf_op jit(solution)/shard_map/local/pallas_call | solution.py:98
  32.6 3.4 %all-to-all-done.1 = bf16[8,32,256]{2,1,0:T(8,128)(2,1)S(1)} async-done(((bf16[8,32,256]{2,1,0:T(8,128)(2,1)}), bf16[8,32,256]{2,1,0:T(8,128)(2,1)S(1)}, u32[]{:S(2)}, u32[]{:S(2)}) %all-to-all-start.1) | async-done | bytes 131104 | tf_op jit(solution)/shard_map/all_to_all | solution.py:446
  36.0 0.0 collective-permute-start.4
  36.0 1.3 %collective-permute-done.4.refs_4_ = bf16[256,256]{1,0:T(8,128)(2,1)S(1)} collective-permute-done((bf16[256,256]{1,0:T(8,128)(2,1)S(1)}, bf16[256,256]{1,0:T(8,128)(2,1)S(1)}, u32[]{:S(2)}, u32[]{:S(2)}) %collective-permute-start.4) | collective-permute-done | bytes 131104 | tf_op jit(solution)/shard_map/ppermute | solution.py:450
  37.3 6.2 %turn.1 = (bf16[1536,256]{1,0:T(8,128)(2,1)}, bf16[1536,256]{1,0:T(8,128)(2,1)S(1)}, bf16[256,256]{1,0:T(8,128)(2,1)}, bf16[768,256]{1,0:T(8,128)(2,1)}) custom-call(s32[1]{0:T(128)S(6)} %copy.29.refs_0_, s32[256,128]{1,0:T(8,128)} %get-tuple-element.38.refs_1_, s32[1,512]{1,0:T(1,128)S(1)} %get-tuple-element.39.refs_2_, bf16[256,256]{1,0:T(8,128)(2,1)S(1)} %bitcast.28, ...), custom_call_target="tpu_custom_call" | custom-call | flops 4429185024 | bytes 6424580 | tf_op jit(solution)/shard_map/turn/pallas_call | solution.py:98
  43.5 3.4 %all-to-all-start.2 = ((bf16[8,32,256]{2,1,0:T(8,128)(2,1)}), bf16[8,32,256]{2,1,0:T(8,128)(2,1)S(1)}, u32[]{:S(2)}, u32[]{:S(2)}) async-start(bf16[8,32,256]{2,1,0:T(8,128)(2,1)} %bitcast.32), calls=%async_computation.2 | async-start | bytes 262144 | tf_op jit(solution)/shard_map/all_to_all | solution.py:446
  46.9 4.5 %turned_local.2.refs_11_ = bf16[1536,256]{1,0:T(8,128)(2,1)S(1)} custom-call(s32[1]{0:T(128)S(6)} %copy.29.refs_0_, s32[12,8]{1,0:T(8,128)S(1)} %copy.24.refs_2_.refs_0_.refs_1_, bf16[1536,256]{1,0:T(8,128)(2,1)S(1)} %get-tuple-element.55.refs_2_, bf16[1536,256]{1,0:T(8,128)(2,1)} %refs_3_.5, bf16[12,8,128,128]{3,2,1,0:T(8,128)(2,1)} %refs_4_.5), custom_call_target="tpu_custom_call" | custom-call | flops 1207959552 | bytes 5505412 | tf_op jit(solution)/shard_map/turned_local/pallas_call | solution.py:98
  51.4 3.0 %all-to-all-done.2 = bf16[8,32,256]{2,1,0:T(8,128)(2,1)S(1)} async-done(((bf16[8,32,256]{2,1,0:T(8,128)(2,1)}), bf16[8,32,256]{2,1,0:T(8,128)(2,1)S(1)}, u32[]{:S(2)}, u32[]{:S(2)}) %all-to-all-start.2) | async-done | bytes 131104 | tf_op jit(solution)/shard_map/all_to_all | solution.py:446
  54.4 0.0 collective-permute-start.5
  54.4 1.3 %collective-permute-done.5.refs_4_ = bf16[256,256]{1,0:T(8,128)(2,1)S(1)} collective-permute-done((bf16[256,256]{1,0:T(8,128)(2,1)S(1)}, bf16[256,256]{1,0:T(8,128)(2,1)S(1)}, u32[]{:S(2)}, u32[]{:S(2)}) %collective-permute-start.5) | collective-permute-done | bytes 131104 | tf_op jit(solution)/shard_map/ppermute | solution.py:450
  55.8 3.7 %all-to-all-start.3 = ((bf16[8,96,256]{2,1,0:T(8,128)(2,1)}), bf16[8,96,256]{2,1,0:T(8,128)(2,1)S(1)}, u32[]{:S(2)}, u32[]{:S(2)}) async-start(bf16[8,96,256]{2,1,0:T(8,128)(2,1)} %bitcast.6), calls=%async_computation.3 | async-start | bytes 786432 | tf_op jit(solution)/shard_map/all_to_all | solution.py:446
  59.5 6.5 %backward.1 = (bf16[1536,256]{1,0:T(8,128)(2,1)}, bf16[1536,256]{1,0:T(8,128)(2,1)S(1)}, bf16[8,128,256]{2,1,0:T(8,128)(2,1)}) custom-call(s32[1]{0:T(128)S(6)} %copy.29.refs_0_, s32[256,128]{1,0:T(8,128)} %get-tuple-element.38.refs_1_, s32[1,512]{1,0:T(1,128)S(1)} %get-tuple-element.54.refs_2_.refs_1_, bf16[256,256]{1,0:T(8,128)(2,1)S(1)} %bitcast.26, ...), custom_call_target="tpu_custom_call" | custom-call | flops 4429185024 | bytes 5638148 | tf_op jit(solution)/shard_map/backward/pallas_call | solution.py:98
  65.9 5.5 %all-to-all-done.3 = bf16[8,96,256]{2,1,0:T(8,128)(2,1)S(1)} async-done(((bf16[8,96,256]{2,1,0:T(8,128)(2,1)}), bf16[8,96,256]{2,1,0:T(8,128)(2,1)S(1)}, u32[]{:S(2)}, u32[]{:S(2)}) %all-to-all-start.3) | async-done | bytes 393248 | tf_op jit(solution)/shard_map/all_to_all | solution.py:446
  71.4 0.1 reduce_sum.24
  71.5 3.6 %all-to-all-start.4 = ((bf16[8,128,256]{2,1,0:T(8,128)(2,1)}), bf16[8,128,256]{2,1,0:T(8,128)(2,1)S(1)}, u32[]{:S(2)}, u32[]{:S(2)}) async-start(bf16[8,128,256]{2,1,0:T(8,128)(2,1)} %get-tuple-element.67), calls=%async_computation.4 | async-start | bytes 1048576 | tf_op jit(solution)/shard_map/all_to_all | solution.py:446
  75.1 4.5 %turned_local.3.refs_4_ = bf16[1536,256]{1,0:T(8,128)(2,1)S(1)} custom-call(s32[1]{0:T(128)S(6)} %copy.29.refs_0_, s32[12,8]{1,0:T(8,128)S(1)} %copy.24.refs_2_.refs_0_.refs_1_, bf16[1536,256]{1,0:T(8,128)(2,1)S(1)} %get-tuple-element.63.refs_2_, bf16[1536,256]{1,0:T(8,128)(2,1)} %get-tuple-element.64.refs_3_, bf16[12,8,128,128]{3,2,1,0:T(8,128)(2,1)} %refs_4_.5), custom_call_target="tpu_custom_call" | custom-call | flops 1207959552 | bytes 5505412 | tf_op jit(solution)/shard_map/turned_local/pallas_call | solution.py:98
  79.6 10.2 %all-to-all-done.4 = bf16[8,128,256]{2,1,0:T(8,128)(2,1)S(1)} async-done(((bf16[8,128,256]{2,1,0:T(8,128)(2,1)}), bf16[8,128,256]{2,1,0:T(8,128)(2,1)S(1)}, u32[]{:S(2)}, u32[]{:S(2)}) %all-to-all-start.4) | async-done | bytes 524320 | tf_op jit(solution)/shard_map/all_to_all | solution.py:446
  89.8 0.1 slice_reduce_fusion
  89.9 0.9 broadcast_in_dim.2
  90.8 3.6 %all-to-all-start.5 = ((bf16[8,192,256]{2,1,0:T(8,128)(2,1)}), bf16[8,192,256]{2,1,0:T(8,128)(2,1)S(1)}, u32[]{:S(2)}, u32[]{:S(2)}) async-start(bf16[8,192,256]{2,1,0:T(8,128)(2,1)} %broadcast_in_dim.2), calls=%async_computation.5 | async-start | bytes 1572864 | tf_op jit(solution)/shard_map/all_to_all | solution.py:446
  94.5 0.1 collective-permute-start.6
  94.5 1.3 %collective-permute-done.6.refs_3_ = bf16[256,256]{1,0:T(8,128)(2,1)S(1)} collective-permute-done((bf16[256,256]{1,0:T(8,128)(2,1)S(1)}, bf16[256,256]{1,0:T(8,128)(2,1)S(1)}, u32[]{:S(2)}, u32[]{:S(2)}) %collective-permute-start.6) | collective-permute-done | bytes 131104 | tf_op jit(solution)/shard_map/ppermute | solution.py:450
  95.9 1.8 %last.1 = f32[1536,256]{1,0:T(8,128)} custom-call(s32[1]{0:T(128)S(6)} %copy.29.refs_0_, s32[1,512]{1,0:T(1,128)S(1)} %get-tuple-element.54.refs_2_.refs_1_, bf16[256,256]{1,0:T(8,128)(2,1)S(1)} %bitcast.22, bf16[256,256]{1,0:T(8,128)(2,1)S(1)} %collective-permute-done.6.refs_3_, bf16[1536,256]{1,0:T(8,128)(2,1)S(1)} %turned_local.3.refs_4_), custom_call_target="tpu_custom_call" | custom-call | flops 402653184 | bytes 2623492 | tf_op jit(solution)/shard_map/last/pallas_call | solution.py:98
  97.7 17.2 %all-to-all-done.5 = bf16[8,192,256]{2,1,0:T(8,128)(2,1)S(1)} async-done(((bf16[8,192,256]{2,1,0:T(8,128)(2,1)}), bf16[8,192,256]{2,1,0:T(8,128)(2,1)S(1)}, u32[]{:S(2)}, u32[]{:S(2)}) %all-to-all-start.5) | async-done | bytes 786464 | tf_op jit(solution)/shard_map/all_to_all | solution.py:446
  114.8 0.2 convert_bitcast_fusion
  115.0 0.1 copy.28
  115.1 1.2 %slice_bitcast_fusion = (f32[2,256,256]{2,1,0:T(8,128)}, f32[2,256,256]{2,1,0:T(8,128)}, f32[2,256,256]{2,1,0:T(8,128)}) fusion(f32[3,2,256,256]{3,2,0,1:T(8,128)S(1)} %bitcast.29), kind=kLoop, calls=%fused_computation.1 | loop fusion | bytes 3145728 | tf_op jit(solution)/shard_map/squeeze | solution.py:604
  (8 shorter events, 0.0 us)
Async XLA Ops:
  0.6 11.1 %copy-start.2 = (s32[1,8]{1,0:T(1,128)S(1)}, s32[1,8]{1,0:T(1,128)}, u32[]{:S(2)}) copy-start(s32[1,8]{1,0:T(1,128)} %refs_1_.5) | copy-start | bytes 100
  0.6 10.9 %copy-start.4 = (bf16[2,256,256]{2,1,0:T(8,128)(2,1)S(1)}, bf16[2,256,256]{2,1,0:T(8,128)(2,1)}, u32[]{:S(2)}) copy-start(bf16[2,256,256]{2,1,0:T(8,128)(2,1)} %refs_7_.2) | copy-start | bytes 786436
  0.7 10.4 %copy-start.1 = (bf16[2,256,256]{2,1,0:T(8,128)(2,1)S(1)}, bf16[2,256,256]{2,1,0:T(8,128)(2,1)}, u32[]{:S(2)}) copy-start(bf16[2,256,256]{2,1,0:T(8,128)(2,1)} %refs_6_.4) | copy-start | bytes 786436
  0.7 10.3 %copy-start = (bf16[2,256,256]{2,1,0:T(8,128)(2,1)S(1)}, bf16[2,256,256]{2,1,0:T(8,128)(2,1)}, u32[]{:S(2)}) copy-start(bf16[2,256,256]{2,1,0:T(8,128)(2,1)} %refs_5_.4) | copy-start | bytes 786436
  0.7 11.0 %copy-start.3 = (s32[12,8]{0,1:T(8,128)S(1)}, s32[12,8]{0,1:T(8,128)}, u32[]{:S(2)}) copy-start(s32[12,8]{0,1:T(8,128)} %param.13) | copy-start | bytes 1156
  3.6 14.7 %all-to-all-start = ((bf16[8,32,256]{2,1,0:T(8,128)(2,1)}), bf16[8,32,256]{2,1,0:T(8,128)(2,1)S(1)}, u32[]{:S(2)}, u32[]{:S(2)}) async-start(bf16[8,32,256]{2,1,0:T(8,128)(2,1)} %bitcast.31), calls=%async_computation | async-start | bytes 262144 | tf_op jit(solution)/shard_map/all_to_all | solution.py:446
  11.0 7.3 %collective-permute-start.1 = (bf16[2,256,256]{2,1,0:T(8,128)(2,1)S(1)}, bf16[2,256,256]{2,1,0:T(8,128)(2,1)S(1)}, u32[]{:S(2)}, u32[]{:S(2)}) collective-permute-start(bf16[2,256,256]{2,1,0:T(8,128)(2,1)S(1)} %copy-done), channel_id=1, source_target_pairs={{0,1},{1,0},{2,3},{3,2},{4,5},{5,4},{6,7},{7,6},{8,9},{9,8},{10,11... | collective-permute-start | bytes 786440 | tf_op jit(solution)/shard_map/ppermute | solution.py:492
  11.0 7.3 %collective-permute-start.2 = (bf16[2,256,256]{2,1,0:T(8,128)(2,1)S(1)}, bf16[2,256,256]{2,1,0:T(8,128)(2,1)S(1)}, u32[]{:S(2)}, u32[]{:S(2)}) collective-permute-start(bf16[2,256,256]{2,1,0:T(8,128)(2,1)S(1)} %copy-done.1), channel_id=1, source_target_pairs={{0,1},{1,0},{2,3},{3,2},{4,5},{5,4},{6,7},{7,6},{8,9},{9,8},{10,11... | collective-permute-start | bytes 786440 | tf_op jit(solution)/shard_map/ppermute | solution.py:492
  11.5 6.8 %collective-permute-start.3 = (bf16[2,256,256]{2,1,0:T(8,128)(2,1)S(1)}, bf16[2,256,256]{2,1,0:T(8,128)(2,1)S(1)}, u32[]{:S(2)}, u32[]{:S(2)}) collective-permute-start(bf16[2,256,256]{2,1,0:T(8,128)(2,1)S(1)} %copy-done.4), channel_id=1, source_target_pairs={{0,1},{1,0},{2,3},{3,2},{4,5},{5,4},{6,7},{7,6},{8,9},{9,8},{10,11... | collective-permute-start | bytes 786440 | tf_op jit(solution)/shard_map/ppermute | solution.py:492
  18.3 1.3 %collective-permute-start = (bf16[256,256]{1,0:T(8,128)(2,1)S(1)}, bf16[256,256]{1,0:T(8,128)(2,1)S(1)}, u32[]{:S(2)}, u32[]{:S(2)}) collective-permute-start(bf16[256,256]{1,0:T(8,128)(2,1)S(1)} %bitcast.23), channel_id=1, source_target_pairs={{0,1},{1,0},{2,3},{3,2},{4,5},{5,4},{6,7},{7,6},{8,9},{9,8},{10,11... | collective-permute-start | bytes 393224 | tf_op jit(solution)/shard_map/ppermute | solution.py:450
  18.3 1.3 %copy-start.5 = (bf16[2,256,256]{2,1,0:T(8,128)(2,1)}, bf16[2,256,256]{2,1,0:T(8,128)(2,1)S(1)}, u32[]{:S(2)}) copy-start(bf16[2,256,256]{2,1,0:T(8,128)(2,1)S(1)} %collective-permute-done.3.refs_10_) | copy-start | bytes 786436
  23.9 12.1 %all-to-all-start.1 = ((bf16[8,32,256]{2,1,0:T(8,128)(2,1)}), bf16[8,32,256]{2,1,0:T(8,128)(2,1)S(1)}, u32[]{:S(2)}, u32[]{:S(2)}) async-start(bf16[8,32,256]{2,1,0:T(8,128)(2,1)} %bitcast.33), calls=%async_computation.1 | async-start | bytes 262144 | tf_op jit(solution)/shard_map/all_to_all | solution.py:446
  36.0 1.3 %collective-permute-start.4 = (bf16[256,256]{1,0:T(8,128)(2,1)S(1)}, bf16[256,256]{1,0:T(8,128)(2,1)S(1)}, u32[]{:S(2)}, u32[]{:S(2)}) collective-permute-start(bf16[256,256]{1,0:T(8,128)(2,1)S(1)} %bitcast.27), channel_id=1, source_target_pairs={{0,1},{1,0},{2,3},{3,2},{4,5},{5,4},{6,7},{7,6},{8,9},{9,8},{10,11... | collective-permute-start | bytes 393224 | tf_op jit(solution)/shard_map/ppermute | solution.py:450
  43.5 10.9 %all-to-all-start.2 = ((bf16[8,32,256]{2,1,0:T(8,128)(2,1)}), bf16[8,32,256]{2,1,0:T(8,128)(2,1)S(1)}, u32[]{:S(2)}, u32[]{:S(2)}) async-start(bf16[8,32,256]{2,1,0:T(8,128)(2,1)} %bitcast.32), calls=%async_computation.2 | async-start | bytes 262144 | tf_op jit(solution)/shard_map/all_to_all | solution.py:446
  54.4 1.3 %collective-permute-start.5 = (bf16[256,256]{1,0:T(8,128)(2,1)S(1)}, bf16[256,256]{1,0:T(8,128)(2,1)S(1)}, u32[]{:S(2)}, u32[]{:S(2)}) collective-permute-start(bf16[256,256]{1,0:T(8,128)(2,1)S(1)} %bitcast.25), channel_id=1, source_target_pairs={{0,1},{1,0},{2,3},{3,2},{4,5},{5,4},{6,7},{7,6},{8,9},{9,8},{10,11... | collective-permute-start | bytes 393224 | tf_op jit(solution)/shard_map/ppermute | solution.py:450
  55.8 15.7 %all-to-all-start.3 = ((bf16[8,96,256]{2,1,0:T(8,128)(2,1)}), bf16[8,96,256]{2,1,0:T(8,128)(2,1)S(1)}, u32[]{:S(2)}, u32[]{:S(2)}) async-start(bf16[8,96,256]{2,1,0:T(8,128)(2,1)} %bitcast.6), calls=%async_computation.3 | async-start | bytes 786432 | tf_op jit(solution)/shard_map/all_to_all | solution.py:446
  71.5 18.3 %all-to-all-start.4 = ((bf16[8,128,256]{2,1,0:T(8,128)(2,1)}), bf16[8,128,256]{2,1,0:T(8,128)(2,1)S(1)}, u32[]{:S(2)}, u32[]{:S(2)}) async-start(bf16[8,128,256]{2,1,0:T(8,128)(2,1)} %get-tuple-element.67), calls=%async_computation.4 | async-start | bytes 1048576 | tf_op jit(solution)/shard_map/all_to_all | solution.py:446
  90.8 24.0 %all-to-all-start.5 = ((bf16[8,192,256]{2,1,0:T(8,128)(2,1)}), bf16[8,192,256]{2,1,0:T(8,128)(2,1)S(1)}, u32[]{:S(2)}, u32[]{:S(2)}) async-start(bf16[8,192,256]{2,1,0:T(8,128)(2,1)} %broadcast_in_dim.2), calls=%async_computation.5 | async-start | bytes 1572864 | tf_op jit(solution)/shard_map/all_to_all | solution.py:446
  94.5 1.4 %collective-permute-start.6 = (bf16[256,256]{1,0:T(8,128)(2,1)S(1)}, bf16[256,256]{1,0:T(8,128)(2,1)S(1)}, u32[]{:S(2)}, u32[]{:S(2)}) collective-permute-start(bf16[256,256]{1,0:T(8,128)(2,1)S(1)} %bitcast.21), channel_id=1, source_target_pairs={{0,1},{1,0},{2,3},{3,2},{4,5},{5,4},{6,7},{7,6},{8,9},{9,8},{10,11... | collective-permute-start | bytes 393224 | tf_op jit(solution)/shard_map/ppermute | solution.py:450

commit v3 on v2

--- a/solution.py
+++ b/solution.py
@@ -28,10 +28,10 @@
 
 
 class Traffic:
-    def __init__(self, ins, outs, in_sems, out_sems):
+    def __init__(self, ins, outs, in_sems, out_sems, late):
         self.ins, self.outs, self.in_sems, self.out_sems = ins, outs, in_sems, out_sems
         self.leaving = []
-        for k in range(len(ins)):
+        for k in sorted(range(len(ins)), key=lambda k: late(k)):
             if self.moves(k):
                 self.arriving(k).start()
 
@@ -82,6 +82,7 @@
             [(n, f, cut) for n, f, (_, cut) in zip(near_out, far_out, outs)],
             in_sems,
             out_sems,
+            lambda k: far_ins[k][0].shape[-1] == LANES,
         )
         shown = [near_out[k] for k in range(len(outs)) if outs[k][1] != "later"]
         kernel(traffic, *fixed, *near_in, *shown, *own)
@@ -250,12 +251,13 @@
     sum_ref, send_row_ref, recv_row_ref, recv_col_ref, near_ref, dense_ref, sems, state_ref,
 ):
     dense = Dense(cols_ref, tile_ref, near_ref, dense_ref, sems)
-    dense.zero()
     rows, width = feats_ref.shape
-    traffic.need(send_ref, recv_ref, feats_ref)
+    traffic.need(send_ref, recv_ref)
     fill_row(parts, send_row_ref, send_ref, sent(count_ref, used_ref))
     fill_row(parts, recv_row_ref, recv_ref, always)
     fill_columns(recv_col_ref, recv_ref, always)
+    dense.zero()
+    traffic.need(feats_ref)
     state_ref[...] = jnp.where(live(count_ref, 0, rows, width), feats_ref[...], jnp.zeros((), BF16))
     for k in (1, 2, 3):
         traffic.put(k)
@@ -351,10 +353,14 @@
     traffic.put(2)
 
 
-def turn_kernel(parts, layer, traffic, count_ref, col_ref, row_ref, *refs):
+def turn_kernel(parts, layer, paired, traffic, count_ref, col_ref, row_ref, *refs):
     arriving, refs = refs[:parts], refs[parts:]
     weights = triples(refs[: 3 * parts], layer)
-    sum_ref, state_ref, grad_ref, final_ref, agg_ref, out_ref, dw_ref, acts_ref, *kept = refs[3 * parts :]
+    sum_ref, state_ref, grad_ref, final_ref, agg_ref, out_ref, *refs = refs[3 * parts :]
+    if paired:
+        acts_ref, *kept, dw_ref, sems = refs
+    else:
+        dw_ref, acts_ref, *kept = refs
     width = state_ref.shape[1]
     for at in pieces_of(state_ref.shape[0]):
         size = at.stop - at.start
@@ -362,10 +368,12 @@
         acts_ref[at, :] = acts
         terms = gates(acts, weights)
         if at.start == 0:
-            traffic.need(*(down_ref for _, _, down_ref in weights), state_ref, grad_ref)
+            traffic.need(*(down_ref for _, _, down_ref in weights), state_ref)
         after = state_ref[at, :].astype(F32) + mix(terms, weights)
         alive = live(count_ref, at.start, size, width)
         final_ref[at, :] = jnp.where(alive, after, 0.0).astype(BF16)
+        if at.start == 0:
+            traffic.need(grad_ref)
         down_in = jnp.where(alive, grad_ref[at, :], jnp.zeros((), BF16))
         layer_grads(at, acts, terms, down_in, weights, agg_ref, kept)
     traffic.put(0)
@@ -373,27 +381,42 @@
     gather_rows(col_ref, agg_ref, out_ref)
     traffic.put(2)
     weight_grads(acts_ref, kept, dw_ref)
-    traffic.put(3)
-
-
-def put_pieces(traffic, k, sources, sem):
+    if paired:
+        put_halves(traffic, 3, dw_ref, sems)
+    else:
+        traffic.put(3)
+
+
+def put_halves(traffic, k, source, sems):
+    half = source.shape[0] // 2
+    mine = lax.rem(lax.axis_index("dom"), 2)
+    for j, which in enumerate((mine, 1 - mine)):
+        at = pl.ds(pl.multiple_of(which * half, half), half)
+        copy = pltpu.make_async_copy(source.at[at], traffic.outs[k + j][1], sems.at[j])
+        copy.start()
+        traffic.leaving.append(copy)
+
+
+def put_pieces(traffic, k, first, source, sems):
     far = traffic.outs[k][1]
+    rows = source.shape[0] // far.shape[0]
     for q in range(far.shape[0]):
-        first = 0
-        for source in sources:
-            rows = source.shape[0] // far.shape[0]
-            copy = pltpu.make_async_copy(
-                source.at[pl.ds(q * rows, rows)], far.at[q, pl.ds(first, rows)], sem.at[q]
-            )
-            copy.start()
-            traffic.leaving.append(copy)
-            first += rows
-
-
-def backward_kernel(parts, layer, traffic, count_ref, col_ref, row_ref, *refs):
+        copy = pltpu.make_async_copy(source.at[pl.ds(q * rows, rows)], far.at[q, pl.ds(first, rows)], sems.at[q])
+        copy.start()
+        traffic.leaving.append(copy)
+    return first + rows
+
+
+def backward_kernel(parts, layer, counts, traffic, count_ref, col_ref, row_ref, *refs):
     arriving, refs = refs[:parts], refs[parts:]
     weights = triples(refs[: 3 * parts], layer)
-    sum_ref, acts_ref, upstream_ref, agg_ref, out_ref, dw_ref, sem, *kept = refs[3 * parts :]
+    sum_ref, acts_ref, *refs = refs[3 * parts :]
+    earlier, refs = refs[: sum(counts)], refs[sum(counts) :]
+    upstream_ref, agg_ref, out_ref, dw_ref, *refs = refs
+    if counts:
+        added, sems, kept = refs[: len(counts)], refs[len(counts)], refs[len(counts) + 1 :]
+    else:
+        kept = refs
     rows, width = acts_ref.shape
     for at in pieces_of(rows):
         size = at.stop - at.start
@@ -404,10 +427,24 @@
     for at in pieces_of(rows):
         acts = acts_ref[at, :]
         layer_grads(at, acts, gates(acts, weights), upstream_ref[at, :], weights, agg_ref, kept)
-    traffic.need(col_ref)
+    traffic.need(col_ref, *earlier)
     gather_rows(col_ref, agg_ref, out_ref)
+    if not counts:
+        traffic.put(2)
+        weight_grads(acts_ref, (*kept, upstream_ref), dw_ref)
+        traffic.put(3)
+        return
+    first = put_pieces(traffic, 2, 0, out_ref, sems.at[0])
+    taken = 0
+    for k, count in enumerate(counts):
+        total = earlier[taken][...].astype(F32)
+        for ref in earlier[taken + 1 : taken + count]:
+            total = total + ref[...].astype(F32)
+        added[k][...] = total.astype(BF16)
+        taken += count
+        first = put_pieces(traffic, 2, first, added[k], sems.at[1 + k])
     weight_grads(acts_ref, (*kept, upstream_ref), dw_ref)
-    put_pieces(traffic, 2, (out_ref, dw_ref), sem)
+    put_pieces(traffic, 2, first, dw_ref, sems.at[1 + len(counts)])
 
 
 def last_kernel(traffic, count_ref, row_ref, *refs):
@@ -533,20 +570,29 @@
             local_kernel, [near(sum_shape)], [cols, state, tiles], local_flops, "local", dense_scratch
         )
         total, arriving = share_after(total, arriving)
-    final, agg, outgoing, dw = call(
-        functools.partial(turn_kernel, parts, layers - 1),
-        [far(state_shape), near(state_shape), far(slot_shape), far(dw_shape)],
+    half_dw = shape((dw_shape.shape[0] // 2, width), BF16)
+    paired = peers % 2 == 0 and layers > 1 and half_dw.shape[0] % (16 * peers) == 0
+    dw_scratch = pltpu.VMEM(dw_shape.shape, BF16)
+    final, agg, outgoing, *dw = call(
+        functools.partial(turn_kernel, parts, layers - 1, paired),
+        [
+            far(state_shape), near(state_shape), far(slot_shape),
+            *([(half_dw, "later")] * 2 if paired else [far(dw_shape)]),
+        ],
         [
             count, far(recv_col), near(recv_row), *map(near, arriving), *weights(layers - 1), near(total),
             state, far(out_grad),
         ],
         3 * layer_flops + 2 * slot_flops,
         "turn",
-        [pltpu.VMEM((rows, width), BF16), *kept_shapes],
+        [
+            pltpu.VMEM((rows, width), BF16),
+            *kept_shapes,
+            *([dw_scratch, pltpu.SemaphoreType.DMA((2,))] if paired else []),
+        ],
     )
     piece = dw_shape.shape[0] // peers
     own_slots = slot_count // parts
-    both_shape = shape((peers, own_slots + piece, width), BF16)
 
     def turned_local(agg, upstream):
         return call(
@@ -558,39 +604,44 @@
             dense_scratch,
         )[0]
 
-    def added(pieces):
-        return jnp.sum(pieces.astype(F32), axis=0).astype(BF16)
-
-    arriving = exchange(outgoing)
-    total, arriving = share_after(turned_local(agg, out_grad), arriving)
-    reduced = [None] * layers
+    upstream = out_grad
+    earlier = []
     for layer in reversed(range(layers - 1)):
-        if layer == layers - 2:
-            arriving, dw = lax.optimization_barrier((arriving, dw))
-            pieces = swap(dw.reshape(peers, piece, width))
-        upstream, agg, both = call(
-            functools.partial(backward_kernel, parts, layer),
-            [far(sum_shape), near(state_shape), (both_shape, "later")],
+        moved = exchange(outgoing)
+        if len(dw) == 2:
+            dw = [dw[0], lax.ppermute(dw[1], "dom", [(d, d ^ 1) for d in range(peers)])]
+        total, arriving = share_after(turned_local(agg, upstream), moved)
+        earlier.append(dw)
+        bottom = layer == 0
+        counts = [len(addends) for addends in earlier] if bottom else []
+        lengths = [addends[0].shape[0] for addends in earlier]
+        wide = shape((peers, own_slots + sum(lengths) // peers + piece, width), BF16)
+        upstream, agg, outgoing, *dw = call(
+            functools.partial(backward_kernel, parts, layer, counts),
+            [far(sum_shape), near(state_shape), *([(wide, "later")] if bottom else [far(slot_shape), far(dw_shape)])],
             [
                 count, far(recv_col), near(send_row), *map(near, arriving), *weights(layer), near(total),
-                far(kept[layer]),
+                far(kept[layer]), *(far(x) for addends in earlier for x in addends if bottom),
             ],
             3 * layer_flops + 2 * slot_flops,
             "backward",
             [
-                pltpu.VMEM(slot_shape.shape, BF16),
-                pltpu.VMEM(dw_shape.shape, BF16),
-                pltpu.SemaphoreType.DMA((peers,)),
+                *([pltpu.VMEM(slot_shape.shape, BF16), dw_scratch] if bottom else []),
+                *(pltpu.VMEM((n, width), BF16) for n in lengths if bottom),
+                *([pltpu.SemaphoreType.DMA((2 + len(counts), peers))] if bottom else []),
                 *kept_shapes[:2],
             ],
         )
-        if layer == layers - 2:
-            both, reduced[layer + 1] = lax.optimization_barrier((both, added(pieces)))
-        both = swap(both)
-        total, both = lax.optimization_barrier((turned_local(agg, upstream), both))
-        arriving = share(both[:, :own_slots])
-        reduced[layer] = added(both[:, own_slots:])
-    own = jnp.concatenate(reduced)
+    total, pieces = lax.optimization_barrier((turned_local(agg, upstream), swap(outgoing)))
+    arriving = share(pieces[:, :own_slots])
+    sizes = [n // peers for n in lengths] + [piece]
+    cuts = [own_slots + sum(sizes[:k]) for k in range(len(sizes))]
+    owned = []
+    for first, size in zip(cuts, sizes):
+        groups = piece // size
+        part = pieces[:, first : first + size].astype(F32).reshape(peers // groups, groups * size, width)
+        owned.append(jnp.sum(part, axis=0).astype(BF16))
+    own = jnp.concatenate(owned)
     full = swap(jnp.broadcast_to(own[None], (peers, *own.shape)))
     (feat_grad,) = call(
         last_kernel,
@@ -599,8 +650,12 @@
         slot_flops,
         "last",
     )
-    full = full.reshape(peers, layers, piece, width).swapaxes(0, 1).reshape(layers, 3, width, hidden_width)
-    full = full.swapaxes(0, 1).astype(F32)
+    by_layer = []
+    for k, size in enumerate(sizes):
+        groups = piece // size
+        rows_of_layer = full[:, k * piece : (k + 1) * piece].reshape(peers, groups, size, width).swapaxes(0, 1)
+        by_layer.append(rows_of_layer.reshape(3, width, hidden_width))
+    full = jnp.stack(by_layer[::-1], axis=1).astype(F32)
     return (final, feat_grad, full[0], full[1], full[2])
 
 

time: 117 us -> 113 us (0.966)
  waiting for transfers between devices: 46.2 us -> 43.1 us
  starting transfers between devices: 26.9 us -> 25.6 us
    all_to_all x6 -> x5, waiting for transfers between devices: 40.8 us -> 37.7 us  [swap(): lax.all_to_all(blocks, 'dom', split_axis=0, concat_axis=0, tiled=True)]
    all_to_all x6 -> x5, starting transfers between devices: 26.2 us -> 23.2 us  [swap(): lax.all_to_all(blocks, 'dom', split_axis=0, concat_axis=0, tiled=True)]
    ppermute x0 -> x1, starting transfers between devices: none -> 1.7 us  [local(): dw = [dw[0], lax.ppermute(dw[1], 'dom', [(d, d ^ 1) for d in range(peers)])]]
  transfers between devices with their start and end apart: 13 -> 13, of which waited for: 10 -> 10; matrix products, arithmetic and copies ran while one was open for 0% -> 0% of each run, Pallas kernels for 23% -> 17%
where the time goes in v3:
time: 113 us; the launch traced here: 112 us
  waiting for transfers between devices  43.1 us (38%)
  Pallas kernels  38.8 us (34%)
  starting transfers between devices  25.6 us (23%)
  local copies, waits for them, and re-layouts  2.72 us (2%)
  between operations  1.58 us (1%)
    pallas_call x9, Pallas kernels, call(): pl.pallas_call(body, out_shape=[space(cut)(x.shape, x.dtype) for x, cut i...  38.8 us
    all_to_all x5, waiting for transfers between devices, swap(): lax.all_to_all(blocks, 'dom', split_axis=0, concat_axis=0, tiled=True)  37.7 us
    all_to_all x5, starting transfers between devices, swap(): lax.all_to_all(blocks, 'dom', split_axis=0, concat_axis=0, tiled=True)  23.2 us
    ppermute x4, waiting for transfers between devices, share(): return [rows] + [lax.ppermute(rows, 'mp', turn) for turn in turns]  4.27 us
  transfers between devices with their start and end apart: 13, of which 10 were waited for; matrix products, arithmetic and copies ran while one was open for 0% of the time, Pallas kernels for 17%

profile of v3, /device:TPU:0, one launch (start us, length us, event | category | flops | bytes accessed | tf_op | source)
XLA Modules:
  0.0 111.9 jit_solution(1114795117469955335)
XLA Ops:
  0.6 0.0 copy-start.2
  0.6 0.0 copy-start.4
  0.7 0.0 copy-start.1
  1.4 2.2 %send.1 = (bf16[256,256]{1,0:T(8,128)(2,1)}, s32[256,128]{1,0:T(8,128)}) custom-call(s32[1]{0:T(128)S(6)} %copy.30.refs_0_, s32[1,8]{1,0:T(1,128)} %refs_1_.5, s32[1,8,64]{2,1,0:T(8,128)} %refs_2_.3, bf16[1536,256]{1,0:T(8,128)(2,1)} %refs_12_.1), custom_call_target="tpu_custom_call" | custom-call | flops 402653184 | bytes 1050660 | tf_op jit(solution)/shard_map/send/pallas_call | solution.py:99
  3.6 7.3 %all-to-all-start = ((bf16[8,32,256]{2,1,0:T(8,128)(2,1)}), bf16[8,32,256]{2,1,0:T(8,128)(2,1)S(1)}, u32[]{:S(2)}, u32[]{:S(2)}) async-start(bf16[8,32,256]{2,1,0:T(8,128)(2,1)} %bitcast.33), calls=%async_computation | async-start | bytes 262144 | tf_op jit(solution)/shard_map/all_to_all | solution.py:483
  11.0 0.1 collective-permute-start.1
  11.0 0.0 copy-done.1
  11.0 0.5 collective-permute-start.2
  11.5 0.0 copy-done.4
  11.5 0.1 collective-permute-start.3
  11.6 0.1 copy.25.refs_2_.refs_0_.refs_1_
  11.7 4.7 %first_local.1 = (bf16[1536,256]{1,0:T(8,128)(2,1)S(1)}, s32[1,512]{1,0:T(1,128)S(1)}, s32[1,512]{1,0:T(1,128)S(1)}, s32[256,128]{1,0:T(8,128)}) custom-call(s32[1]{0:T(128)S(6)} %copy.30.refs_0_, s32[1,8]{1,0:T(1,128)S(1)} %copy-done.2, s32[12,8]{1,0:T(8,128)S(1)} %copy.25.refs_2_.refs_0_.refs_1_, s32[1,8,64]{2,1,0:T(8,128)} %refs_2_.3, ...), custom_call_target="tpu_custom_call" | custom-call | flops 1207959552 | bytes 4858276 | tf_op jit(solution)/shard_map/first_local/pallas_call | solution.py:99
  16.4 1.9 %all-to-all-done = bf16[8,32,256]{2,1,0:T(8,128)(2,1)S(1)} async-done(((bf16[8,32,256]{2,1,0:T(8,128)(2,1)}), bf16[8,32,256]{2,1,0:T(8,128)(2,1)S(1)}, u32[]{:S(2)}, u32[]{:S(2)}) %all-to-all-start) | async-done | bytes 131104 | tf_op jit(solution)/shard_map/all_to_all | solution.py:483
  18.3 0.0 collective-permute-start
  18.3 0.0 collective-permute-done.1.refs_8_
  18.3 0.0 collective-permute-done.2.refs_9_
  18.3 0.0 collective-permute-done.3.refs_10_
  18.3 0.0 copy-start.5
  18.3 1.3 %collective-permute-done.refs_4_ = bf16[256,256]{1,0:T(8,128)(2,1)S(1)} collective-permute-done((bf16[256,256]{1,0:T(8,128)(2,1)S(1)}, bf16[256,256]{1,0:T(8,128)(2,1)S(1)}, u32[]{:S(2)}, u32[]{:S(2)}) %collective-permute-start) | collective-permute-done | bytes 131104 | tf_op jit(solution)/shard_map/ppermute | solution.py:487
  19.6 4.2 %forward.1 = (bf16[1536,256]{1,0:T(8,128)(2,1)}, bf16[1536,256]{1,0:T(8,128)(2,1)S(1)}, bf16[256,256]{1,0:T(8,128)(2,1)}) custom-call(s32[1]{0:T(128)S(6)} %copy.30.refs_0_, s32[256,128]{1,0:T(8,128)} %get-tuple-element.36.refs_1_, s32[1,512]{1,0:T(1,128)S(1)} %get-tuple-element.35.refs_2_, bf16[256,256]{1,0:T(8,128)(2,1)S(1)} %bitcast.24, ...), custom_call_target="tpu_custom_call" | custom-call | flops 2013265920 | bytes 5244932 | tf_op jit(solution)/shard_map/forward/pallas_call | solution.py:99
  23.9 4.2 %all-to-all-start.1 = ((bf16[8,32,256]{2,1,0:T(8,128)(2,1)}), bf16[8,32,256]{2,1,0:T(8,128)(2,1)S(1)}, u32[]{:S(2)}, u32[]{:S(2)}) async-start(bf16[8,32,256]{2,1,0:T(8,128)(2,1)} %bitcast.35), calls=%async_computation.1 | async-start | bytes 262144 | tf_op jit(solution)/shard_map/all_to_all | solution.py:483
  28.0 4.1 %local.1.refs_11_ = bf16[1536,256]{1,0:T(8,128)(2,1)S(1)} custom-call(s32[12,8]{1,0:T(8,128)S(1)} %copy.25.refs_2_.refs_0_.refs_1_, bf16[1536,256]{1,0:T(8,128)(2,1)S(1)} %get-tuple-element.45.refs_1_.refs_12_, bf16[12,8,128,128]{3,2,1,0:T(8,128)(2,1)} %refs_4_.5), custom_call_target="tpu_custom_call" | custom-call | flops 1207959552 | bytes 4718976 | tf_op jit(solution)/shard_map/local/pallas_call | solution.py:99
  32.2 3.4 %all-to-all-done.1 = bf16[8,32,256]{2,1,0:T(8,128)(2,1)S(1)} async-done(((bf16[8,32,256]{2,1,0:T(8,128)(2,1)}), bf16[8,32,256]{2,1,0:T(8,128)(2,1)S(1)}, u32[]{:S(2)}, u32[]{:S(2)}) %all-to-all-start.1) | async-done | bytes 131104 | tf_op jit(solution)/shard_map/all_to_all | solution.py:483
  35.5 0.0 collective-permute-start.4
  35.5 1.3 %collective-permute-done.4.refs_4_ = bf16[256,256]{1,0:T(8,128)(2,1)S(1)} collective-permute-done((bf16[256,256]{1,0:T(8,128)(2,1)S(1)}, bf16[256,256]{1,0:T(8,128)(2,1)S(1)}, u32[]{:S(2)}, u32[]{:S(2)}) %collective-permute-start.4) | collective-permute-done | bytes 131104 | tf_op jit(solution)/shard_map/ppermute | solution.py:487
  36.9 6.3 %turn.1 = (bf16[1536,256]{1,0:T(8,128)(2,1)}, bf16[1536,256]{1,0:T(8,128)(2,1)S(1)}, bf16[256,256]{1,0:T(8,128)(2,1)}, bf16[384,256]{1,0:T(8,128)(2,1)}, bf16[384,256]{1,0:T(8,128)(2,1)}) custom-call(s32[1]{0:T(128)S(6)} %copy.30.refs_0_, s32[256,128]{1,0:T(8,128)} %get-tuple-element.34.refs_1_, s32[1,512]{1,0:T(1,128)S(1)} %get-tuple-element.35.refs_2_, ...), custom_call_target="tpu_custom_call" | custom-call | flops 4429185024 | bytes 6424580 | tf_op jit(solution)/shard_map/turn/pallas_call | solution.py:99
  43.2 3.6 %all-to-all-start.2 = ((bf16[8,32,256]{2,1,0:T(8,128)(2,1)}), bf16[8,32,256]{2,1,0:T(8,128)(2,1)S(1)}, u32[]{:S(2)}, u32[]{:S(2)}) async-start(bf16[8,32,256]{2,1,0:T(8,128)(2,1)} %bitcast.34), calls=%async_computation.2 | async-start | bytes 262144 | tf_op jit(solution)/shard_map/all_to_all | solution.py:483
  46.8 1.7 %collective-permute-start.6 = (bf16[384,256]{1,0:T(8,128)(2,1)}, bf16[384,256]{1,0:T(8,128)(2,1)S(1)}, u32[]{:S(2)}, u32[]{:S(2)}) collective-permute-start(bf16[384,256]{1,0:T(8,128)(2,1)} %get-tuple-element.57), channel_id=1, source_target_pairs={{0,2},{2,0},{4,6},{6,4},{8,10},{10,8},{12,14},{14,12},{1,3},{3,1},... | collective-permute-start | bytes 589832 | tf_op jit(solution)/shard_map/ppermute | solution.py:612
  48.5 4.5 %turned_local.2.refs_11_ = bf16[1536,256]{1,0:T(8,128)(2,1)S(1)} custom-call(s32[1]{0:T(128)S(6)} %copy.30.refs_0_, s32[12,8]{1,0:T(8,128)S(1)} %copy.25.refs_2_.refs_0_.refs_1_, bf16[1536,256]{1,0:T(8,128)(2,1)S(1)} %get-tuple-element.51.refs_2_, bf16[1536,256]{1,0:T(8,128)(2,1)} %refs_3_.5, bf16[12,8,128,128]{3,2,1,0:T(8,128)(2,1)} %refs_4_.5), custom_call_target="tpu_custom_call" | custom-call | flops 1207959552 | bytes 5505412 | tf_op jit(solution)/shard_map/turned_local/pallas_call | solution.py:99
  52.9 1.2 %all-to-all-done.2 = bf16[8,32,256]{2,1,0:T(8,128)(2,1)S(1)} async-done(((bf16[8,32,256]{2,1,0:T(8,128)(2,1)}), bf16[8,32,256]{2,1,0:T(8,128)(2,1)S(1)}, u32[]{:S(2)}, u32[]{:S(2)}) %all-to-all-start.2) | async-done | bytes 131104 | tf_op jit(solution)/shard_map/all_to_all | solution.py:483
  54.2 0.0 collective-permute-start.5
  54.2 1.1 collective-permute-done.6.refs_14_
  55.2 0.3 collective-permute-done.5.refs_4_
  55.5 0.4 copy-done.6
  55.9 6.6 %backward.1 = (bf16[1536,256]{1,0:T(8,128)(2,1)}, bf16[1536,256]{1,0:T(8,128)(2,1)S(1)}, bf16[8,176,256]{2,1,0:T(8,128)(2,1)}) custom-call(s32[1]{0:T(128)S(6)} %copy.30.refs_0_, s32[256,128]{1,0:T(8,128)} %get-tuple-element.34.refs_1_, s32[1,512]{1,0:T(1,128)S(1)} %get-tuple-element.50.refs_2_.refs_1_, bf16[256,256]{1,0:T(8,128)(2,1)S(1)} %bitcast.26, ...), custom_call_target="tpu_custom_call" | custom-call | flops 4429185024 | bytes 6227972 | tf_op jit(solution)/shard_map/backward/pallas_call | solution.py:99
  62.5 4.5 %all-to-all-start.3 = ((bf16[8,176,256]{2,1,0:T(8,128)(2,1)}), bf16[8,176,256]{2,1,0:T(8,128)(2,1)S(1)}, u32[]{:S(2)}, u32[]{:S(2)}) async-start(bf16[8,176,256]{2,1,0:T(8,128)(2,1)} %get-tuple-element.60), calls=%async_computation.3 | async-start | bytes 1441792 | tf_op jit(solution)/shard_map/all_to_all | solution.py:483
  67.0 4.5 %turned_local.3.refs_4_ = bf16[1536,256]{1,0:T(8,128)(2,1)S(1)} custom-call(s32[1]{0:T(128)S(6)} %copy.30.refs_0_, s32[12,8]{1,0:T(8,128)S(1)} %copy.25.refs_2_.refs_0_.refs_1_, bf16[1536,256]{1,0:T(8,128)(2,1)S(1)} %get-tuple-element.58.refs_2_, bf16[1536,256]{1,0:T(8,128)(2,1)} %get-tuple-element.59.refs_3_, bf16[12,8,128,128]{3,2,1,0:T(8,128)(2,1)} %refs_4_.5), custom_call_target="tpu_custom_call" | custom-call | flops 1207959552 | bytes 5505412 | tf_op jit(solution)/shard_map/turned_local/pallas_call | solution.py:99
  71.4 14.0 %all-to-all-done.3 = bf16[8,176,256]{2,1,0:T(8,128)(2,1)S(1)} async-done(((bf16[8,176,256]{2,1,0:T(8,128)(2,1)}), bf16[8,176,256]{2,1,0:T(8,128)(2,1)S(1)}, u32[]{:S(2)}, u32[]{:S(2)}) %all-to-all-start.3) | async-done | bytes 720928 | tf_op jit(solution)/shard_map/all_to_all | solution.py:483
  85.5 0.1 slice_reduce_fusion
  85.6 0.9 broadcast_in_dim.2
  86.6 3.6 %all-to-all-start.4 = ((bf16[8,192,256]{2,1,0:T(8,128)(2,1)}), bf16[8,192,256]{2,1,0:T(8,128)(2,1)S(1)}, u32[]{:S(2)}, u32[]{:S(2)}) async-start(bf16[8,192,256]{2,1,0:T(8,128)(2,1)} %broadcast_in_dim.2), calls=%async_computation.4 | async-start | bytes 1572864 | tf_op jit(solution)/shard_map/all_to_all | solution.py:483
  90.2 0.1 collective-permute-start.7
  90.2 1.3 %collective-permute-done.7.refs_3_ = bf16[256,256]{1,0:T(8,128)(2,1)S(1)} collective-permute-done((bf16[256,256]{1,0:T(8,128)(2,1)S(1)}, bf16[256,256]{1,0:T(8,128)(2,1)S(1)}, u32[]{:S(2)}, u32[]{:S(2)}) %collective-permute-start.7) | collective-permute-done | bytes 131104 | tf_op jit(solution)/shard_map/ppermute | solution.py:487
  91.6 1.8 %last.1 = f32[1536,256]{1,0:T(8,128)} custom-call(s32[1]{0:T(128)S(6)} %copy.30.refs_0_, s32[1,512]{1,0:T(1,128)S(1)} %get-tuple-element.50.refs_2_.refs_1_, bf16[256,256]{1,0:T(8,128)(2,1)S(1)} %bitcast.22, bf16[256,256]{1,0:T(8,128)(2,1)S(1)} %collective-permute-done.7.refs_3_, bf16[1536,256]{1,0:T(8,128)(2,1)S(1)} %turned_local.3.refs_4_), custom_call_target="tpu_custom_call" | custom-call | flops 402653184 | bytes 2623492 | tf_op jit(solution)/shard_map/last/pallas_call | solution.py:99
  93.3 17.2 %all-to-all-done.4 = bf16[8,192,256]{2,1,0:T(8,128)(2,1)S(1)} async-done(((bf16[8,192,256]{2,1,0:T(8,128)(2,1)}), bf16[8,192,256]{2,1,0:T(8,128)(2,1)S(1)}, u32[]{:S(2)}, u32[]{:S(2)}) %all-to-all-start.4) | async-done | bytes 786464 | tf_op jit(solution)/shard_map/all_to_all | solution.py:483
  110.5 0.1 fusion
  110.6 0.1 maximum_convert_fusion
  110.7 1.2 %slice_bitcast_fusion = (f32[2,256,256]{2,1,0:T(8,128)}, f32[2,256,256]{2,1,0:T(8,128)}, f32[2,256,256]{2,1,0:T(8,128)}) fusion(f32[3,2,256,256]{3,2,0,1:T(8,128)S(1)} %maximum_convert_fusion), kind=kLoop, calls=%fused_computation.1 | loop fusion | bytes 3145728 | tf_op jit(solution)/shard_map/squeeze | solution.py:659
  (12 shorter events, 0.1 us)
Async XLA Ops:
  0.6 11.1 %copy-start.2 = (s32[1,8]{1,0:T(1,128)S(1)}, s32[1,8]{1,0:T(1,128)}, u32[]{:S(2)}) copy-start(s32[1,8]{1,0:T(1,128)} %refs_1_.5) | copy-start | bytes 100
  0.6 10.9 %copy-start.4 = (bf16[2,256,256]{2,1,0:T(8,128)(2,1)S(1)}, bf16[2,256,256]{2,1,0:T(8,128)(2,1)}, u32[]{:S(2)}) copy-start(bf16[2,256,256]{2,1,0:T(8,128)(2,1)} %refs_7_.2) | copy-start | bytes 786436
  0.7 10.4 %copy-start.1 = (bf16[2,256,256]{2,1,0:T(8,128)(2,1)S(1)}, bf16[2,256,256]{2,1,0:T(8,128)(2,1)}, u32[]{:S(2)}) copy-start(bf16[2,256,256]{2,1,0:T(8,128)(2,1)} %refs_6_.4) | copy-start | bytes 786436
  0.7 10.3 %copy-start = (bf16[2,256,256]{2,1,0:T(8,128)(2,1)S(1)}, bf16[2,256,256]{2,1,0:T(8,128)(2,1)}, u32[]{:S(2)}) copy-start(bf16[2,256,256]{2,1,0:T(8,128)(2,1)} %refs_5_.4) | copy-start | bytes 786436
  0.7 11.0 %copy-start.3 = (s32[12,8]{0,1:T(8,128)S(1)}, s32[12,8]{0,1:T(8,128)}, u32[]{:S(2)}) copy-start(s32[12,8]{0,1:T(8,128)} %param.13) | copy-start | bytes 1156
  3.6 14.7 %all-to-all-start = ((bf16[8,32,256]{2,1,0:T(8,128)(2,1)}), bf16[8,32,256]{2,1,0:T(8,128)(2,1)S(1)}, u32[]{:S(2)}, u32[]{:S(2)}) async-start(bf16[8,32,256]{2,1,0:T(8,128)(2,1)} %bitcast.33), calls=%async_computation | async-start | bytes 262144 | tf_op jit(solution)/shard_map/all_to_all | solution.py:483
  11.0 7.3 %collective-permute-start.1 = (bf16[2,256,256]{2,1,0:T(8,128)(2,1)S(1)}, bf16[2,256,256]{2,1,0:T(8,128)(2,1)S(1)}, u32[]{:S(2)}, u32[]{:S(2)}) collective-permute-start(bf16[2,256,256]{2,1,0:T(8,128)(2,1)S(1)} %copy-done), channel_id=1, source_target_pairs={{0,1},{1,0},{2,3},{3,2},{4,5},{5,4},{6,7},{7,6},{8,9},{9,8},{10,11... | collective-permute-start | bytes 786440 | tf_op jit(solution)/shard_map/ppermute | solution.py:529
  11.0 7.3 %collective-permute-start.2 = (bf16[2,256,256]{2,1,0:T(8,128)(2,1)S(1)}, bf16[2,256,256]{2,1,0:T(8,128)(2,1)S(1)}, u32[]{:S(2)}, u32[]{:S(2)}) collective-permute-start(bf16[2,256,256]{2,1,0:T(8,128)(2,1)S(1)} %copy-done.1), channel_id=1, source_target_pairs={{0,1},{1,0},{2,3},{3,2},{4,5},{5,4},{6,7},{7,6},{8,9},{9,8},{10,11... | collective-permute-start | bytes 786440 | tf_op jit(solution)/shard_map/ppermute | solution.py:529
  11.5 6.8 %collective-permute-start.3 = (bf16[2,256,256]{2,1,0:T(8,128)(2,1)S(1)}, bf16[2,256,256]{2,1,0:T(8,128)(2,1)S(1)}, u32[]{:S(2)}, u32[]{:S(2)}) collective-permute-start(bf16[2,256,256]{2,1,0:T(8,128)(2,1)S(1)} %copy-done.4), channel_id=1, source_target_pairs={{0,1},{1,0},{2,3},{3,2},{4,5},{5,4},{6,7},{7,6},{8,9},{9,8},{10,11... | collective-permute-start | bytes 786440 | tf_op jit(solution)/shard_map/ppermute | solution.py:529
  18.3 1.3 %collective-permute-start = (bf16[256,256]{1,0:T(8,128)(2,1)S(1)}, bf16[256,256]{1,0:T(8,128)(2,1)S(1)}, u32[]{:S(2)}, u32[]{:S(2)}) collective-permute-start(bf16[256,256]{1,0:T(8,128)(2,1)S(1)} %bitcast.23), channel_id=1, source_target_pairs={{0,1},{1,0},{2,3},{3,2},{4,5},{5,4},{6,7},{7,6},{8,9},{9,8},{10,11... | collective-permute-start | bytes 393224 | tf_op jit(solution)/shard_map/ppermute | solution.py:487
  18.3 1.3 %copy-start.5 = (bf16[2,256,256]{2,1,0:T(8,128)(2,1)}, bf16[2,256,256]{2,1,0:T(8,128)(2,1)S(1)}, u32[]{:S(2)}) copy-start(bf16[2,256,256]{2,1,0:T(8,128)(2,1)S(1)} %collective-permute-done.3.refs_10_) | copy-start | bytes 786436
  23.9 11.7 %all-to-all-start.1 = ((bf16[8,32,256]{2,1,0:T(8,128)(2,1)}), bf16[8,32,256]{2,1,0:T(8,128)(2,1)S(1)}, u32[]{:S(2)}, u32[]{:S(2)}) async-start(bf16[8,32,256]{2,1,0:T(8,128)(2,1)} %bitcast.35), calls=%async_computation.1 | async-start | bytes 262144 | tf_op jit(solution)/shard_map/all_to_all | solution.py:483
  35.5 1.3 %collective-permute-start.4 = (bf16[256,256]{1,0:T(8,128)(2,1)S(1)}, bf16[256,256]{1,0:T(8,128)(2,1)S(1)}, u32[]{:S(2)}, u32[]{:S(2)}) collective-permute-start(bf16[256,256]{1,0:T(8,128)(2,1)S(1)} %bitcast.27), channel_id=1, source_target_pairs={{0,1},{1,0},{2,3},{3,2},{4,5},{5,4},{6,7},{7,6},{8,9},{9,8},{10,11... | collective-permute-start | bytes 393224 | tf_op jit(solution)/shard_map/ppermute | solution.py:487
  43.2 11.0 %all-to-all-start.2 = ((bf16[8,32,256]{2,1,0:T(8,128)(2,1)}), bf16[8,32,256]{2,1,0:T(8,128)(2,1)S(1)}, u32[]{:S(2)}, u32[]{:S(2)}) async-start(bf16[8,32,256]{2,1,0:T(8,128)(2,1)} %bitcast.34), calls=%async_computation.2 | async-start | bytes 262144 | tf_op jit(solution)/shard_map/all_to_all | solution.py:483
  46.8 8.5 %collective-permute-start.6 = (bf16[384,256]{1,0:T(8,128)(2,1)}, bf16[384,256]{1,0:T(8,128)(2,1)S(1)}, u32[]{:S(2)}, u32[]{:S(2)}) collective-permute-start(bf16[384,256]{1,0:T(8,128)(2,1)} %get-tuple-element.57), channel_id=1, source_target_pairs={{0,2},{2,0},{4,6},{6,4},{8,10},{10,8},{12,14},{14,12},{1,3},{3,1},... | collective-permute-start | bytes 589832 | tf_op jit(solution)/shard_map/ppermute | solution.py:612
  54.2 1.3 %collective-permute-start.5 = (bf16[256,256]{1,0:T(8,128)(2,1)S(1)}, bf16[256,256]{1,0:T(8,128)(2,1)S(1)}, u32[]{:S(2)}, u32[]{:S(2)}) collective-permute-start(bf16[256,256]{1,0:T(8,128)(2,1)S(1)} %bitcast.25), channel_id=1, source_target_pairs={{0,1},{1,0},{2,3},{3,2},{4,5},{5,4},{6,7},{7,6},{8,9},{9,8},{10,11... | collective-permute-start | bytes 393224 | tf_op jit(solution)/shard_map/ppermute | solution.py:487
  55.2 0.7 copy-start.6
  62.5 23.0 %all-to-all-start.3 = ((bf16[8,176,256]{2,1,0:T(8,128)(2,1)}), bf16[8,176,256]{2,1,0:T(8,128)(2,1)S(1)}, u32[]{:S(2)}, u32[]{:S(2)}) async-start(bf16[8,176,256]{2,1,0:T(8,128)(2,1)} %get-tuple-element.60), calls=%async_computation.3 | async-start | bytes 1441792 | tf_op jit(solution)/shard_map/all_to_all | solution.py:483
  86.6 24.0 %all-to-all-start.4 = ((bf16[8,192,256]{2,1,0:T(8,128)(2,1)}), bf16[8,192,256]{2,1,0:T(8,128)(2,1)S(1)}, u32[]{:S(2)}, u32[]{:S(2)}) async-start(bf16[8,192,256]{2,1,0:T(8,128)(2,1)} %broadcast_in_dim.2), calls=%async_computation.4 | async-start | bytes 1572864 | tf_op jit(solution)/shard_map/all_to_all | solution.py:483
  90.2 1.4 %collective-permute-start.7 = (bf16[256,256]{1,0:T(8,128)(2,1)S(1)}, bf16[256,256]{1,0:T(8,128)(2,1)S(1)}, u32[]{:S(2)}, u32[]{:S(2)}) collective-permute-start(bf16[256,256]{1,0:T(8,128)(2,1)S(1)} %bitcast.21), channel_id=1, source_target_pairs={{0,1},{1,0},{2,3},{3,2},{4,5},{5,4},{6,7},{7,6},{8,9},{9,8},{10,11... | collective-permute-start | bytes 393224 | tf_op jit(solution)/shard_map/ppermute | solution.py:487

commit v4 on v3

--- a/solution.py
+++ b/solution.py
@@ -15,7 +15,7 @@
 SUB = 512
 SLOTS = 512
 GRANT = 48 * 1024 * 1024
-TILE_COPIES = 3
+TILE_COPIES = 2
 
 
 def shape(dims, dtype):
@@ -204,11 +204,15 @@
     return total
 
 
-def send_kernel(traffic, count_ref, used_ref, list_ref, feats_ref, out_ref, col_ref, pick_ref):
-    traffic.need(used_ref, list_ref)
+def send_kernel(
+    traffic, count_ref, used_ref, list_ref, recv_ref, feats_ref, out_ref, col_ref, recv_col_ref, pick_ref
+):
+    traffic.need(used_ref, list_ref, recv_ref)
     fill_columns(col_ref, list_ref, sent(count_ref, used_ref))
     traffic.put(1)
     pick_ref[...] = picks(col_ref[...], feats_ref.shape[0])
+    fill_columns(recv_col_ref, recv_ref, always)
+    traffic.put(2)
     traffic.need(feats_ref)
     out_ref[...] = mm(pick_ref[...], feats_ref[...]).astype(BF16)
     traffic.put(0)
@@ -248,19 +252,16 @@
 
 def first_local_kernel(
     parts, traffic, count_ref, used_ref, cols_ref, send_ref, recv_ref, feats_ref, tile_ref,
-    sum_ref, send_row_ref, recv_row_ref, recv_col_ref, near_ref, dense_ref, sems, state_ref,
+    sum_ref, send_row_ref, recv_row_ref, near_ref, dense_ref, sems, state_ref,
 ):
     dense = Dense(cols_ref, tile_ref, near_ref, dense_ref, sems)
     rows, width = feats_ref.shape
     traffic.need(send_ref, recv_ref)
     fill_row(parts, send_row_ref, send_ref, sent(count_ref, used_ref))
     fill_row(parts, recv_row_ref, recv_ref, always)
-    fill_columns(recv_col_ref, recv_ref, always)
     dense.zero()
     traffic.need(feats_ref)
     state_ref[...] = jnp.where(live(count_ref, 0, rows, width), feats_ref[...], jnp.zeros((), BF16))
-    for k in (1, 2, 3):
-        traffic.put(k)
     local_sums(traffic, dense, state_ref, sum_ref, 0)
 
 
@@ -516,10 +517,10 @@
     layer_flops = 6 * rows * width * hidden_width * parts
     count = (cell_count, None)
 
-    outgoing, send_col = call(
+    outgoing, send_col, recv_col = call(
         send_kernel,
-        [far(slot_shape), far(col_shape)],
-        [count, (send_count, "scalars"), far(send_list), far(feats)],
+        [far(slot_shape), far(col_shape), far(col_shape)],
+        [count, (send_count, "scalars"), far(send_list), far(recv_list), far(feats)],
         slot_flops,
         "send",
         [pltpu.VMEM((slots // parts, rows), BF16)],
@@ -531,13 +532,12 @@
     def weights(layer):
         return [spec for gate, up, down in held for spec in (near(gate), near(up), (down, Layer(layer)))]
 
-    total, send_row, recv_row, recv_col = call(
+    total, send_row, recv_row = call(
         functools.partial(first_local_kernel, parts),
         [
             near(sum_shape),
             near(row_shape),
             near(row_shape),
-            far(col_shape),
         ],
         [
             count,

time: 113 us -> 113 us (level)
  transfers between devices with their start and end apart: 13 -> 13, of which waited for: 10 -> 10; matrix products, arithmetic and copies ran while one was open for 0% -> 0% of each run, Pallas kernels for 17% -> 18%
where the time goes in v4:
time: 113 us; the launch traced here: 112 us
  waiting for transfers between devices  42.8 us (38%)
  Pallas kernels  39.2 us (35%)
  starting transfers between devices  25.5 us (23%)
  local copies, waits for them, and re-layouts  2.72 us (2%)
  between operations  1.58 us (1%)
    pallas_call x9, Pallas kernels, call(): pl.pallas_call(body, out_shape=[space(cut)(x.shape, x.dtype) for x, cut i...  39.2 us
    all_to_all x5, waiting for transfers between devices, swap(): lax.all_to_all(blocks, 'dom', split_axis=0, concat_axis=0, tiled=True)  37.5 us
    all_to_all x5, starting transfers between devices, swap(): lax.all_to_all(blocks, 'dom', split_axis=0, concat_axis=0, tiled=True)  23.1 us
    ppermute x4, waiting for transfers between devices, share(): return [rows] + [lax.ppermute(rows, 'mp', turn) for turn in turns]  4.27 us
  transfers between devices with their start and end apart: 13, of which 10 were waited for; matrix products, arithmetic and copies ran while one was open for 0% of the time, Pallas kernels for 18%

profile of v4, /device:TPU:0, one launch (start us, length us, event | category | flops | bytes accessed | tf_op | source)
XLA Modules:
  0.0 112.0 jit_solution(13679739780967879624)
XLA Ops:
  0.6 0.0 copy-start.4
  0.7 0.0 copy-start.1
  0.7 0.0 copy-start
  0.7 0.0 copy-start.3
  1.4 2.4 %send.1 = (bf16[256,256]{1,0:T(8,128)(2,1)}, s32[256,128]{1,0:T(8,128)}, s32[256,128]{1,0:T(8,128)}) custom-call(s32[1]{0:T(128)S(6)} %copy.30.refs_0_, s32[1,8]{1,0:T(1,128)} %refs_1_.5, s32[1,8,64]{2,1,0:T(8,128)} %refs_3_.4, s32[1,8,64]{2,1,0:T(8,128)} %refs_4_.5, bf16[1536,256]{1,0:T(8,128)(2,1)} %refs_12_.1), custom_call_target="tpu_custom_call" | custom-call | flops 402653184 | bytes 1183780 | tf_op jit(solution)/shard_map/send/pallas_call | solution.py:99
  3.8 7.3 %all-to-all-start = ((bf16[8,32,256]{2,1,0:T(8,128)(2,1)}), bf16[8,32,256]{2,1,0:T(8,128)(2,1)S(1)}, u32[]{:S(2)}, u32[]{:S(2)}) async-start(bf16[8,32,256]{2,1,0:T(8,128)(2,1)} %bitcast.33), calls=%async_computation | async-start | bytes 262144 | tf_op jit(solution)/shard_map/all_to_all | solution.py:484
  11.1 0.1 collective-permute-start.1
  11.2 0.5 collective-permute-start.2
  11.7 0.1 collective-permute-start.3
  11.8 0.1 copy.25.refs_2_.refs_0_.refs_1_
  11.9 0.0 copy-done.2
  11.9 4.6 %first_local.1 = (bf16[1536,256]{1,0:T(8,128)(2,1)S(1)}, s32[1,512]{1,0:T(1,128)S(1)}, s32[1,512]{1,0:T(1,128)S(1)}) custom-call(s32[1]{0:T(128)S(6)} %copy.30.refs_0_, s32[1,8]{1,0:T(1,128)S(1)} %copy-done.2, s32[12,8]{1,0:T(8,128)S(1)} %copy.25.refs_2_.refs_0_.refs_1_, s32[1,8,64]{2,1,0:T(8,128)} %refs_3_.4, s32[1,8,64]{2,1,0:T(8,128)} %refs_4_.5, ...), custom_call_target="tpu_custom_call" | custom-call | flops 1207959552 | bytes 4727204 | tf_op jit(solution)/shard_map/first_local/pallas_call | solution.py:99
  16.5 2.0 %all-to-all-done = bf16[8,32,256]{2,1,0:T(8,128)(2,1)S(1)} async-done(((bf16[8,32,256]{2,1,0:T(8,128)(2,1)}), bf16[8,32,256]{2,1,0:T(8,128)(2,1)S(1)}, u32[]{:S(2)}, u32[]{:S(2)}) %all-to-all-start) | async-done | bytes 131104 | tf_op jit(solution)/shard_map/all_to_all | solution.py:484
  18.5 0.0 collective-permute-start
  18.5 0.0 collective-permute-done.1.refs_8_
  18.5 0.0 collective-permute-done.2.refs_9_
  18.5 0.0 collective-permute-done.3.refs_10_
  18.5 0.0 copy-start.5
  18.5 1.3 %collective-permute-done.refs_4_ = bf16[256,256]{1,0:T(8,128)(2,1)S(1)} collective-permute-done((bf16[256,256]{1,0:T(8,128)(2,1)S(1)}, bf16[256,256]{1,0:T(8,128)(2,1)S(1)}, u32[]{:S(2)}, u32[]{:S(2)}) %collective-permute-start) | collective-permute-done | bytes 131104 | tf_op jit(solution)/shard_map/ppermute | solution.py:488
  19.8 4.2 %forward.1 = (bf16[1536,256]{1,0:T(8,128)(2,1)}, bf16[1536,256]{1,0:T(8,128)(2,1)S(1)}, bf16[256,256]{1,0:T(8,128)(2,1)}) custom-call(s32[1]{0:T(128)S(6)} %copy.30.refs_0_, s32[256,128]{1,0:T(8,128)} %get-tuple-element.36.refs_1_, s32[1,512]{1,0:T(1,128)S(1)} %get-tuple-element.35.refs_2_, bf16[256,256]{1,0:T(8,128)(2,1)S(1)} %bitcast.24, ...), custom_call_target="tpu_custom_call" | custom-call | flops 2013265920 | bytes 5244932 | tf_op jit(solution)/shard_map/forward/pallas_call | solution.py:99
  24.0 4.1 %all-to-all-start.1 = ((bf16[8,32,256]{2,1,0:T(8,128)(2,1)}), bf16[8,32,256]{2,1,0:T(8,128)(2,1)S(1)}, u32[]{:S(2)}, u32[]{:S(2)}) async-start(bf16[8,32,256]{2,1,0:T(8,128)(2,1)} %bitcast.35), calls=%async_computation.1 | async-start | bytes 262144 | tf_op jit(solution)/shard_map/all_to_all | solution.py:484
  28.1 4.3 %local.1.refs_11_ = bf16[1536,256]{1,0:T(8,128)(2,1)S(1)} custom-call(s32[12,8]{1,0:T(8,128)S(1)} %copy.25.refs_2_.refs_0_.refs_1_, bf16[1536,256]{1,0:T(8,128)(2,1)S(1)} %get-tuple-element.45.refs_1_.refs_12_, bf16[12,8,128,128]{3,2,1,0:T(8,128)(2,1)} %refs_4_.7), custom_call_target="tpu_custom_call" | custom-call | flops 1207959552 | bytes 4718976 | tf_op jit(solution)/shard_map/local/pallas_call | solution.py:99
  32.3 3.2 %all-to-all-done.1 = bf16[8,32,256]{2,1,0:T(8,128)(2,1)S(1)} async-done(((bf16[8,32,256]{2,1,0:T(8,128)(2,1)}), bf16[8,32,256]{2,1,0:T(8,128)(2,1)S(1)}, u32[]{:S(2)}, u32[]{:S(2)}) %all-to-all-start.1) | async-done | bytes 131104 | tf_op jit(solution)/shard_map/all_to_all | solution.py:484
  35.6 0.0 collective-permute-start.4
  35.6 1.3 %collective-permute-done.4.refs_4_ = bf16[256,256]{1,0:T(8,128)(2,1)S(1)} collective-permute-done((bf16[256,256]{1,0:T(8,128)(2,1)S(1)}, bf16[256,256]{1,0:T(8,128)(2,1)S(1)}, u32[]{:S(2)}, u32[]{:S(2)}) %collective-permute-start.4) | collective-permute-done | bytes 131104 | tf_op jit(solution)/shard_map/ppermute | solution.py:488
  36.9 6.3 %turn.1 = (bf16[1536,256]{1,0:T(8,128)(2,1)}, bf16[1536,256]{1,0:T(8,128)(2,1)S(1)}, bf16[256,256]{1,0:T(8,128)(2,1)}, bf16[384,256]{1,0:T(8,128)(2,1)}, bf16[384,256]{1,0:T(8,128)(2,1)}) custom-call(s32[1]{0:T(128)S(6)} %copy.30.refs_0_, s32[256,128]{1,0:T(8,128)} %get-tuple-element.34.refs_1_, s32[1,512]{1,0:T(1,128)S(1)} %get-tuple-element.35.refs_2_, ...), custom_call_target="tpu_custom_call" | custom-call | flops 4429185024 | bytes 6424580 | tf_op jit(solution)/shard_map/turn/pallas_call | solution.py:99
  43.2 3.6 %all-to-all-start.2 = ((bf16[8,32,256]{2,1,0:T(8,128)(2,1)}), bf16[8,32,256]{2,1,0:T(8,128)(2,1)S(1)}, u32[]{:S(2)}, u32[]{:S(2)}) async-start(bf16[8,32,256]{2,1,0:T(8,128)(2,1)} %bitcast.34), calls=%async_computation.2 | async-start | bytes 262144 | tf_op jit(solution)/shard_map/all_to_all | solution.py:484
  46.8 1.7 %collective-permute-start.6 = (bf16[384,256]{1,0:T(8,128)(2,1)}, bf16[384,256]{1,0:T(8,128)(2,1)S(1)}, u32[]{:S(2)}, u32[]{:S(2)}) collective-permute-start(bf16[384,256]{1,0:T(8,128)(2,1)} %get-tuple-element.57), channel_id=1, source_target_pairs={{0,2},{2,0},{4,6},{6,4},{8,10},{10,8},{12,14},{14,12},{1,3},{3,1},... | collective-permute-start | bytes 589832 | tf_op jit(solution)/shard_map/ppermute | solution.py:612
  48.5 4.6 %turned_local.2.refs_11_ = bf16[1536,256]{1,0:T(8,128)(2,1)S(1)} custom-call(s32[1]{0:T(128)S(6)} %copy.30.refs_0_, s32[12,8]{1,0:T(8,128)S(1)} %copy.25.refs_2_.refs_0_.refs_1_, bf16[1536,256]{1,0:T(8,128)(2,1)S(1)} %get-tuple-element.51.refs_2_, bf16[1536,256]{1,0:T(8,128)(2,1)} %refs_3_.5, bf16[12,8,128,128]{3,2,1,0:T(8,128)(2,1)} %refs_4_.7), custom_call_target="tpu_custom_call" | custom-call | flops 1207959552 | bytes 5505412 | tf_op jit(solution)/shard_map/turned_local/pallas_call | solution.py:99
  53.1 1.1 all-to-all-done.2
  54.2 0.0 collective-permute-start.5
  54.2 1.1 collective-permute-done.6.refs_14_
  55.3 0.3 collective-permute-done.5.refs_4_
  55.6 0.4 copy-done.6
  56.0 6.6 %backward.1 = (bf16[1536,256]{1,0:T(8,128)(2,1)}, bf16[1536,256]{1,0:T(8,128)(2,1)S(1)}, bf16[8,176,256]{2,1,0:T(8,128)(2,1)}) custom-call(s32[1]{0:T(128)S(6)} %copy.30.refs_0_, s32[256,128]{1,0:T(8,128)} %get-tuple-element.34.refs_1_, s32[1,512]{1,0:T(1,128)S(1)} %get-tuple-element.50.refs_2_.refs_1_, bf16[256,256]{1,0:T(8,128)(2,1)S(1)} %bitcast.26, ...), custom_call_target="tpu_custom_call" | custom-call | flops 4429185024 | bytes 6227972 | tf_op jit(solution)/shard_map/backward/pallas_call | solution.py:99
  62.5 4.5 %all-to-all-start.3 = ((bf16[8,176,256]{2,1,0:T(8,128)(2,1)}), bf16[8,176,256]{2,1,0:T(8,128)(2,1)S(1)}, u32[]{:S(2)}, u32[]{:S(2)}) async-start(bf16[8,176,256]{2,1,0:T(8,128)(2,1)} %get-tuple-element.60), calls=%async_computation.3 | async-start | bytes 1441792 | tf_op jit(solution)/shard_map/all_to_all | solution.py:484
  67.0 4.6 %turned_local.3.refs_4_ = bf16[1536,256]{1,0:T(8,128)(2,1)S(1)} custom-call(s32[1]{0:T(128)S(6)} %copy.30.refs_0_, s32[12,8]{1,0:T(8,128)S(1)} %copy.25.refs_2_.refs_0_.refs_1_, bf16[1536,256]{1,0:T(8,128)(2,1)S(1)} %get-tuple-element.58.refs_2_, bf16[1536,256]{1,0:T(8,128)(2,1)} %get-tuple-element.59.refs_3_, bf16[12,8,128,128]{3,2,1,0:T(8,128)(2,1)} %refs_4_.7), custom_call_target="tpu_custom_call" | custom-call | flops 1207959552 | bytes 5505412 | tf_op jit(solution)/shard_map/turned_local/pallas_call | solution.py:99
  71.6 13.9 %all-to-all-done.3 = bf16[8,176,256]{2,1,0:T(8,128)(2,1)S(1)} async-done(((bf16[8,176,256]{2,1,0:T(8,128)(2,1)}), bf16[8,176,256]{2,1,0:T(8,128)(2,1)S(1)}, u32[]{:S(2)}, u32[]{:S(2)}) %all-to-all-start.3) | async-done | bytes 720928 | tf_op jit(solution)/shard_map/all_to_all | solution.py:484
  85.5 0.1 slice_reduce_fusion
  85.7 0.9 broadcast_in_dim.2
  86.6 3.6 %all-to-all-start.4 = ((bf16[8,192,256]{2,1,0:T(8,128)(2,1)}), bf16[8,192,256]{2,1,0:T(8,128)(2,1)S(1)}, u32[]{:S(2)}, u32[]{:S(2)}) async-start(bf16[8,192,256]{2,1,0:T(8,128)(2,1)} %broadcast_in_dim.2), calls=%async_computation.4 | async-start | bytes 1572864 | tf_op jit(solution)/shard_map/all_to_all | solution.py:484
  90.2 0.1 collective-permute-start.7
  90.3 1.3 %collective-permute-done.7.refs_3_ = bf16[256,256]{1,0:T(8,128)(2,1)S(1)} collective-permute-done((bf16[256,256]{1,0:T(8,128)(2,1)S(1)}, bf16[256,256]{1,0:T(8,128)(2,1)S(1)}, u32[]{:S(2)}, u32[]{:S(2)}) %collective-permute-start.7) | collective-permute-done | bytes 131104 | tf_op jit(solution)/shard_map/ppermute | solution.py:488
  91.6 1.8 %last.1 = f32[1536,256]{1,0:T(8,128)} custom-call(s32[1]{0:T(128)S(6)} %copy.30.refs_0_, s32[1,512]{1,0:T(1,128)S(1)} %get-tuple-element.50.refs_2_.refs_1_, bf16[256,256]{1,0:T(8,128)(2,1)S(1)} %bitcast.22, bf16[256,256]{1,0:T(8,128)(2,1)S(1)} %collective-permute-done.7.refs_3_, bf16[1536,256]{1,0:T(8,128)(2,1)S(1)} %turned_local.3.refs_4_), custom_call_target="tpu_custom_call" | custom-call | flops 402653184 | bytes 2623492 | tf_op jit(solution)/shard_map/last/pallas_call | solution.py:99
  93.4 17.2 %all-to-all-done.4 = bf16[8,192,256]{2,1,0:T(8,128)(2,1)S(1)} async-done(((bf16[8,192,256]{2,1,0:T(8,128)(2,1)}), bf16[8,192,256]{2,1,0:T(8,128)(2,1)S(1)}, u32[]{:S(2)}, u32[]{:S(2)}) %all-to-all-start.4) | async-done | bytes 786464 | tf_op jit(solution)/shard_map/all_to_all | solution.py:484
  110.6 0.1 fusion
  110.7 0.1 maximum_convert_fusion
  110.8 1.2 %slice_bitcast_fusion = (f32[2,256,256]{2,1,0:T(8,128)}, f32[2,256,256]{2,1,0:T(8,128)}, f32[2,256,256]{2,1,0:T(8,128)}) fusion(f32[3,2,256,256]{3,2,0,1:T(8,128)S(1)} %maximum_convert_fusion), kind=kLoop, calls=%fused_computation.1 | loop fusion | bytes 3145728 | tf_op jit(solution)/shard_map/squeeze | solution.py:659
  (12 shorter events, 0.1 us)
Async XLA Ops:
  0.6 11.3 %copy-start.2 = (s32[1,8]{1,0:T(1,128)S(1)}, s32[1,8]{1,0:T(1,128)}, u32[]{:S(2)}) copy-start(s32[1,8]{1,0:T(1,128)} %refs_1_.5) | copy-start | bytes 100
  0.6 11.1 %copy-start.4 = (bf16[2,256,256]{2,1,0:T(8,128)(2,1)S(1)}, bf16[2,256,256]{2,1,0:T(8,128)(2,1)}, u32[]{:S(2)}) copy-start(bf16[2,256,256]{2,1,0:T(8,128)(2,1)} %refs_7_.2) | copy-start | bytes 786436
  0.7 10.6 %copy-start.1 = (bf16[2,256,256]{2,1,0:T(8,128)(2,1)S(1)}, bf16[2,256,256]{2,1,0:T(8,128)(2,1)}, u32[]{:S(2)}) copy-start(bf16[2,256,256]{2,1,0:T(8,128)(2,1)} %refs_6_.4) | copy-start | bytes 786436
  0.7 10.5 %copy-start = (bf16[2,256,256]{2,1,0:T(8,128)(2,1)S(1)}, bf16[2,256,256]{2,1,0:T(8,128)(2,1)}, u32[]{:S(2)}) copy-start(bf16[2,256,256]{2,1,0:T(8,128)(2,1)} %refs_5_.4) | copy-start | bytes 786436
  0.7 11.1 %copy-start.3 = (s32[12,8]{0,1:T(8,128)S(1)}, s32[12,8]{0,1:T(8,128)}, u32[]{:S(2)}) copy-start(s32[12,8]{0,1:T(8,128)} %param.13) | copy-start | bytes 1156
  3.8 14.7 %all-to-all-start = ((bf16[8,32,256]{2,1,0:T(8,128)(2,1)}), bf16[8,32,256]{2,1,0:T(8,128)(2,1)S(1)}, u32[]{:S(2)}, u32[]{:S(2)}) async-start(bf16[8,32,256]{2,1,0:T(8,128)(2,1)} %bitcast.33), calls=%async_computation | async-start | bytes 262144 | tf_op jit(solution)/shard_map/all_to_all | solution.py:484
  11.1 7.3 %collective-permute-start.1 = (bf16[2,256,256]{2,1,0:T(8,128)(2,1)S(1)}, bf16[2,256,256]{2,1,0:T(8,128)(2,1)S(1)}, u32[]{:S(2)}, u32[]{:S(2)}) collective-permute-start(bf16[2,256,256]{2,1,0:T(8,128)(2,1)S(1)} %copy-done), channel_id=1, source_target_pairs={{0,1},{1,0},{2,3},{3,2},{4,5},{5,4},{6,7},{7,6},{8,9},{9,8},{10,11... | collective-permute-start | bytes 786440 | tf_op jit(solution)/shard_map/ppermute | solution.py:530
  11.2 7.3 %collective-permute-start.2 = (bf16[2,256,256]{2,1,0:T(8,128)(2,1)S(1)}, bf16[2,256,256]{2,1,0:T(8,128)(2,1)S(1)}, u32[]{:S(2)}, u32[]{:S(2)}) collective-permute-start(bf16[2,256,256]{2,1,0:T(8,128)(2,1)S(1)} %copy-done.1), channel_id=1, source_target_pairs={{0,1},{1,0},{2,3},{3,2},{4,5},{5,4},{6,7},{7,6},{8,9},{9,8},{10,11... | collective-permute-start | bytes 786440 | tf_op jit(solution)/shard_map/ppermute | solution.py:530
  11.7 6.8 %collective-permute-start.3 = (bf16[2,256,256]{2,1,0:T(8,128)(2,1)S(1)}, bf16[2,256,256]{2,1,0:T(8,128)(2,1)S(1)}, u32[]{:S(2)}, u32[]{:S(2)}) collective-permute-start(bf16[2,256,256]{2,1,0:T(8,128)(2,1)S(1)} %copy-done.4), channel_id=1, source_target_pairs={{0,1},{1,0},{2,3},{3,2},{4,5},{5,4},{6,7},{7,6},{8,9},{9,8},{10,11... | collective-permute-start | bytes 786440 | tf_op jit(solution)/shard_map/ppermute | solution.py:530
  18.5 1.3 %collective-permute-start = (bf16[256,256]{1,0:T(8,128)(2,1)S(1)}, bf16[256,256]{1,0:T(8,128)(2,1)S(1)}, u32[]{:S(2)}, u32[]{:S(2)}) collective-permute-start(bf16[256,256]{1,0:T(8,128)(2,1)S(1)} %bitcast.23), channel_id=1, source_target_pairs={{0,1},{1,0},{2,3},{3,2},{4,5},{5,4},{6,7},{7,6},{8,9},{9,8},{10,11... | collective-permute-start | bytes 393224 | tf_op jit(solution)/shard_map/ppermute | solution.py:488
  18.5 1.3 %copy-start.5 = (bf16[2,256,256]{2,1,0:T(8,128)(2,1)}, bf16[2,256,256]{2,1,0:T(8,128)(2,1)S(1)}, u32[]{:S(2)}) copy-start(bf16[2,256,256]{2,1,0:T(8,128)(2,1)S(1)} %collective-permute-done.3.refs_10_) | copy-start | bytes 786436
  24.0 11.6 %all-to-all-start.1 = ((bf16[8,32,256]{2,1,0:T(8,128)(2,1)}), bf16[8,32,256]{2,1,0:T(8,128)(2,1)S(1)}, u32[]{:S(2)}, u32[]{:S(2)}) async-start(bf16[8,32,256]{2,1,0:T(8,128)(2,1)} %bitcast.35), calls=%async_computation.1 | async-start | bytes 262144 | tf_op jit(solution)/shard_map/all_to_all | solution.py:484
  35.6 1.3 %collective-permute-start.4 = (bf16[256,256]{1,0:T(8,128)(2,1)S(1)}, bf16[256,256]{1,0:T(8,128)(2,1)S(1)}, u32[]{:S(2)}, u32[]{:S(2)}) collective-permute-start(bf16[256,256]{1,0:T(8,128)(2,1)S(1)} %bitcast.27), channel_id=1, source_target_pairs={{0,1},{1,0},{2,3},{3,2},{4,5},{5,4},{6,7},{7,6},{8,9},{9,8},{10,11... | collective-permute-start | bytes 393224 | tf_op jit(solution)/shard_map/ppermute | solution.py:488
  43.2 11.0 %all-to-all-start.2 = ((bf16[8,32,256]{2,1,0:T(8,128)(2,1)}), bf16[8,32,256]{2,1,0:T(8,128)(2,1)S(1)}, u32[]{:S(2)}, u32[]{:S(2)}) async-start(bf16[8,32,256]{2,1,0:T(8,128)(2,1)} %bitcast.34), calls=%async_computation.2 | async-start | bytes 262144 | tf_op jit(solution)/shard_map/all_to_all | solution.py:484
  46.8 8.5 %collective-permute-start.6 = (bf16[384,256]{1,0:T(8,128)(2,1)}, bf16[384,256]{1,0:T(8,128)(2,1)S(1)}, u32[]{:S(2)}, u32[]{:S(2)}) collective-permute-start(bf16[384,256]{1,0:T(8,128)(2,1)} %get-tuple-element.57), channel_id=1, source_target_pairs={{0,2},{2,0},{4,6},{6,4},{8,10},{10,8},{12,14},{14,12},{1,3},{3,1},... | collective-permute-start | bytes 589832 | tf_op jit(solution)/shard_map/ppermute | solution.py:612
  54.2 1.3 %collective-permute-start.5 = (bf16[256,256]{1,0:T(8,128)(2,1)S(1)}, bf16[256,256]{1,0:T(8,128)(2,1)S(1)}, u32[]{:S(2)}, u32[]{:S(2)}) collective-permute-start(bf16[256,256]{1,0:T(8,128)(2,1)S(1)} %bitcast.25), channel_id=1, source_target_pairs={{0,1},{1,0},{2,3},{3,2},{4,5},{5,4},{6,7},{7,6},{8,9},{9,8},{10,11... | collective-permute-start | bytes 393224 | tf_op jit(solution)/shard_map/ppermute | solution.py:488
  55.3 0.7 copy-start.6
  62.5 23.0 %all-to-all-start.3 = ((bf16[8,176,256]{2,1,0:T(8,128)(2,1)}), bf16[8,176,256]{2,1,0:T(8,128)(2,1)S(1)}, u32[]{:S(2)}, u32[]{:S(2)}) async-start(bf16[8,176,256]{2,1,0:T(8,128)(2,1)} %get-tuple-element.60), calls=%async_computation.3 | async-start | bytes 1441792 | tf_op jit(solution)/shard_map/all_to_all | solution.py:484
  86.6 24.0 %all-to-all-start.4 = ((bf16[8,192,256]{2,1,0:T(8,128)(2,1)}), bf16[8,192,256]{2,1,0:T(8,128)(2,1)S(1)}, u32[]{:S(2)}, u32[]{:S(2)}) async-start(bf16[8,192,256]{2,1,0:T(8,128)(2,1)} %broadcast_in_dim.2), calls=%async_computation.4 | async-start | bytes 1572864 | tf_op jit(solution)/shard_map/all_to_all | solution.py:484
  90.2 1.4 %collective-permute-start.7 = (bf16[256,256]{1,0:T(8,128)(2,1)S(1)}, bf16[256,256]{1,0:T(8,128)(2,1)S(1)}, u32[]{:S(2)}, u32[]{:S(2)}) collective-permute-start(bf16[256,256]{1,0:T(8,128)(2,1)S(1)} %bitcast.21), channel_id=1, source_target_pairs={{0,1},{1,0},{2,3},{3,2},{4,5},{5,4},{6,7},{7,6},{8,9},{9,8},{10,11... | collective-permute-start | bytes 393224 | tf_op jit(solution)/shard_map/ppermute | solution.py:488
